TPU v7x, 128 devices: a whole 4x4x4 slice. The times are simulated.
128 devices in a mesh: dp: 32 (over x, y_lo, z), gz: 4 (over y_hi, core).
Axes of the slice: x: 4, y: 4 (y_hi: 2, y_lo: 2; y = y_hi * 2 + y_lo), z: 4, core: 2. Of those that a mesh axis runs over, the one named last changes fastest.
Arguments:
- field: bfloat16 [32, 16, 96, 9216], P('dp', None, 'gz'), may hold values from -6 to 6
- cotangent: bfloat16 [32, 16, 96, 9216], P('dp', None, 'gz'), may hold values from -36 to 36, as said below
- spec_weight: float32 [16, 16, 16, 256], P('gz'), may hold values from -1.5 to 1.5
- point_weight: bfloat16 [16, 16], replicated, may hold values from -1.5 to 1.5
- bias: float32 [16], replicated, may hold values from -3 to 3
Outputs:
- field_grad: bfloat16 [32, 16, 96, 9216], P('dp', None, 'gz')
- spectral_grad: float32 [16, 16, 16, 256], P('gz')
- point_grad: float32 [16, 16], replicated
- bias_grad: float32 [16], replicated
Inputs may be any that keep to these rules, and one draw needn't show every extreme that they name: `cotangent`: the gradient of the loss with respect to the layer's output.
All inputs are finite; a program needn't handle non-finite values.
Results may differ from a plain program's by a relative error of at most 0.007.
Values sent between devices are 32-bit elements; how exact they have to be, the bound alone decides.
No kernel may reach another device: no remote copies, remote signals or barrier semaphores. Data moves between devices by JAX's collectives and lax.ppermute only.
A program may use at most 192 MiB of HBM per device.

v0:
```python
import math

import jax
import jax.numpy as jnp
from jax import lax
from jax.sharding import PartitionSpec as P

N = 96
M = 16


root_half = 0.7071067811865476
density_norm = 0.3989422804014327


def basis_table(count_modes, length):
    mode_index = jnp.arange(count_modes, dtype=jnp.int32)
    half_count = count_modes // 2
    frequency = jnp.where(mode_index < half_count, mode_index, mode_index - half_count + 1)
    position = jnp.arange(length, dtype=jnp.int32)
    turns = frequency[:, None] * position[None, :] % length
    angle = turns.astype(jnp.float32) * (2.0 * math.pi / length)
    return jnp.where((mode_index < half_count)[:, None], jnp.cos(angle), jnp.sin(angle))


def kron_table(basis):
    outer = basis[:, None, :, None] * basis[None, :, None, :]
    return outer.reshape(M * M, N * N)


def gelu_slope(values):
    cumulative = 0.5 * (1.0 + lax.erf(values * root_half))
    return cumulative + values * jnp.exp(-0.5 * values * values) * density_norm


def shards(field, cotangent, spec_weight, point_weight, bias):
    highest = lax.Precision.HIGHEST
    samples_dev, channels, slab_rows, plane_cells = field.shape
    scale_fwd = (2.0 / N) ** 1.5
    scale_inv = (2.0 / M) ** 1.5
    basis = basis_table(M, N)
    kron = kron_table(basis)
    row_basis = lax.dynamic_slice_in_dim(basis, lax.axis_index("gz") * slab_rows, slab_rows, 1)
    contract_cells = (((1,), (1,)), ((), ()))

    def to_modes(values):
        flattened = values.reshape(samples_dev * channels * slab_rows, plane_cells).astype(
            jnp.float32
        )
        return lax.dot_general(flattened, kron, contract_cells, precision=highest).reshape(
            samples_dev, channels, slab_rows, M * M
        )

    def add_inverse(piece):
        piece_rows = piece.shape[0]
        inner = jnp.dot(
            piece.reshape(piece_rows * samples_dev * channels, M * M), kron, precision=highest
        )
        inner = inner.reshape(piece_rows, samples_dev, channels, plane_cells)
        return jnp.einsum("ax,asoz->soxz", row_basis, inner, precision=highest)

    line_modes = to_modes(field)
    rows_part = row_basis
    coefficients = lax.psum_scatter(
        scale_fwd * jnp.einsum("ax,scxp->ascp", rows_part, line_modes, precision=highest),
        "gz",
        scatter_dimension=0,
        tiled=True,
    )
    mixed_modes = jnp.einsum("asip,aiop->asop", coefficients, spec_weight, precision=highest)
    spectral = scale_inv * add_inverse(lax.all_gather(mixed_modes, "gz", axis=0, tiled=True))
    pre_act = (
        spectral
        + jnp.einsum("sixz,io->soxz", field, point_weight, preferred_element_type=jnp.float32)
        + bias[None, :, None, None]
    )
    grad_pre = (cotangent.astype(jnp.float32) * gelu_slope(pre_act)).astype(jnp.bfloat16)
    grad_line = to_modes(grad_pre)
    rows_part = row_basis
    grad_modes = lax.psum_scatter(
        scale_inv * jnp.einsum("ax,soxp->asop", rows_part, grad_line, precision=highest),
        "gz",
        scatter_dimension=0,
        tiled=True,
    )
    back_modes = jnp.einsum("aiop,asop->asip", spec_weight, grad_modes, precision=highest)
    field_spec = scale_fwd * add_inverse(lax.all_gather(back_modes, "gz", axis=0, tiled=True))
    field_grad = (
        field_spec
        + jnp.einsum("soxz,io->sixz", grad_pre, point_weight, preferred_element_type=jnp.float32)
    ).astype(jnp.bfloat16)
    local_point = jnp.einsum("sixz,soxz->io", field, grad_pre, preferred_element_type=jnp.float32)
    local_bias = jnp.sum(grad_pre, axis=(0, 2, 3), dtype=jnp.float32)
    total_point, total_bias = lax.psum((local_point, local_bias), ("dp", "gz"))
    local_spec = jnp.einsum("asip,asop->aiop", coefficients, grad_modes, precision=highest)
    grad_spec = lax.psum(local_spec, "dp")
    all_samples = samples_dev * lax.axis_size("dp")
    cell_norm = math.sqrt(all_samples * N * N * N)
    return (
        field_grad,
        grad_spec / math.sqrt(all_samples * N),
        total_point / cell_norm,
        total_bias / cell_norm,
    )


def solution(mesh):
    return jax.shard_map(
        shards,
        mesh=mesh,
        in_specs=(
            P("dp", None, "gz", None),
            P("dp", None, "gz", None),
            P("gz", None, None, None),
            P(),
            P(),
        ),
        out_specs=(P("dp", None, "gz", None), P("gz", None, None, None), P(), P()),
        check_vma=False,
    )
```

profile of v0, /device:TPU:0, one launch (start us, length us, event | category | flops | bytes accessed | tf_op | source)
XLA Modules:
  0.0 559.2 jit_solution(4819427986787261615)
XLA Ops:
  7.2 0.0 copy-start
  7.2 0.0 reduce-scatter.3.cloned.1.call-start
  7.3 0.1 sine_select_fusion
  7.4 6.2 %broadcast_multiply_fusion = f32[16,16,96,96]{3,2,1,0:T(8,128)} fusion(f32[16,96]{1,0:T(8,128)S(1)} %sine_select_fusion), kind=kLoop, calls=%fused_computation.12 | loop fusion | flops 2359296 | bytes 9443328 | tf_op jit(solution)/shard_map/mul | solution.py:27
  13.6 12.8 %mul.213 = f32[256,9216]{1,0:T(8,128)} reshape(f32[16,16,96,96]{3,2,1,0:T(8,128)} %broadcast_multiply_fusion) | data formatting | bytes 18874368 | tf_op jit(solution)/shard_map/mul | solution.py:27
  26.4 11.1 %convolution_bitcast_fusion = f32[384,256]{0,1:T(8,128)S(1)} fusion(f32[256,9216]{1,0:T(8,128)} %mul.213, bf16[384,9216]{1,0:T(8,128)(2,1)} %bitcast.98), kind=kOutput, calls=%fused_computation.20 | convolution fusion | flops 10871635968 | bytes 16908288 | tf_op jit(solution)/shard_map/dot_general | solution.py:50
  37.5 0.2 copy.31
  37.7 0.4 fusion.16
  38.1 0.9 copy.32
  39.0 0.0 reduce-scatter.3.cloned.1.call-update
  39.0 0.0 reduce-scatter.5.cloned.1.call-start
  39.0 12.9 %reshape.211 = f32[256,9216,1]{1,0,2:T(8,128)} reshape(f32[16,16,96,96]{3,2,1,0:T(8,128)} %broadcast_multiply_fusion) | data formatting | bytes 18874368 | tf_op jit(solution)/shard_map/mul | solution.py:27
  51.9 0.0 copy-done
  51.9 0.0 copy-start.1
  51.9 11.7 %fusion.13 = f32[16,24,9216]{2,0,1:T(8,128)} fusion(bf16[16,24,9216]{2,1,0:T(8,128)(2,1)} %bitcast.99, bf16[16,16]{1,0:T(8,128)(2,1)S(1)} %copy-done), kind=kOutput, calls=%fused_computation.18 | convolution fusion | flops 113246208 | bytes 21234176 | tf_op jit(solution)/shard_map/sixz,io->soxz/dot_general | solution.py:74
  63.6 5.0 reduce-scatter.3.cloned.1.call-done
  68.6 0.0 copy-done.1
  68.6 0.0 slice-start.5
  68.6 1.1 multiply_reduce_fusion.1
  69.8 7.4 %all_gather.6 = f32[16,1,16,256]{3,2,1,0:T(8,128)S(1)} all-gather(f32[4,1,16,256]{3,2,1,0:T(8,128)S(1)} %bitcast.109), channel_id=1, replica_groups=mesh['dp'=32,'gz'=4] {'gz'}, dimensions={0}, use_global_device_ids=true | all-gather | bytes 327680 | tf_op jit(solution)/shard_map/all_gather | solution.py:71
  77.2 0.0 slice-start.6
  77.2 0.0 copy-start.3
  77.2 0.0 slice-start
  77.2 12.2 %fusion.24 = f32[16,16,9216]{2,0,1:T(8,128)S(1)} fusion(f32[256,9216,1]{1,0,2:T(8,128)} %reshape.211, f32[16,1,16,256]{3,2,1,0:T(8,128)S(1)} %all_gather.6), kind=kOutput, calls=%fused_computation.32 | convolution fusion | flops 7247757312 | bytes 19136512 | tf_op jit(solution)/shard_map/dot_general | solution.py:56
  89.4 0.0 slice-done.5
  89.4 0.0 slice-done.6
  89.4 0.0 copy-done.3
  89.4 0.0 slice-start.1
  89.4 0.0 slice-start.2
  89.4 25.9 %convert_reduce_fusion = (f32[16]{0:T(128)S(1)}, bf16[1,16,24,9216]{3,2,1,0:T(8,128)(2,1)}) fusion(f32[16]{0:T(128)S(1)} %copy-done.3, f32[16,24,9216]{2,0,1:T(8,128)} %fusion.13, f32[16,16,9216]{2,0,1:T(8,128)S(1)} %fusion.24, f32[16,96]{1,0:T(8,128)S(1)} %sine_select_fusion, s32[]{:T(128)S(6)} %select_n.65, bf16[1,16,24,9216]{3,2,1,0:T(8,128)(2,1)S(1)} %bitcast.112), kind=kOutput, calls=%fused_computation.11 | convolution fusion | flops 736100352 | bytes 37755012 | tf_op jit(solution)/shard_map/ax,asoz->soxz/dot_general | solution.py:60
  115.4 0.0 slice-start.3
  115.4 0.0 slice-done
  115.4 0.0 slice-done.1
  115.4 0.0 slice-done.2
  115.4 0.0 slice-start.4
  115.4 13.4 %fusion.47 = f32[16,24,256]{2,1,0:T(8,128)S(1)} fusion(f32[256,9216,1]{1,0,2:T(8,128)S(1)} %bitcast.97, bf16[1,16,24,9216]{3,2,1,0:T(8,128)(2,1)} %get-tuple-element.21), kind=kOutput, calls=%fused_computation.62 | convolution fusion | flops 10871635968 | bytes 16908288 | tf_op jit(solution)/shard_map/dot_general | solution.py:50
  128.8 0.0 slice-done.3
  128.8 0.0 slice-done.4
  128.9 17.8 %fusion.17 = f32[16,16]{0,1:T(8,128)S(1)} fusion(bf16[16,24,9216]{2,1,0:T(8,128)(2,1)S(1)} %bitcast.102, bf16[16,24,9216]{2,1,0:T(8,128)(2,1)} %bitcast.103), kind=kOutput, calls=%fused_computation.25 | convolution fusion | flops 113246208 | bytes 14156800 | tf_op jit(solution)/shard_map/sixz,soxz->io/dot_general | solution.py:92
  146.7 65.4 %all-reduce = (f32[16,16]{0,1:T(8,128)S(1)}, f32[16]{0:T(128)S(1)}) all-reduce(f32[16,16]{0,1:T(8,128)S(1)} %fusion.17, f32[16]{0:T(128)S(1)} %get-tuple-element.20), channel_id=1, replica_groups=mesh['dp'=32,'gz'=4] {'dp','gz'}, use_global_device_ids=true, to_apply=%region_3.4 | all-reduce | flops 272 | bytes 2176 | tf_op jit(solution)/shard_map/psum | solution.py:94
  212.2 0.7 copy.43
  212.8 0.5 broadcast_multiply_fusion.3
  213.4 0.4 fusion.15
  213.8 0.9 copy.37
  214.6 0.0 reduce-scatter.5.cloned.1.call-update
  214.7 0.0 copy-start.2
  214.7 0.0 all-reduce.3.cloned.1.call-start
  214.7 16.0 %fusion.10 = f32[24,9216,16]{1,2,0:T(8,128)} fusion(bf16[16,24,9216]{2,1,0:T(8,128)(2,1)} %bitcast.104, bf16[16,16]{1,0:T(8,128)(2,1)S(1)} %copy-done), kind=kOutput, calls=%fused_computation.15 | convolution fusion | flops 113246208 | bytes 21234176 | tf_op jit(solution)/shard_map/soxz,io->sixz/dot_general | solution.py:90
  230.7 8.1 %reduce-scatter.5.cloned.1.call-done = f32[4,1,16,256]{3,2,1,0:T(8,128)} async-done(((f32[16,1,16,256]{3,2,1,0:T(8,128)}), f32[4,1,16,256]{3,2,1,0:T(8,128)}) %reduce-scatter.5.cloned.1.call-update) | async-done | bytes 65552 | tf_op jit(solution)/shard_map/reduce_scatter | solution.py:80
  238.8 0.0 copy-done.2
  238.8 2.1 multiply_bitcast_fusion
  240.8 0.0 all-reduce.3.cloned.1.call-update
  240.9 7.3 %all_gather.7 = f32[16,1,16,256]{3,2,1,0:T(8,128)S(1)} all-gather(f32[4,1,16,256]{3,2,1,0:T(8,128)S(1)} %bitcast.108), channel_id=1, replica_groups=mesh['dp'=32,'gz'=4] {'gz'}, dimensions={0}, use_global_device_ids=true | all-gather | bytes 327680 | tf_op jit(solution)/shard_map/all_gather | solution.py:87
  248.2 12.2 %fusion.22 = f32[16,16,9216]{2,0,1:T(8,128)S(1)} fusion(f32[256,9216,1]{1,0,2:T(8,128)} %reshape.211, f32[16,1,16,256]{3,2,1,0:T(8,128)S(1)} %all_gather.7), kind=kOutput, calls=%fused_computation.30 | convolution fusion | flops 7247757312 | bytes 19136512 | tf_op jit(solution)/shard_map/dot_general | solution.py:56
  260.4 25.8 %fusion.6 = bf16[1,16,24,9216]{3,2,1,0:T(8,128)(2,1)} fusion(f32[24,9216,16]{1,2,0:T(8,128)} %fusion.10, f32[16,16,9216]{2,0,1:T(8,128)S(1)} %fusion.22, f32[16,96]{1,0:T(8,128)S(1)} %sine_select_fusion, s32[]{:T(128)S(6)} %select_n.65), kind=kOutput, calls=%fused_computation.8 | convolution fusion | flops 690094080 | bytes 30676996 | tf_op jit(solution)/shard_map/ax,asoz->soxz/dot_general | solution.py:60
  286.2 263.8 %all-reduce.3.cloned.1.call-done = f32[4,16,16,256]{3,2,1,0:T(8,128)} async-done(((f32[4,16,16,256]{3,2,1,0:T(8,128)}), f32[4,16,16,256]{3,2,1,0:T(8,128)}) %all-reduce.3.cloned.1.call-update) | async-done | bytes 1048592 | tf_op jit(solution)/shard_map/psum | solution.py:96
  550.0 2.3 broadcast_multiply_fusion.1
  (6 shorter events, 0.0 us)
Async XLA Ops:
  7.2 44.8 %copy-start = (bf16[16,16]{1,0:T(8,128)(2,1)S(1)}, bf16[16,16]{1,0:T(8,128)(2,1)}, u32[]{:S(2)}) copy-start(bf16[16,16]{1,0:T(8,128)(2,1)} %param.8) | copy-start | bytes 1540
  7.2 61.4 %reduce-scatter.3.cloned.1.call-start = ((), (), s32[]{:S(2)}) async-start(), calls=%async_computation.2 | async-start | bytes 327680 | tf_op jit(solution)/shard_map/reduce_scatter | solution.py:64
  39.0 199.8 %reduce-scatter.5.cloned.1.call-start = ((), (), s32[]{:S(2)}) async-start(), calls=%async_computation.3 | async-start | bytes 327680 | tf_op jit(solution)/shard_map/reduce_scatter | solution.py:80
  51.9 16.7 %copy-start.1 = (f32[4,16,16,256]{3,2,1,0:T(8,128)S(1)}, f32[4,16,16,256]{3,2,1,0:T(8,128)}, u32[]{:S(2)}) copy-start(f32[4,16,16,256]{3,2,1,0:T(8,128)} %param.7) | copy-start | bytes 3145732
  68.6 20.8 %slice-start.5 = ((s8[7077888]{0:T(1024)(128)(4,1)}), s8[4194304]{0:T(1024)(128)(4,1)S(1)}, s32[]{:S(2)}) async-start(s8[7077888]{0:T(1024)(128)(4,1)} %bitcast.111), calls=%async_computation.10 | async-start | bytes 8388608
  77.2 12.2 %slice-start.6 = ((s8[7077888]{0:T(1024)(128)(4,1)}), s8[2883584]{0:T(1024)(128)(4,1)S(1)}, s32[]{:S(2)}) async-start(s8[7077888]{0:T(1024)(128)(4,1)} %bitcast.111), calls=%async_computation.11 | async-start | bytes 5767168
  77.2 12.2 %copy-start.3 = (f32[16]{0:T(128)S(1)}, f32[16]{0:T(128)}, u32[]{:S(2)}) copy-start(f32[16]{0:T(128)} %param.9) | copy-start | bytes 196
  77.2 38.2 %slice-start = ((s8[9437184]{0:T(1024)(128)(4,1)}), s8[4194304]{0:T(1024)(128)(4,1)S(1)}, s32[]{:S(2)}) async-start(s8[9437184]{0:T(1024)(128)(4,1)} %bitcast.96), calls=%async_computation.5 | async-start | bytes 8388608
  89.4 26.0 %slice-start.1 = ((s8[9437184]{0:T(1024)(128)(4,1)}), s8[4194304]{0:T(1024)(128)(4,1)S(1)}, s32[]{:S(2)}) async-start(s8[9437184]{0:T(1024)(128)(4,1)} %bitcast.96), calls=%async_computation.6 | async-start | bytes 8388608
  89.4 26.0 %slice-start.2 = ((s8[9437184]{0:T(1024)(128)(4,1)}), s8[1048576]{0:T(1024)(128)(4,1)S(1)}, s32[]{:S(2)}) async-start(s8[9437184]{0:T(1024)(128)(4,1)} %bitcast.96), calls=%async_computation.7 | async-start | bytes 2097152
  115.4 13.5 %slice-start.3 = ((s8[7077888]{0:T(1024)(128)(4,1)}), s8[4194304]{0:T(1024)(128)(4,1)S(1)}, s32[]{:S(2)}) async-start(s8[7077888]{0:T(1024)(128)(4,1)} %bitcast.100), calls=%async_computation.8 | async-start | bytes 8388608
  115.4 13.4 %slice-start.4 = ((s8[7077888]{0:T(1024)(128)(4,1)}), s8[2883584]{0:T(1024)(128)(4,1)S(1)}, s32[]{:S(2)}) async-start(s8[7077888]{0:T(1024)(128)(4,1)} %bitcast.100), calls=%async_computation.9 | async-start | bytes 5767168
  214.7 24.1 %copy-start.2 = (f32[4,1,16,256]{3,2,1,0:T(8,128)S(1)}, f32[4,1,16,256]{3,2,1,0:T(8,128)}, u32[]{:S(2)}) copy-start(f32[4,1,16,256]{3,2,1,0:T(8,128)} %reduce-scatter.3.cloned.1.call-done) | copy-start | bytes 196612
  214.7 335.3 %all-reduce.3.cloned.1.call-start = ((), (), s32[]{:S(2)}) async-start(), calls=%async_computation.4 | async-start | bytes 2097152 | tf_op jit(solution)/shard_map/psum | solution.py:96
Sparse Core Ops, SparseCore 0:
  39.1 29.4 reduce-scatter.2
  214.8 23.9 reduce-scatter.4
  241.8 308.1 all-reduce.2
where the time goes:
time: 568 us; the launch traced here: 559 us
  waiting for transfers between devices  277 us (49%)
  matrix products  147 us (26%)
  blocking collectives  80.2 us (14%)
  local copies, waits for them, and re-layouts  28.3 us (5%)
  between operations  14.3 us (3%)
  other arithmetic  12.4 us (2%)
    psum x1, waiting for transfers between devices, shards(): grad_spec = lax.psum(local_spec, 'dp')  264 us
    psum x1, blocking collectives, shards(): total_point, total_bias = lax.psum((local_point, local_bias), ('dp', 'gz'))  65.4 us
    dot_general x2, matrix products, add_inverse(): return jnp.einsum('ax,asoz->soxz', row_basis, inner, precision=highest)  51.8 us
    mul x2, local copies, waits for them, and re-layouts, kron_table(): outer = basis[:, None, :, None] * basis[None, :, None, :]  25.7 us
    dot_general x2, matrix products, to_modes(): lax.dot_general(flattened, kron, contract_cells, precision=highest)  24.5 us
    dot_general x2, matrix products, add_inverse(): jnp.dot(piece.reshape(piece_rows * samples_dev * channels, M * M), kron,...  24.4 us
    dot_general x1, matrix products, shards(): jnp.einsum('sixz,soxz->io', field, grad_pre, preferred_element_type=jnp.f...  17.8 us
    dot_general x1, matrix products, shards(): jnp.einsum('soxz,io->sixz', grad_pre, point_weight, preferred_element_typ...  16 us
  transfers between devices with their start and end apart: 3, of which 3 were waited for; matrix products, arithmetic and copies ran while one was open for 14% of the time, Pallas kernels for 0%

commit v1 on v0

v1 whole, which is shorter than its diff:
```python
import functools
import math

import jax
import jax.numpy as jnp
import numpy as np
from jax import lax
from jax.experimental import pallas as pl
from jax.experimental.pallas import tpu as pltpu
from jax.sharding import PartitionSpec as P

N = 96
M = 16
C = 16
GZ = 4
ROWS = N // GZ
CELLS = N * N
MODES = M * M
OWNED = M // GZ * C
SUB = 8

root_half = 0.7071067811865476
density_norm = 0.3989422804014327
scale_fwd = (2.0 / N) ** 1.5
scale_inv = (2.0 / M) ** 1.5
HIGHEST = lax.Precision.HIGHEST
NT = (((1,), (1,)), ((), ()))
TN = (((0,), (0,)), ((), ()))
VMEM_LIMIT = 48 << 20


def basis_table():
    mode_index = np.arange(M)
    half_count = M // 2
    frequency = np.where(mode_index < half_count, mode_index, mode_index - half_count + 1)
    turns = frequency[:, None] * np.arange(N)[None, :] % N
    angle = turns.astype(np.float64) * (2.0 * math.pi / N)
    return np.where((mode_index < half_count)[:, None], np.cos(angle), np.sin(angle)).astype(
        np.float32
    )


def row_matrices(basis):
    out = np.zeros((GZ, M, C, C, ROWS), np.float32)
    for slab in range(GZ):
        for channel in range(C):
            out[slab, :, channel, channel, :] = basis[:, slab * ROWS : (slab + 1) * ROWS]
    return out.reshape(GZ, M * C, C * ROWS)


def gelu_slope(values):
    cumulative = 0.5 * (1.0 + lax.erf(values * root_half))
    return cumulative + values * jnp.exp(-0.5 * values * values) * density_norm


def kron_cells(outer_ref, inner_ref, first, count):
    inner = inner_ref[...]
    parts = [outer_ref[pl.ds(first + k, 1), :] * inner for k in range(count)]
    return jnp.concatenate(parts, 0).astype(jnp.bfloat16)


def one_hot_rows(count, dtype):
    row = lax.broadcasted_iota(jnp.int32, (count * SUB, count), 0) >> 3
    col = lax.broadcasted_iota(jnp.int32, (count * SUB, count), 1)
    return jnp.where(row == col, 1.0, 0.0).astype(dtype)


def same_sub(count):
    row = lax.broadcasted_iota(jnp.int32, (count * SUB, count * SUB), 0) & 7
    col = lax.broadcasted_iota(jnp.int32, (count * SUB, count * SUB), 1) & 7
    return row == col


def spread(weight):
    hot = one_hot_rows(C, jnp.bfloat16)
    tall = jnp.dot(hot, weight, preferred_element_type=jnp.float32).astype(jnp.bfloat16)
    wide = lax.dot_general(tall, hot, NT, preferred_element_type=jnp.float32)
    return jnp.where(same_sub(C), wide, 0.0).astype(jnp.bfloat16)


def send_parts(slab_ref, row_ref, acc, scale, refs):
    for k in range(GZ):
        first = pl.multiple_of((slab_ref[0] ^ k) * OWNED, OWNED)
        rows = row_ref[0, pl.ds(first, OWNED), :]
        refs[k][0:OWNED, :] = scale * jnp.dot(
            rows, acc, precision=HIGHEST, preferred_element_type=jnp.float32
        )


def field_modes_kernel(width, slab_ref, outer_ref, inner_ref, row_ref, field_ref, *rest):
    parts, acc = rest[:GZ], rest[GZ]
    step = pl.program_id(0)

    @pl.when(step == 0)
    def _():
        acc[...] = jnp.zeros_like(acc)

    kron = kron_cells(outer_ref, inner_ref, step * (width // N), width // N)
    acc[...] += jnp.dot(
        field_ref[0].reshape(C * ROWS, width), kron, preferred_element_type=jnp.float32
    )

    @pl.when(step == pl.num_programs(0) - 1)
    def _():
        send_parts(slab_ref, row_ref, acc[...], scale_fwd, parts)


def slope_kernel(
    width,
    sub_width,
    slab_ref,
    outer_ref,
    inner_ref,
    row_ref,
    weight_ref,
    bias_ref,
    mixed_ref,
    field_ref,
    cot_ref,
    dpre_ref,
    *rest,
):
    parts = rest[:GZ]
    lines, blocks, bias_rows, acc, point_acc, kron = rest[GZ:]
    step = pl.program_id(0)

    @pl.when(step == 0)
    def _():
        acc[...] = jnp.zeros_like(acc)
        point_acc[...] = jnp.zeros_like(point_acc)
        full = lax.dot_general(
            row_ref[0], mixed_ref[...], TN, precision=HIGHEST, preferred_element_type=jnp.float32
        )
        lines[...] = (scale_inv * full).reshape(C, ROWS, MODES).astype(jnp.bfloat16)
        blocks[...] = spread(weight_ref[...].T)
        bias_rows[...] = jnp.dot(
            one_hot_rows(C, jnp.float32),
            bias_ref[...],
            precision=HIGHEST,
            preferred_element_type=jnp.float32,
        )

    kron[...] = kron_cells(outer_ref, inner_ref, step * (width // N), width // N)
    for s in range(width // sub_width):
        cols = pl.ds(s * sub_width, sub_width)
        for x in range(ROWS // SUB):
            rows = pl.ds(x * SUB, SUB)
            values = field_ref[0, :, rows, cols].reshape(C * SUB, sub_width)
            pre = lax.dot_general(
                lines[:, rows, :].reshape(C * SUB, MODES),
                kron[cols, :],
                NT,
                preferred_element_type=jnp.float32,
            )
            pre = pre + jnp.dot(blocks[...], values, preferred_element_type=jnp.float32)
            pre = pre + bias_rows[...]
            cot = cot_ref[0, :, rows, cols].reshape(C * SUB, sub_width).astype(jnp.float32)
            dpre = (cot * gelu_slope(pre)).astype(jnp.bfloat16)
            dpre_ref[0, :, rows, cols] = dpre.reshape(C, SUB, sub_width)
    for x in range(ROWS // SUB):
        rows = pl.ds(x * SUB, SUB)
        point_acc[...] += lax.dot_general(
            field_ref[0, :, rows, :].reshape(C * SUB, width),
            dpre_ref[0, :, rows, :].reshape(C * SUB, width),
            NT,
            preferred_element_type=jnp.float32,
        )
    acc[...] += jnp.dot(
        dpre_ref[0].reshape(C * ROWS, width), kron[...], preferred_element_type=jnp.float32
    )

    @pl.when(step == pl.num_programs(0) - 1)
    def _():
        send_parts(slab_ref, row_ref, acc[...], scale_inv, parts)
        hot = one_hot_rows(C, jnp.float32)
        half = jnp.dot(
            jnp.where(same_sub(C), point_acc[...], 0.0),
            hot,
            precision=HIGHEST,
            preferred_element_type=jnp.float32,
        )
        point = lax.dot_general(
            hot, half, TN, precision=HIGHEST, preferred_element_type=jnp.float32
        )
        sums = acc[:, 0:128].reshape(C, ROWS, 128).sum(1)[:, 0:1]
        packed = pack_small(point, sums)
        for k in range(GZ):
            parts[k][OWNED : OWNED + SUB, 0:128] = packed
            parts[k][OWNED : OWNED + SUB, 128:256] = jnp.zeros_like(packed)


def lane_masks():
    row = lax.broadcasted_iota(jnp.int32, (C, 128), 0)
    lane = lax.broadcasted_iota(jnp.int32, (C, 128), 1)
    return row, lane


def pack_small(point, sums):
    row, lane = lane_masks()
    tile = jnp.where((lane & 15) == row, 1.0, 0.0)
    wide = jnp.dot(point, tile, precision=HIGHEST, preferred_element_type=jnp.float32)
    wide = jnp.where((row & 7) == (lane >> 4), wide, 0.0)
    vector = jnp.where(row == lane, sums, 0.0).sum(0, keepdims=True)
    low = wide[0:8].sum(0, keepdims=True)
    high = wide[8:16].sum(0, keepdims=True)
    return jnp.concatenate([low, high, vector, jnp.zeros((5, 128), jnp.float32)], 0)


def unpack_small(packed):
    row, lane = lane_masks()
    wide = jnp.where(row < 8, packed[0:1], packed[1:2])
    wide = jnp.where((row & 7) == (lane >> 4), wide, 0.0)
    tile = jnp.where((lane & 15) == row, 1.0, 0.0)
    point = lax.dot_general(
        wide, tile, NT, precision=HIGHEST, preferred_element_type=jnp.float32
    )
    return point, packed[2:3, 0:C]


def gathered_sum(refs):
    own, one, two, three = (ref[...] for ref in refs)
    return (own + one) + (two + three)


def mix_kernel(own_ref, one_ref, two_ref, three_ref, weight_ref, coef_ref, mixed_ref):
    coef = gathered_sum((own_ref, one_ref, two_ref, three_ref))
    coef_ref[...] = coef
    for a in range(M // GZ):
        total = jnp.zeros((C, MODES), jnp.float32)
        for i in range(C):
            total = total + coef_ref[a * C + i : a * C + i + 1, :] * weight_ref[a, i]
        mixed_ref[a * C : (a + 1) * C, :] = total


def back_kernel(own_ref, one_ref, two_ref, three_ref, weight_ref, coef_ref, back_ref, send_ref):
    full = gathered_sum((own_ref, one_ref, two_ref, three_ref))
    small = full[OWNED : OWNED + SUB]
    for a in range(M // GZ):
        grad = full[a * C : (a + 1) * C]
        for i in range(C):
            back_ref[a * C + i : a * C + i + 1, :] = (weight_ref[a, i] * grad).sum(
                0, keepdims=True
            )
        for pair in range(C // 2):
            owner = a * (C // 2) + pair
            first = a * C + 2 * pair
            send_ref[owner, 0:C, :] = grad
            send_ref[owner, C : C + SUB, :] = jnp.concatenate(
                [coef_ref[first : first + 2, :], small[0:6]], 0
            )


def outer_kernel(spec_norm, cell_norm, got_ref, spread_ref, point_ref, bias_ref):
    samples = got_ref.shape[0]

    def body(s, carry):
        zero, one, small = carry
        grad = got_ref[s, 0:C, :]
        tail = got_ref[s, C : C + SUB, :]
        return zero + tail[0:1] * grad, one + tail[1:2] * grad, small + tail

    start = (
        jnp.zeros((C, MODES), jnp.float32),
        jnp.zeros((C, MODES), jnp.float32),
        jnp.zeros((SUB, MODES), jnp.float32),
    )
    zero, one, small = lax.fori_loop(0, samples, body, start, unroll=8)
    zero = zero * spec_norm
    one = one * spec_norm
    for k in range(samples):
        spread_ref[k, 0] = zero
        spread_ref[k, 1] = one
    point, sums = unpack_small(small[2:8, 0:128])
    point_ref[...] = point * cell_norm
    bias_ref[...] = sums * cell_norm


def field_grad_kernel(
    width,
    sub_width,
    slab_ref,
    outer_ref,
    inner_ref,
    row_ref,
    weight_ref,
    back_ref,
    dpre_ref,
    out_ref,
    lines,
    blocks,
    kron,
):
    step = pl.program_id(0)

    @pl.when(step == 0)
    def _():
        full = lax.dot_general(
            row_ref[0], back_ref[...], TN, precision=HIGHEST, preferred_element_type=jnp.float32
        )
        lines[...] = (scale_fwd * full).reshape(C, ROWS, MODES).astype(jnp.bfloat16)
        blocks[...] = spread(weight_ref[...])

    kron[...] = kron_cells(outer_ref, inner_ref, step * (width // N), width // N)
    for s in range(width // sub_width):
        cols = pl.ds(s * sub_width, sub_width)
        for x in range(ROWS // SUB):
            rows = pl.ds(x * SUB, SUB)
            dpre = dpre_ref[0, :, rows, cols].reshape(C * SUB, sub_width)
            out = lax.dot_general(
                lines[:, rows, :].reshape(C * SUB, MODES),
                kron[cols, :],
                NT,
                preferred_element_type=jnp.float32,
            )
            out = out + jnp.dot(blocks[...], dpre, preferred_element_type=jnp.float32)
            out_ref[0, :, rows, cols] = out.astype(jnp.bfloat16).reshape(C, SUB, sub_width)


def whole(shape):
    return pl.BlockSpec(shape, lambda step, slab: (0,) * len(shape))


def cells(width):
    return pl.BlockSpec((1, C, ROWS, width), lambda step, slab: (0, 0, 0, step))


def slab_rows():
    return pl.BlockSpec((1, M * C, C * ROWS), lambda step, slab: (slab[0], 0, 0))


def f32(*shape):
    return jax.ShapeDtypeStruct(shape, jnp.float32)


params = pltpu.CompilerParams(vmem_limit_bytes=VMEM_LIMIT)


def shards(field, cotangent, spec_weight, point_weight, bias):
    dp = lax.axis_size("dp")
    basis = basis_table()
    slab = lax.axis_index("gz").astype(jnp.int32).reshape(1)
    outer_rows = jnp.asarray(np.repeat(basis.T, M, axis=1))
    inner_rows = jnp.asarray(np.tile(basis.T, (1, M)))
    row_mats = jnp.asarray(row_matrices(basis))

    def exchange(parts):
        got = [parts[0]]
        for k in range(1, GZ):
            got.append(lax.ppermute(parts[k], "gz", [(g, g ^ k) for g in range(GZ)]))
        return got

    width = 2304
    coef_parts = pl.pallas_call(
        functools.partial(field_modes_kernel, width),
        out_shape=tuple(f32(OWNED, MODES) for _ in range(GZ)),
        grid_spec=pltpu.PrefetchScalarGridSpec(
            num_scalar_prefetch=1,
            grid=(CELLS // width,),
            in_specs=[whole((N, MODES)), whole((N, MODES)), slab_rows(), cells(width)],
            out_specs=tuple(whole((OWNED, MODES)) for _ in range(GZ)),
            scratch_shapes=[pltpu.VMEM((C * ROWS, MODES), jnp.float32)],
        ),
        compiler_params=params,
        name="field_modes",
    )(slab, outer_rows, inner_rows, row_mats, field)

    coef, mixed = pl.pallas_call(
        mix_kernel,
        out_shape=(f32(OWNED, MODES), f32(OWNED, MODES)),
        compiler_params=params,
        name="mix_modes",
    )(*exchange(coef_parts), spec_weight)
    mixed_all = lax.all_gather(mixed, "gz", axis=0, tiled=True)

    width = 1152
    dpre, *grad_parts = pl.pallas_call(
        functools.partial(slope_kernel, width, 384),
        out_shape=(jax.ShapeDtypeStruct(field.shape, jnp.bfloat16),)
        + tuple(f32(OWNED + SUB, MODES) for _ in range(GZ)),
        grid_spec=pltpu.PrefetchScalarGridSpec(
            num_scalar_prefetch=1,
            grid=(CELLS // width,),
            in_specs=[
                whole((N, MODES)),
                whole((N, MODES)),
                slab_rows(),
                whole((C, C)),
                whole((C, 1)),
                whole((M * C, MODES)),
                cells(width),
                cells(width),
            ],
            out_specs=(cells(width),) + tuple(whole((OWNED + SUB, MODES)) for _ in range(GZ)),
            scratch_shapes=[
                pltpu.VMEM((C, ROWS, MODES), jnp.bfloat16),
                pltpu.VMEM((C * SUB, C * SUB), jnp.bfloat16),
                pltpu.VMEM((C * SUB, 1), jnp.float32),
                pltpu.VMEM((C * ROWS, MODES), jnp.float32),
                pltpu.VMEM((C * SUB, C * SUB), jnp.float32),
                pltpu.VMEM((width, MODES), jnp.bfloat16),
            ],
        ),
        compiler_params=params,
        name="slope_and_modes",
    )(
        slab,
        outer_rows,
        inner_rows,
        row_mats,
        point_weight,
        bias.reshape(C, 1),
        mixed_all,
        field,
        cotangent,
    )

    back, send = pl.pallas_call(
        back_kernel,
        out_shape=(f32(OWNED, MODES), f32(dp, C + SUB, MODES)),
        compiler_params=params,
        name="back_modes",
    )(*exchange(grad_parts), spec_weight, coef)

    got = lax.all_to_all(send, "dp", 0, 0, tiled=True)
    cell_norm = 1.0 / math.sqrt(dp * N * N * N)
    copies, point_grad, bias_grad = pl.pallas_call(
        functools.partial(outer_kernel, 1.0 / math.sqrt(dp * N), cell_norm),
        out_shape=(f32(dp, 2, C, MODES), f32(C, C), f32(1, C)),
        compiler_params=params,
        name="sample_sum",
    )(got)
    spec_grad = lax.all_to_all(copies, "dp", 0, 0, tiled=True)

    back_all = lax.all_gather(back, "gz", axis=0, tiled=True)
    width = 2304
    field_grad = pl.pallas_call(
        functools.partial(field_grad_kernel, width, 384),
        out_shape=jax.ShapeDtypeStruct(field.shape, jnp.bfloat16),
        grid_spec=pltpu.PrefetchScalarGridSpec(
            num_scalar_prefetch=1,
            grid=(CELLS // width,),
            in_specs=[
                whole((N, MODES)),
                whole((N, MODES)),
                slab_rows(),
                whole((C, C)),
                whole((M * C, MODES)),
                cells(width),
            ],
            out_specs=cells(width),
            scratch_shapes=[
                pltpu.VMEM((C, ROWS, MODES), jnp.bfloat16),
                pltpu.VMEM((C * SUB, C * SUB), jnp.bfloat16),
                pltpu.VMEM((width, MODES), jnp.bfloat16),
            ],
        ),
        compiler_params=params,
        name="field_grad",
    )(slab, outer_rows, inner_rows, row_mats, point_weight, back_all, dpre)

    return (
        field_grad,
        spec_grad.reshape(M // GZ, C, C, MODES),
        point_grad,
        bias_grad.reshape(C),
    )


def solution(mesh):
    return jax.shard_map(
        shards,
        mesh=mesh,
        in_specs=(
            P("dp", None, "gz", None),
            P("dp", None, "gz", None),
            P("gz", None, None, None),
            P(),
            P(),
        ),
        out_specs=(P("dp", None, "gz", None), P("gz", None, None, None), P(), P()),
        check_vma=False,
    )
```

time: 568 us -> 111 us (0.20); the launches traced: 559 us -> 109 us
  waiting for transfers between devices: 277 us -> 9.78 us
  matrix products: 147 us -> 0 us
  Pallas kernels: 0 us -> 37.6 us
  blocking collectives: 80.2 us -> 45.3 us
  local copies, waits for them, and re-layouts: 28.3 us -> 4.27 us
  between operations: 14.3 us -> 0.71 us
  other arithmetic: 12.4 us -> 0 us
  starting transfers between devices: 0.12 us -> 11.2 us
    psum x1 -> x0, waiting for transfers between devices: 264 us -> none  [shards(): grad_spec = lax.psum(local_spec, 'dp')]
    dot_general x11 -> x0, matrix products: 147 us -> none  [the longest x2 51.8 us: add_inverse(): return jnp.einsum('ax,asoz->soxz', row_basis, inner, precision=highest)]
    psum x1 -> x0, blocking collectives: 65.4 us -> none  [shards(): total_point, total_bias = lax.psum((local_point, local_bias), ('dp', 'gz'))]
    pallas_call x0 -> x6, Pallas kernels: none -> 37.6 us  [the longest x1 18.9 us: shards(): pl.pallas_call(functools.partial(slope_kernel, width, 384), out_shape=(ja...]
    mul x4 -> x0, local copies, waits for them, and re-layouts: 27.4 us -> none  [the longest x2 25.7 us: kron_table(): outer = basis[:, None, :, None] * basis[None, :, None, :]]
    all_to_all x0 -> x1, blocking collectives: none -> 22.5 us  [shards(): got = lax.all_to_all(send, 'dp', 0, 0, tiled=True)]
    reduce_scatter x2 -> x0, waiting for transfers between devices: 13.1 us -> none  [the longest x1 8.07 us: shards(): lax.psum_scatter(scale_inv * jnp.einsum('ax,soxp->asop', rows_part, grad_...]
    ppermute x0 -> x6, waiting for transfers between devices: none -> 9.78 us  [exchange(): got.append(lax.ppermute(parts[k], 'gz', [(g, g ^ k) for g in range(GZ)]))]
  transfers between devices with their start and end apart: 3 -> 7, of which waited for: 3 -> 4; matrix products, arithmetic and copies ran while one was open for 14% -> 0% of each run, Pallas kernels for 0% -> 10%
where the time goes in v1:
time: 111 us; the launch traced here: 109 us
  blocking collectives  45.3 us (41%)
  Pallas kernels  37.6 us (34%)
  starting transfers between devices  11.2 us (10%)
  waiting for transfers between devices  9.78 us (9%)
  local copies, waits for them, and re-layouts  4.27 us (4%)
    all_to_all x1, blocking collectives, shards(): got = lax.all_to_all(send, 'dp', 0, 0, tiled=True)  22.5 us
    pallas_call x1, Pallas kernels, shards(): pl.pallas_call(functools.partial(slope_kernel, width, 384), out_shape=(ja...  18.9 us
    all_gather x1, blocking collectives, shards(): back_all = lax.all_gather(back, 'gz', axis=0, tiled=True)  15.5 us
    pallas_call x1, Pallas kernels, shards(): pl.pallas_call(functools.partial(field_grad_kernel, width, 384), out_shap...  11.1 us
    ppermute x6, waiting for transfers between devices, exchange(): got.append(lax.ppermute(parts[k], 'gz', [(g, g ^ k) for g in range(GZ)]))  9.78 us
    all_gather x1, blocking collectives, shards(): mixed_all = lax.all_gather(mixed, 'gz', axis=0, tiled=True)  7.29 us
    ppermute x6, starting transfers between devices, exchange(): got.append(lax.ppermute(parts[k], 'gz', [(g, g ^ k) for g in range(GZ)]))  6.87 us
    pallas_call x1, Pallas kernels, shards(): pl.pallas_call(functools.partial(field_modes_kernel, width), out_shape=tu...  6.15 us
  transfers between devices with their start and end apart: 7, of which 4 were waited for; matrix products, arithmetic and copies ran while one was open for 0% of the time, Pallas kernels for 10%

profile of v1, /device:TPU:0, one launch (start us, length us, event | category | flops | bytes accessed | tf_op | source)
XLA Modules:
  0.0 108.9 jit_solution(2756766125030436645)
XLA Ops:
  0.6 0.0 copy-start.8
  0.6 0.0 copy-start.7
  0.7 0.0 copy-start
  0.7 1.4 %copy-done = f32[4,256,384]{2,1,0:T(8,128)S(1)} copy-done((f32[4,256,384]{2,1,0:T(8,128)S(1)}, f32[4,256,384]{2,1,0:T(8,128)}, u32[]{:S(2)}) %copy-start) | copy-done | bytes 1572888
  2.1 0.0 copy-start.3
  2.1 0.9 copy-done.3
  3.0 0.0 copy-start.5
  3.0 0.9 copy-done.5
  3.9 0.0 copy-start.2
  3.9 0.0 copy-start.1
  3.9 0.0 copy-start.4
  3.9 0.0 copy-start.6
  3.9 6.2 %field_modes.1 = (f32[64,256]{1,0:T(8,128)S(1)}, f32[64,256]{1,0:T(8,128)S(1)}, f32[64,256]{1,0:T(8,128)S(1)}, f32[64,256]{1,0:T(8,128)S(1)}) custom-call(s32[1]{0:T(128)} %bitcast.slab_ref, f32[96,256]{1,0:T(8,128)S(1)} %copy-done.5, f32[96,256]{1,0:T(8,128)S(1)} %copy-done.3, f32[4,256,384]{2,1,0:T(8,128)S(1)} %copy-done, bf16[1,16,24,9216]{3,2,1,0:T(8,128)(2,1)} %field_ref.3), custom_call_target="tpu_custom_call" | custom-call | tf_op jit(solution)/shard_map/field_modes/pallas_call | solution.py:353
  10.0 0.1 collective-permute-start
  10.1 3.4 %collective-permute-start.1 = (f32[64,256]{1,0:T(8,128)S(1)}, f32[64,256]{1,0:T(8,128)S(1)}, u32[]{:S(2)}, u32[]{:S(2)}) collective-permute-start(f32[64,256]{1,0:T(8,128)S(1)} %get-tuple-element.22), channel_id=1, source_target_pairs={{0,2},{1,3},{2,0},{3,1},{4,6},{5,7},{6,4},{7,5},{8,10},{9,11},{10,... | collective-permute-start | bytes 196616 | tf_op jit(solution)/shard_map/ppermute | solution.py:349
  13.5 0.1 collective-permute-start.2
  13.5 0.0 copy-done.8
  13.5 0.1 copy.12.bias_ref
  13.6 0.0 collective-permute-done.one_ref
  13.6 2.5 %collective-permute-done.1.two_ref = f32[64,256]{1,0:T(8,128)S(1)} collective-permute-done((f32[64,256]{1,0:T(8,128)S(1)}, f32[64,256]{1,0:T(8,128)S(1)}, u32[]{:S(2)}, u32[]{:S(2)}) %collective-permute-start.1) | collective-permute-done | bytes 65568 | tf_op jit(solution)/shard_map/ppermute | solution.py:349
  16.2 2.9 %collective-permute-done.2.three_ref = f32[64,256]{1,0:T(8,128)S(1)} collective-permute-done((f32[64,256]{1,0:T(8,128)S(1)}, f32[64,256]{1,0:T(8,128)S(1)}, u32[]{:S(2)}, u32[]{:S(2)}) %collective-permute-start.2) | collective-permute-done | bytes 65568 | tf_op jit(solution)/shard_map/ppermute | solution.py:349
  19.0 0.0 copy-done.2
  19.1 0.1 mix_modes.1
  19.1 7.3 %all_gather.6.mixed_ref = f32[256,256]{1,0:T(8,128)S(1)} all-gather(f32[64,256]{1,0:T(8,128)S(1)} %get-tuple-element.24), channel_id=1, replica_groups=mesh['dp'=32,'gz'=4] {'gz'}, dimensions={0}, use_global_device_ids=true | all-gather | bytes 327680 | tf_op jit(solution)/shard_map/all_gather | solution.py:373
  26.4 0.0 copy-done.7
  26.4 0.0 copy-done.1
  26.4 0.0 copy-done.4
  26.4 0.0 copy-done.6
  26.4 18.9 %slope_and_modes.1 = (bf16[1,16,24,9216]{3,2,1,0:T(8,128)(2,1)}, f32[72,256]{1,0:T(8,128)S(1)}, f32[72,256]{1,0:T(8,128)S(1)}, f32[72,256]{1,0:T(8,128)S(1)}, f32[72,256]{1,0:T(8,128)S(1)}) custom-call(s32[1]{0:T(128)} %bitcast.slab_ref, f32[96,256]{1,0:T(8,128)S(1)} %copy-done.6, f32[96,256]{1,0:T(8,128)S(1)} %copy-done.4, f32[4,256,384]{2,1,0:T(8,128)S(1)} %copy-done.1, ...), custom_call_target="tpu_custom_call" | custom-call | tf_op jit(solution)/shard_map/slope_and_modes/pallas_call | solution.py:376
  45.3 0.4 collective-permute-start.3
  45.7 1.3 %collective-permute-start.4 = (f32[72,256]{1,0:T(8,128)S(1)}, f32[72,256]{1,0:T(8,128)S(1)}, u32[]{:S(2)}, u32[]{:S(2)}) collective-permute-start(f32[72,256]{1,0:T(8,128)S(1)} %get-tuple-element.27), channel_id=1, source_target_pairs={{0,2},{1,3},{2,0},{3,1},{4,6},{5,7},{6,4},{7,5},{8,10},{9,11},{10,... | collective-permute-start | bytes 221192 | tf_op jit(solution)/shard_map/ppermute | solution.py:349
  47.0 1.7 %collective-permute-start.5 = (f32[72,256]{1,0:T(8,128)S(1)}, f32[72,256]{1,0:T(8,128)S(1)}, u32[]{:S(2)}, u32[]{:S(2)}) collective-permute-start(f32[72,256]{1,0:T(8,128)S(1)} %get-tuple-element.28), channel_id=1, source_target_pairs={{0,3},{1,2},{2,1},{3,0},{4,7},{5,6},{6,5},{7,4},{8,11},{9,10},{10,... | collective-permute-start | bytes 221192 | tf_op jit(solution)/shard_map/ppermute | solution.py:349
  48.7 0.0 collective-permute-done.3.one_ref
  48.7 2.9 %collective-permute-done.4.two_ref = f32[72,256]{1,0:T(8,128)S(1)} collective-permute-done((f32[72,256]{1,0:T(8,128)S(1)}, f32[72,256]{1,0:T(8,128)S(1)}, u32[]{:S(2)}, u32[]{:S(2)}) %collective-permute-start.4) | collective-permute-done | bytes 73760 | tf_op jit(solution)/shard_map/ppermute | solution.py:349
  51.6 1.4 %collective-permute-done.5.three_ref = f32[72,256]{1,0:T(8,128)S(1)} collective-permute-done((f32[72,256]{1,0:T(8,128)S(1)}, f32[72,256]{1,0:T(8,128)S(1)}, u32[]{:S(2)}, u32[]{:S(2)}) %collective-permute-start.5) | collective-permute-done | bytes 73760 | tf_op jit(solution)/shard_map/ppermute | solution.py:349
  53.0 0.2 back_modes.1
  53.3 22.5 %all_to_all.10.got_ref = f32[32,24,256]{2,1,0:T(8,128)S(1)} all-to-all(f32[32,24,256]{2,1,0:T(8,128)S(1)} %get-tuple-element.32), channel_id=1, replica_groups=mesh['dp'=32,'gz'=4] {'dp'}, dimensions={0} | all-to-all | bytes 1572864 | tf_op jit(solution)/shard_map/all_to_all | solution.py:424
  75.7 1.1 %sample_sum.1 = (f32[32,2,16,256]{3,2,1,0:T(8,128)}, f32[16,16]{1,0:T(8,128)}, f32[1,16]{1,0:T(1,128)}) custom-call(f32[32,24,256]{2,1,0:T(8,128)S(1)} %all_to_all.10.got_ref), custom_call_target="tpu_custom_call" | custom-call | tf_op jit(solution)/shard_map/sample_sum/pallas_call | solution.py:426
  76.9 4.4 %all-to-all-start.1 = ((f32[32,2,16,256]{3,2,1,0:T(8,128)}), f32[32,2,16,256]{3,2,1,0:T(8,128)S(1)}, u32[]{:S(2)}, u32[]{:S(2)}) async-start(f32[32,2,16,256]{3,2,1,0:T(8,128)} %get-tuple-element.33), calls=%async_computation.1 | async-start | bytes 2097152 | tf_op jit(solution)/shard_map/all_to_all | solution.py:432
  81.3 15.5 %all_gather.7.back_ref = f32[256,256]{1,0:T(8,128)S(1)} all-gather(f32[64,256]{1,0:T(8,128)S(1)} %get-tuple-element.30), channel_id=1, replica_groups=mesh['dp'=32,'gz'=4] {'gz'}, dimensions={0}, use_global_device_ids=true | all-gather | bytes 327680 | tf_op jit(solution)/shard_map/all_gather | solution.py:434
  96.8 11.1 %field_grad.1 = bf16[1,16,24,9216]{3,2,1,0:T(8,128)(2,1)} custom-call(s32[1]{0:T(128)} %bitcast.slab_ref, f32[96,256]{1,0:T(8,128)S(1)} %copy-done.6, f32[96,256]{1,0:T(8,128)S(1)} %copy-done.4, f32[4,256,384]{2,1,0:T(8,128)S(1)} %copy-done.1, bf16[16,16]{1,0:T(8,128)(2,1)S(1)} %copy-done.7, f32[256,256]{1,0:T(8,128)S(1)} %all_gather.7.back_ref, ...), custom_call_target="tpu_custom_call" | custom-call | tf_op jit(solution)/shard_map/field_grad/pallas_call | solution.py:436
  107.9 0.0 all-to-all-done.1
  107.9 1.0 copy.14
Async XLA Ops:
  0.6 12.9 %copy-start.8 = (f32[16]{0:T(128)S(1)}, f32[16]{0:T(128)}, u32[]{:S(2)}) copy-start(f32[16]{0:T(128)} %param.12) | copy-start | bytes 196
  0.6 25.8 %copy-start.7 = (bf16[16,16]{1,0:T(8,128)(2,1)S(1)}, bf16[16,16]{1,0:T(8,128)(2,1)}, u32[]{:S(2)}) copy-start(bf16[16,16]{1,0:T(8,128)(2,1)} %weight_ref.7) | copy-start | bytes 1540
  0.7 1.4 %copy-start = (f32[4,256,384]{2,1,0:T(8,128)S(1)}, f32[4,256,384]{2,1,0:T(8,128)}, u32[]{:S(2)}) copy-start(f32[4,256,384]{2,1,0:T(8,128)} %constant.12.clone.row_ref) | copy-start | bytes 4718596
  2.1 0.9 copy-start.3
  3.0 0.9 copy-start.5
  3.9 15.2 %copy-start.2 = (f32[4,16,16,256]{3,2,1,0:T(8,128)S(1)}, f32[4,16,16,256]{3,2,1,0:T(8,128)}, u32[]{:S(2)}) copy-start(f32[4,16,16,256]{3,2,1,0:T(8,128)} %weight_ref.6) | copy-start | bytes 3145732
  3.9 22.6 %copy-start.1 = (f32[4,256,384]{2,1,0:T(8,128)S(1)}, f32[4,256,384]{2,1,0:T(8,128)}, u32[]{:S(2)}) copy-start(f32[4,256,384]{2,1,0:T(8,128)} %constant.12.clone.row_ref) | copy-start | bytes 4718596
  3.9 22.6 %copy-start.4 = (f32[96,256]{1,0:T(8,128)S(1)}, f32[96,256]{1,0:T(8,128)}, u32[]{:S(2)}) copy-start(f32[96,256]{1,0:T(8,128)} %constant.11.clone.inner_ref) | copy-start | bytes 294916
  3.9 22.6 %copy-start.6 = (f32[96,256]{1,0:T(8,128)S(1)}, f32[96,256]{1,0:T(8,128)}, u32[]{:S(2)}) copy-start(f32[96,256]{1,0:T(8,128)} %constant.10.clone.outer_ref) | copy-start | bytes 294916
  10.0 3.6 %collective-permute-start = (f32[64,256]{1,0:T(8,128)S(1)}, f32[64,256]{1,0:T(8,128)S(1)}, u32[]{:S(2)}, u32[]{:S(2)}) collective-permute-start(f32[64,256]{1,0:T(8,128)S(1)} %get-tuple-element.21), channel_id=1, source_target_pairs={{0,1},{1,0},{2,3},{3,2},{4,5},{5,4},{6,7},{7,6},{8,9},{9,8},{10,11... | collective-permute-start | bytes 196616 | tf_op jit(solution)/shard_map/ppermute | solution.py:349
  10.1 6.0 %collective-permute-start.1 = (f32[64,256]{1,0:T(8,128)S(1)}, f32[64,256]{1,0:T(8,128)S(1)}, u32[]{:S(2)}, u32[]{:S(2)}) collective-permute-start(f32[64,256]{1,0:T(8,128)S(1)} %get-tuple-element.22), channel_id=1, source_target_pairs={{0,2},{1,3},{2,0},{3,1},{4,6},{5,7},{6,4},{7,5},{8,10},{9,11},{10,... | collective-permute-start | bytes 196616 | tf_op jit(solution)/shard_map/ppermute | solution.py:349
  13.5 5.6 %collective-permute-start.2 = (f32[64,256]{1,0:T(8,128)S(1)}, f32[64,256]{1,0:T(8,128)S(1)}, u32[]{:S(2)}, u32[]{:S(2)}) collective-permute-start(f32[64,256]{1,0:T(8,128)S(1)} %get-tuple-element.23), channel_id=1, source_target_pairs={{0,3},{1,2},{2,1},{3,0},{4,7},{5,6},{6,5},{7,4},{8,11},{9,10},{10,... | collective-permute-start | bytes 196616 | tf_op jit(solution)/shard_map/ppermute | solution.py:349
  45.3 3.4 %collective-permute-start.3 = (f32[72,256]{1,0:T(8,128)S(1)}, f32[72,256]{1,0:T(8,128)S(1)}, u32[]{:S(2)}, u32[]{:S(2)}) collective-permute-start(f32[72,256]{1,0:T(8,128)S(1)} %get-tuple-element.26), channel_id=1, source_target_pairs={{0,1},{1,0},{2,3},{3,2},{4,5},{5,4},{6,7},{7,6},{8,9},{9,8},{10,11... | collective-permute-start | bytes 221192 | tf_op jit(solution)/shard_map/ppermute | solution.py:349
  45.7 5.9 %collective-permute-start.4 = (f32[72,256]{1,0:T(8,128)S(1)}, f32[72,256]{1,0:T(8,128)S(1)}, u32[]{:S(2)}, u32[]{:S(2)}) collective-permute-start(f32[72,256]{1,0:T(8,128)S(1)} %get-tuple-element.27), channel_id=1, source_target_pairs={{0,2},{1,3},{2,0},{3,1},{4,6},{5,7},{6,4},{7,5},{8,10},{9,11},{10,... | collective-permute-start | bytes 221192 | tf_op jit(solution)/shard_map/ppermute | solution.py:349
  47.0 6.0 %collective-permute-start.5 = (f32[72,256]{1,0:T(8,128)S(1)}, f32[72,256]{1,0:T(8,128)S(1)}, u32[]{:S(2)}, u32[]{:S(2)}) collective-permute-start(f32[72,256]{1,0:T(8,128)S(1)} %get-tuple-element.28), channel_id=1, source_target_pairs={{0,3},{1,2},{2,1},{3,0},{4,7},{5,6},{6,5},{7,4},{8,11},{9,10},{10,... | collective-permute-start | bytes 221192 | tf_op jit(solution)/shard_map/ppermute | solution.py:349
  76.9 31.0 %all-to-all-start.1 = ((f32[32,2,16,256]{3,2,1,0:T(8,128)}), f32[32,2,16,256]{3,2,1,0:T(8,128)S(1)}, u32[]{:S(2)}, u32[]{:S(2)}) async-start(f32[32,2,16,256]{3,2,1,0:T(8,128)} %get-tuple-element.33), calls=%async_computation.1 | async-start | bytes 2097152 | tf_op jit(solution)/shard_map/all_to_all | solution.py:432

commit v2 on v0

v2 whole, which is shorter than its diff:
```python
import functools
import math

import jax
import jax.numpy as jnp
from jax import lax
from jax.experimental import pallas as pl
from jax.experimental.pallas import tpu as pltpu
from jax.sharding import PartitionSpec as P

N = 96
M = 16
C = 16
GZ = 4
ROWS = N // GZ
CELLS = N * N
MODES = M * M
OWNED = M // GZ * C
SUB = 8
LANES = 128
CHUNKS = 6
WIDTH = CELLS // CHUNKS

bf16 = jnp.bfloat16
root_half = 0.7071067811865476
density_norm = 0.3989422804014327
scale_fwd = (2.0 / N) ** 1.5
scale_inv = (2.0 / M) ** 1.5
HIGHEST = lax.Precision.HIGHEST
NN = (((1,), (0,)), ((), ()))
NT = (((1,), (1,)), ((), ()))
TN = (((0,), (0,)), ((), ()))


def gelu_slope(values):
    cumulative = 0.5 * (1.0 + lax.erf(values * root_half))
    return cumulative + values * jnp.exp(-0.5 * values * values) * density_norm


def matmul(a, b, dims=NN):
    return lax.dot_general(a, b, dims, preferred_element_type=jnp.float32)


def split(values):
    high = values.astype(bf16)
    return high, (values - high.astype(jnp.float32)).astype(bf16)


def product(a, b, dims):
    return matmul(a[0], b[0], dims) + (matmul(a[0], b[1], dims) + matmul(a[1], b[0], dims))


def iota(shape, dim):
    return lax.broadcasted_iota(jnp.int32, shape, dim)


def quotient(values, divisor):
    return jnp.floor((values + 0.5) * (1.0 / divisor))


def basis_at(mode, position):
    cosine = mode < M // 2
    frequency = jnp.where(cosine, mode, mode - (M // 2 - 1))
    turns = frequency * position + jnp.where(cosine, 0.0, 0.75 * N)
    turns = turns - N * quotient(turns, N)
    return jnp.cos(turns * (2.0 * math.pi / N))


def cell_tables():
    mode = iota((N, MODES), 1)
    cell = iota((N, MODES), 0).astype(jnp.float32)
    outer = basis_at((mode >> 4).astype(jnp.float32), cell)
    return outer, basis_at((mode & 15).astype(jnp.float32), cell)


def row_matrix(slab):
    col = iota((M, C * ROWS), 1).astype(jnp.float32)
    x = col - ROWS * quotient(col, ROWS) + (slab * ROWS).astype(jnp.float32)
    table = basis_at(iota((M, C * ROWS), 0).astype(jnp.float32), x)
    wide = jnp.broadcast_to(table[:, None, :], (M, C, C * ROWS)).reshape(M * C, C * ROWS)
    row_channel = (iota((M * C, C * ROWS), 0) & 15).astype(jnp.float32)
    col_channel = quotient(iota((M * C, C * ROWS), 1).astype(jnp.float32), ROWS)
    return jnp.where(row_channel == col_channel, wide, 0.0)


def one_hot_rows(dtype):
    hit = (iota((C * SUB, C), 0) >> 3) == iota((C * SUB, C), 1)
    return jnp.where(hit, 1.0, 0.0).astype(dtype)


def same_sub():
    return (iota((C * SUB, C * SUB), 0) & 7) == (iota((C * SUB, C * SUB), 1) & 7)


def spread(weight):
    hot = one_hot_rows(bf16)
    tall = matmul(hot, weight).astype(bf16)
    return jnp.where(same_sub(), matmul(tall, hot, NT), 0.0).astype(bf16)


def send_parts(slab, high_ref, low_ref, acc, scale, refs):
    pair = split(acc)
    for k in range(GZ):
        first = pl.multiple_of((slab ^ k) * OWNED, OWNED)
        rows = (high_ref[pl.ds(first, OWNED), :], low_ref[pl.ds(first, OWNED), :])
        refs[k][0:OWNED, :] = scale * product(rows, pair, NN)


def chunk(step):
    return pl.ds(pl.multiple_of(step * WIDTH, LANES), WIDTH)


def copies_in(source, target, sems):
    def copy(step):
        cols = chunk(step)
        return pltpu.make_async_copy(
            source.at[0, :, :, cols], target.at[:, :, cols], sems.at[step]
        )

    return copy


def copies_out(source, target, sems):
    def copy(step):
        cols = chunk(step)
        return pltpu.make_async_copy(
            source.at[:, :, cols], target.at[0, :, :, cols], sems.at[step]
        )

    return copy


def kron_rows(outer, inner, step):
    table = inner[...]
    rows = [
        (outer[pl.ds(step * (WIDTH // N) + k, 1), :] * table).astype(bf16)
        for k in range(WIDTH // N)
    ]
    return jnp.concatenate(rows, 0)


def field_modes_kernel(slab_ref, field_hbm, *rest):
    parts = rest[:GZ]
    outer, inner, high, low, field, acc, sems = rest[GZ:]
    fetch = copies_in(field_hbm, field, sems)
    for step in range(CHUNKS):
        fetch(step).start()
    outer[...], inner[...] = cell_tables()
    high[...], low[...] = split(row_matrix(slab_ref[0]))
    acc[...] = jnp.zeros_like(acc)

    def body(step, carry):
        kron = kron_rows(outer, inner, step)
        fetch(step).wait()
        acc[...] += matmul(field[:, :, chunk(step)].reshape(C * ROWS, WIDTH), kron)
        return carry

    lax.fori_loop(0, CHUNKS, body, 0)
    send_parts(slab_ref[0], high, low, acc[...], scale_fwd, parts)


def slope_kernel(
    sub_width,
    slab_ref,
    field_hbm,
    cot_hbm,
    outer,
    inner,
    high,
    low,
    weight_ref,
    bias_ref,
    mixed_ref,
    dpre_hbm,
    *rest,
):
    parts = rest[:GZ]
    down, bias_rows, field, cot, out, lines, acc, point_acc, kron, kron_t, *sems = rest[GZ:]
    field_sems, cot_sems, out_sems = sems
    fetch_field = copies_in(field_hbm, field, field_sems)
    fetch_cot = copies_in(cot_hbm, cot, cot_sems)
    store = copies_out(out, dpre_hbm, out_sems)
    for step in range(CHUNKS):
        fetch_field(step).start()
        fetch_cot(step).start()
    down[...] = spread(weight_ref[...].T)
    bias_rows[...] = jnp.dot(
        one_hot_rows(jnp.float32),
        bias_ref[...],
        precision=HIGHEST,
        preferred_element_type=jnp.float32,
    )
    full = product((high[...], low[...]), split(mixed_ref[...]), TN)
    lines[...] = (scale_inv * full).reshape(C, ROWS, MODES).astype(bf16)
    acc[...] = jnp.zeros_like(acc)
    point_acc[...] = jnp.zeros_like(point_acc)

    def body(step, carry):
        kron[...] = kron_rows(outer, inner, step)
        kron_t[...] = kron[...].T
        fetch_field(step).wait()
        fetch_cot(step).wait()
        for s in range(WIDTH // sub_width):
            cols = pl.ds(pl.multiple_of(step * WIDTH + s * sub_width, LANES), sub_width)
            table = kron_t[:, s * sub_width : (s + 1) * sub_width]
            for x in range(ROWS // SUB):
                rows = slice(x * SUB, (x + 1) * SUB)
                values = field[:, rows, cols].reshape(C * SUB, sub_width)
                left = jnp.concatenate([lines[:, rows, :].reshape(C * SUB, MODES), down[...]], 1)
                pre = matmul(left, jnp.concatenate([table, values], 0))
                pre = pre + bias_rows[...]
                grad = cot[:, rows, cols].reshape(C * SUB, sub_width).astype(jnp.float32)
                dpre = (grad * gelu_slope(pre)).astype(bf16)
                out[:, rows, cols] = dpre.reshape(C, SUB, sub_width)
        store(step).start()
        cols = chunk(step)
        for x in range(ROWS // SUB):
            rows = slice(x * SUB, (x + 1) * SUB)
            point_acc[...] += matmul(
                field[:, rows, cols].reshape(C * SUB, WIDTH),
                out[:, rows, cols].reshape(C * SUB, WIDTH),
                NT,
            )
        acc[...] += matmul(out[:, :, cols].reshape(C * ROWS, WIDTH), kron[...])
        return carry

    lax.fori_loop(0, CHUNKS, body, 0)
    send_parts(slab_ref[0], high, low, acc[...], scale_inv, parts)
    hot = one_hot_rows(jnp.float32)
    half = jnp.dot(
        jnp.where(same_sub(), point_acc[...], 0.0),
        hot,
        precision=HIGHEST,
        preferred_element_type=jnp.float32,
    )
    point = lax.dot_general(hot, half, TN, precision=HIGHEST, preferred_element_type=jnp.float32)
    sums = acc[:, 0:LANES].reshape(C, ROWS, LANES).sum(1)[:, 0:1]
    packed = pack_small(point, sums)
    for k in range(GZ):
        parts[k][OWNED : OWNED + SUB, 0:LANES] = packed
        parts[k][OWNED : OWNED + SUB, LANES:MODES] = jnp.zeros_like(packed)
    for step in range(CHUNKS):
        store(step).wait()


def lane_masks():
    return iota((C, LANES), 0), iota((C, LANES), 1)


def pack_small(point, sums):
    row, lane = lane_masks()
    tile = jnp.where((lane & 15) == row, 1.0, 0.0)
    wide = jnp.dot(point, tile, precision=HIGHEST, preferred_element_type=jnp.float32)
    wide = jnp.where((row & 7) == (lane >> 4), wide, 0.0)
    vector = jnp.where(row == lane, sums, 0.0).sum(0, keepdims=True)
    low = wide[0:8].sum(0, keepdims=True)
    high = wide[8:16].sum(0, keepdims=True)
    return jnp.concatenate([low, high, vector, jnp.zeros((5, LANES), jnp.float32)], 0)


def unpack_small(packed):
    row, lane = lane_masks()
    wide = jnp.where(row < 8, packed[0:1], packed[1:2])
    wide = jnp.where((row & 7) == (lane >> 4), wide, 0.0)
    tile = jnp.where((lane & 15) == row, 1.0, 0.0)
    point = lax.dot_general(wide, tile, NT, precision=HIGHEST, preferred_element_type=jnp.float32)
    return point, packed[2:3, 0:C]


def gathered_sum(refs):
    own, one, two, three = (ref[...] for ref in refs)
    return (own + one) + (two + three)


def mix_kernel(own_ref, one_ref, two_ref, three_ref, weight_ref, coef_ref, mixed_ref):
    coef = gathered_sum((own_ref, one_ref, two_ref, three_ref))
    coef_ref[...] = coef
    for a in range(M // GZ):
        total = jnp.zeros((C, MODES), jnp.float32)
        for i in range(C):
            total = total + coef_ref[a * C + i : a * C + i + 1, :] * weight_ref[a, i]
        mixed_ref[a * C : (a + 1) * C, :] = total


def pieces():
    for owner in range(M // GZ * 8):
        yield owner, owner // 8, owner // 4 % 2 * SUB, owner // 2 % 2 * SUB, owner % 2 * LANES


def back_kernel(own_ref, one_ref, two_ref, three_ref, weight_ref, coef_ref, back_ref, send_ref):
    full = gathered_sum((own_ref, one_ref, two_ref, three_ref))
    small = full[OWNED : OWNED + SUB, 0:LANES]
    for owner, a, i, o, p in pieces():
        send_ref[owner, 0:SUB, :] = coef_ref[a * C + i : a * C + i + SUB, p : p + LANES]
        send_ref[owner, SUB : 2 * SUB, :] = full[a * C + o : a * C + o + SUB, p : p + LANES]
        send_ref[owner, 2 * SUB : 3 * SUB, :] = small
    for a in range(M // GZ):
        grad = full[a * C : (a + 1) * C]
        for i in range(C):
            back_ref[a * C + i : a * C + i + 1, :] = (weight_ref[a, i] * grad).sum(
                0, keepdims=True
            )


def outer_kernel(spec_norm, cell_norm, got_ref, copies_ref, point_ref, bias_ref):
    samples = got_ref.shape[0]

    def body(s, carry):
        *totals, small = carry
        coef = got_ref[s, 0:SUB, :]
        grad = got_ref[s, SUB : 2 * SUB, :]
        totals = [total + coef[i : i + 1] * grad for i, total in enumerate(totals)]
        return (*totals, small + got_ref[s, 2 * SUB : 3 * SUB, :])

    zero = jnp.zeros((SUB, LANES), jnp.float32)
    *totals, small = lax.fori_loop(0, samples, body, (zero,) * (SUB + 1), unroll=8)
    for i, total in enumerate(totals):
        scaled = total * spec_norm
        for k in range(samples):
            copies_ref[k, i] = scaled
    point, sums = unpack_small(small)
    point_ref[...] = point * cell_norm
    bias_ref[...] = sums * cell_norm


def place_kernel(got_ref, out_ref):
    for owner, a, i, o, p in pieces():
        out_ref[a, i : i + SUB, o : o + SUB, p : p + LANES] = got_ref[owner]


def field_grad_kernel(
    sub_width,
    dpre_hbm,
    outer,
    inner,
    high,
    low,
    weight_ref,
    back_ref,
    out_hbm,
    up,
    dpre,
    out,
    lines,
    kron_t,
    dpre_sems,
    out_sems,
):
    fetch = copies_in(dpre_hbm, dpre, dpre_sems)
    store = copies_out(out, out_hbm, out_sems)
    for step in range(CHUNKS):
        fetch(step).start()
    up[...] = spread(weight_ref[...])
    full = product((high[...], low[...]), split(back_ref[...]), TN)
    lines[...] = (scale_fwd * full).reshape(C, ROWS, MODES).astype(bf16)

    def body(step, carry):
        kron_t[...] = kron_rows(outer, inner, step).T
        fetch(step).wait()
        for s in range(WIDTH // sub_width):
            cols = pl.ds(pl.multiple_of(step * WIDTH + s * sub_width, LANES), sub_width)
            table = kron_t[:, s * sub_width : (s + 1) * sub_width]
            for x in range(ROWS // SUB):
                rows = slice(x * SUB, (x + 1) * SUB)
                values = dpre[:, rows, cols].reshape(C * SUB, sub_width)
                left = jnp.concatenate([lines[:, rows, :].reshape(C * SUB, MODES), up[...]], 1)
                grad = matmul(left, jnp.concatenate([table, values], 0))
                out[:, rows, cols] = grad.astype(bf16).reshape(C, SUB, sub_width)
        store(step).start()
        return carry

    lax.fori_loop(0, CHUNKS, body, 0)
    for step in range(CHUNKS):
        store(step).wait()


def shaped(*shape, dtype=jnp.float32):
    return jax.ShapeDtypeStruct(shape, dtype)


def limit(mebibytes):
    return pltpu.CompilerParams(vmem_limit_bytes=mebibytes << 20)


VM = pl.BlockSpec(memory_space=pltpu.VMEM)
SM = pl.BlockSpec(memory_space=pltpu.SMEM)
ANY = pl.BlockSpec(memory_space=pl.ANY)


def shards(field, cotangent, spec_weight, point_weight, bias):
    dp = lax.axis_size("dp")
    slab = lax.axis_index("gz").astype(jnp.int32).reshape(1)

    def exchange(parts):
        got = [parts[0]]
        for k in range(1, GZ):
            got.append(lax.ppermute(parts[k], "gz", [(g, g ^ k) for g in range(GZ)]))
        return got

    *coef_parts, outer, inner, high, low = pl.pallas_call(
        field_modes_kernel,
        out_shape=tuple(shaped(OWNED, MODES) for _ in range(GZ))
        + (
            shaped(N, MODES),
            shaped(N, MODES),
            shaped(M * C, C * ROWS, dtype=bf16),
            shaped(M * C, C * ROWS, dtype=bf16),
        ),
        in_specs=[SM, ANY],
        out_specs=(VM,) * (GZ + 4),
        scratch_shapes=[
            pltpu.VMEM((C, ROWS, CELLS), bf16),
            pltpu.VMEM((C * ROWS, MODES), jnp.float32),
            pltpu.SemaphoreType.DMA((CHUNKS,)),
        ],
        compiler_params=limit(53),
        name="field_modes",
    )(slab, field)

    coef, mixed = pl.pallas_call(
        mix_kernel,
        out_shape=(shaped(OWNED, MODES), shaped(OWNED, MODES)),
        compiler_params=limit(8),
        name="mix_modes",
    )(*exchange(coef_parts), spec_weight)
    mixed_all = lax.all_gather(mixed, "gz", axis=0, tiled=True)

    dpre, *grad_parts = pl.pallas_call(
        functools.partial(slope_kernel, 768),
        out_shape=(jax.ShapeDtypeStruct(field.shape, bf16),)
        + tuple(shaped(OWNED + SUB, MODES) for _ in range(GZ)),
        in_specs=[SM, ANY, ANY] + [VM] * 7,
        out_specs=(ANY,) + (VM,) * GZ,
        scratch_shapes=[
            pltpu.VMEM((C * SUB, C * SUB), bf16),
            pltpu.VMEM((C * SUB, 1), jnp.float32),
            pltpu.VMEM((C, ROWS, CELLS), bf16),
            pltpu.VMEM((C, ROWS, CELLS), bf16),
            pltpu.VMEM((C, ROWS, CELLS), bf16),
            pltpu.VMEM((C, ROWS, MODES), bf16),
            pltpu.VMEM((C * ROWS, MODES), jnp.float32),
            pltpu.VMEM((C * SUB, C * SUB), jnp.float32),
            pltpu.VMEM((WIDTH, MODES), bf16),
            pltpu.VMEM((MODES, WIDTH), bf16),
            pltpu.SemaphoreType.DMA((CHUNKS,)),
            pltpu.SemaphoreType.DMA((CHUNKS,)),
            pltpu.SemaphoreType.DMA((CHUNKS,)),
        ],
        compiler_params=limit(53),
        name="slope_and_modes",
    )(
        slab,
        field,
        cotangent,
        outer,
        inner,
        high,
        low,
        point_weight,
        bias.reshape(C, 1),
        mixed_all,
    )

    back, send = pl.pallas_call(
        back_kernel,
        out_shape=(shaped(OWNED, MODES), shaped(dp, 3 * SUB, LANES)),
        compiler_params=limit(8),
        name="back_modes",
    )(*exchange(grad_parts), spec_weight, coef)

    got = lax.all_to_all(send, "dp", 0, 0, tiled=True)
    back_all = lax.all_gather(back, "gz", axis=0, tiled=True)
    got, back_all = lax.optimization_barrier((got, back_all))
    copies, point_grad, bias_grad = pl.pallas_call(
        functools.partial(
            outer_kernel, 1.0 / math.sqrt(dp * N), 1.0 / math.sqrt(dp * N * N * N)
        ),
        out_shape=(shaped(dp, SUB, SUB, LANES), shaped(C, C), shaped(1, C)),
        compiler_params=limit(8),
        name="sample_sum",
    )(got)
    owned = lax.all_to_all(copies, "dp", 0, 0, tiled=True)

    field_grad = pl.pallas_call(
        functools.partial(field_grad_kernel, 768),
        out_shape=jax.ShapeDtypeStruct(field.shape, bf16),
        in_specs=[ANY] + [VM] * 6,
        out_specs=ANY,
        scratch_shapes=[
            pltpu.VMEM((C * SUB, C * SUB), bf16),
            pltpu.VMEM((C, ROWS, CELLS), bf16),
            pltpu.VMEM((C, ROWS, CELLS), bf16),
            pltpu.VMEM((C, ROWS, MODES), bf16),
            pltpu.VMEM((MODES, WIDTH), bf16),
            pltpu.SemaphoreType.DMA((CHUNKS,)),
            pltpu.SemaphoreType.DMA((CHUNKS,)),
        ],
        compiler_params=limit(54),
        cost_estimate=pl.CostEstimate(
            flops=2 * C * ROWS * CELLS * (MODES + C * SUB),
            bytes_accessed=2 * C * ROWS * CELLS * 2,
            transcendentals=0,
        ),
        name="field_grad",
    )(dpre, outer, inner, high, low, point_weight, back_all)

    spec_grad = pl.pallas_call(
        place_kernel,
        out_shape=shaped(M // GZ, C, C, MODES),
        compiler_params=limit(8),
        name="place_pieces",
    )(owned)
    return field_grad, spec_grad, point_grad, bias_grad.reshape(C)


def solution(mesh):
    return jax.shard_map(
        shards,
        mesh=mesh,
        in_specs=(
            P("dp", None, "gz", None),
            P("dp", None, "gz", None),
            P("gz", None, None, None),
            P(),
            P(),
        ),
        out_specs=(P("dp", None, "gz", None), P("gz", None, None, None), P(), P()),
        check_vma=False,
    )
```

time: 568 us -> 95.9 us (0.17); the launches traced: 559 us -> 95.5 us
  waiting for transfers between devices: 277 us -> 17.7 us
  matrix products: 147 us -> 0 us
  blocking collectives: 80.2 us -> 17.7 us
  Pallas kernels: 0 us -> 36.8 us
  local copies, waits for them, and re-layouts: 28.3 us -> 0.11 us
  starting transfers between devices: 0.12 us -> 22.4 us
  between operations: 14.3 us -> 0.78 us
  other arithmetic: 12.4 us -> 0 us
    psum x1 -> x0, waiting for transfers between devices: 264 us -> none  [shards(): grad_spec = lax.psum(local_spec, 'dp')]
    dot_general x11 -> x0, matrix products: 147 us -> none  [the longest x2 51.8 us: add_inverse(): return jnp.einsum('ax,asoz->soxz', row_basis, inner, precision=highest)]
    psum x1 -> x0, blocking collectives: 65.4 us -> none  [shards(): total_point, total_bias = lax.psum((local_point, local_bias), ('dp', 'gz'))]
    pallas_call x0 -> x7, Pallas kernels: none -> 36.8 us  [the longest x1 18.6 us: shards(): pl.pallas_call(functools.partial(slope_kernel, 768), out_shape=(jax.Shape...]
    mul x4 -> x0, local copies, waits for them, and re-layouts: 27.4 us -> none  [the longest x2 25.7 us: kron_table(): outer = basis[:, None, :, None] * basis[None, :, None, :]]
    all_to_all x0 -> x2, starting transfers between devices: none -> 15.4 us  [the longest x1 8.47 us: shards(): got = lax.all_to_all(send, 'dp', 0, 0, tiled=True)]
    reduce_scatter x2 -> x0, waiting for transfers between devices: 13.1 us -> none  [the longest x1 8.07 us: shards(): lax.psum_scatter(scale_inv * jnp.einsum('ax,soxp->asop', rows_part, grad_...]
    ppermute x0 -> x6, waiting for transfers between devices: none -> 9.76 us  [exchange(): got.append(lax.ppermute(parts[k], 'gz', [(g, g ^ k) for g in range(GZ)]))]
  transfers between devices with their start and end apart: 3 -> 8, of which waited for: 3 -> 6; matrix products, arithmetic and copies ran while one was open for 14% -> 0% of each run, Pallas kernels for 0% -> 10%
where the time goes in v2:
time: 95.9 us; the launch traced here: 95.5 us
  Pallas kernels  36.8 us (38%)
  starting transfers between devices  22.4 us (23%)
  waiting for transfers between devices  17.7 us (18%)
  blocking collectives  17.7 us (18%)
    pallas_call x1, Pallas kernels, shards(): pl.pallas_call(functools.partial(slope_kernel, 768), out_shape=(jax.Shape...  18.6 us
    all_gather x1, blocking collectives, shards(): back_all = lax.all_gather(back, 'gz', axis=0, tiled=True)  9.95 us
    ppermute x6, waiting for transfers between devices, exchange(): got.append(lax.ppermute(parts[k], 'gz', [(g, g ^ k) for g in range(GZ)]))  9.76 us
    pallas_call x1, Pallas kernels, shards(): pl.pallas_call(functools.partial(field_grad_kernel, 768), out_shape=jax.S...  9.75 us
    all_to_all x1, starting transfers between devices, shards(): got = lax.all_to_all(send, 'dp', 0, 0, tiled=True)  8.47 us
    all_gather x1, blocking collectives, shards(): mixed_all = lax.all_gather(mixed, 'gz', axis=0, tiled=True)  7.74 us
    all_to_all x1, waiting for transfers between devices, shards(): owned = lax.all_to_all(copies, 'dp', 0, 0, tiled=True)  7.2 us
    all_to_all x1, starting transfers between devices, shards(): owned = lax.all_to_all(copies, 'dp', 0, 0, tiled=True)  6.96 us
  transfers between devices with their start and end apart: 8, of which 6 were waited for; matrix products, arithmetic and copies ran while one was open for 0% of the time, Pallas kernels for 10%

profile of v2, /device:TPU:0, one launch (start us, length us, event | category | flops | bytes accessed | tf_op | source)
XLA Modules:
  0.0 95.5 jit_solution(16538789585706831400)
XLA Ops:
  0.6 0.0 copy-start.6
  0.6 0.0 copy-start
  0.7 0.0 copy-start.5
  0.7 5.3 %field_modes.1 = (f32[64,256]{1,0:T(8,128)S(1)}, f32[64,256]{1,0:T(8,128)S(1)}, f32[64,256]{1,0:T(8,128)S(1)}, f32[64,256]{1,0:T(8,128)S(1)}, f32[96,256]{1,0:T(...) custom-call(s32[1]{0:T(128)} %bitcast.slab_ref, ...), custom_call_target="tpu_custom_call" | custom-call | tf_op jit(solution)/shard_map/field_modes/pallas_call | solution.py:400
  6.0 0.0 copy-start.1
  6.0 0.0 copy-start.2
  6.0 0.0 copy-start.3
  6.0 0.0 copy-start.4
  6.0 0.1 collective-permute-start
  6.1 3.4 %collective-permute-start.1 = (f32[64,256]{1,0:T(8,128)S(1)}, f32[64,256]{1,0:T(8,128)S(1)}, u32[]{:S(2)}, u32[]{:S(2)}) collective-permute-start(f32[64,256]{1,0:T(8,128)S(1)} %get-tuple-element.32), channel_id=1, source_target_pairs={{0,2},{1,3},{2,0},{3,1},{4,6},{5,7},{6,4},{7,5},{8,10},{9,11},{10,... | collective-permute-start | bytes 196616 | tf_op jit(solution)/shard_map/ppermute | solution.py:397
  9.5 0.1 collective-permute-start.2
  9.5 0.0 copy-done.6
  9.5 0.1 copy.9.bias_ref
  9.6 0.0 collective-permute-done.one_ref
  9.6 2.5 %collective-permute-done.1.two_ref = f32[64,256]{1,0:T(8,128)S(1)} collective-permute-done((f32[64,256]{1,0:T(8,128)S(1)}, f32[64,256]{1,0:T(8,128)S(1)}, u32[]{:S(2)}, u32[]{:S(2)}) %collective-permute-start.1) | collective-permute-done | bytes 65568 | tf_op jit(solution)/shard_map/ppermute | solution.py:397
  12.1 2.9 %collective-permute-done.2.three_ref = f32[64,256]{1,0:T(8,128)S(1)} collective-permute-done((f32[64,256]{1,0:T(8,128)S(1)}, f32[64,256]{1,0:T(8,128)S(1)}, u32[]{:S(2)}, u32[]{:S(2)}) %collective-permute-start.2) | collective-permute-done | bytes 65568 | tf_op jit(solution)/shard_map/ppermute | solution.py:397
  15.0 0.0 copy-done
  15.0 0.1 mix_modes.1
  15.1 7.7 %all_gather.6.mixed_ref = f32[256,256]{1,0:T(8,128)} all-gather(f32[64,256]{1,0:T(8,128)S(1)} %get-tuple-element.34), channel_id=1, replica_groups=mesh['dp'=32,'gz'=4] {'gz'}, dimensions={0}, use_global_device_ids=true | all-gather | bytes 327680 | tf_op jit(solution)/shard_map/all_gather | solution.py:426
  22.9 0.0 copy-done.5
  22.9 18.6 %slope_and_modes.1 = (bf16[1,16,24,9216]{3,2,1,0:T(8,128)(2,1)}, f32[72,256]{1,0:T(8,128)S(1)}, f32[72,256]{1,0:T(8,128)S(1)}, f32[72,256]{1,0:T(8,128)S(1)}, f32[72,256]{1,0:T(8,128)S(1)}) custom-call(s32[1]{0:T(128)} %bitcast.slab_ref, bf16[1,16,24,9216]{3,2,1,0:T(8,128)(2,1)} %field_hbm.3, bf16[1,16,24,9216]{3,2,1,0:T(8,128)(2,1)} %cot_hbm.1, ...), custom_call_target="tpu_custom_call" | custom-call | tf_op jit(solution)/shard_map/slope_and_modes/pallas_call | solution.py:428
  41.5 0.0 copy-done.1
  41.5 0.0 copy-done.2
  41.5 0.0 copy-done.3
  41.6 0.0 copy-done.4
  41.6 0.4 collective-permute-start.3
  42.0 1.3 %collective-permute-start.4 = (f32[72,256]{1,0:T(8,128)S(1)}, f32[72,256]{1,0:T(8,128)S(1)}, u32[]{:S(2)}, u32[]{:S(2)}) collective-permute-start(f32[72,256]{1,0:T(8,128)S(1)} %get-tuple-element.38), channel_id=1, source_target_pairs={{0,2},{1,3},{2,0},{3,1},{4,6},{5,7},{6,4},{7,5},{8,10},{9,11},{10,... | collective-permute-start | bytes 221192 | tf_op jit(solution)/shard_map/ppermute | solution.py:397
  43.3 1.7 %collective-permute-start.5 = (f32[72,256]{1,0:T(8,128)S(1)}, f32[72,256]{1,0:T(8,128)S(1)}, u32[]{:S(2)}, u32[]{:S(2)}) collective-permute-start(f32[72,256]{1,0:T(8,128)S(1)} %get-tuple-element.39), channel_id=1, source_target_pairs={{0,3},{1,2},{2,1},{3,0},{4,7},{5,6},{6,5},{7,4},{8,11},{9,10},{10,... | collective-permute-start | bytes 221192 | tf_op jit(solution)/shard_map/ppermute | solution.py:397
  45.0 0.0 collective-permute-done.3.one_ref
  45.0 2.9 %collective-permute-done.4.two_ref = f32[72,256]{1,0:T(8,128)S(1)} collective-permute-done((f32[72,256]{1,0:T(8,128)S(1)}, f32[72,256]{1,0:T(8,128)S(1)}, u32[]{:S(2)}, u32[]{:S(2)}) %collective-permute-start.4) | collective-permute-done | bytes 73760 | tf_op jit(solution)/shard_map/ppermute | solution.py:397
  47.9 1.4 %collective-permute-done.5.three_ref = f32[72,256]{1,0:T(8,128)S(1)} collective-permute-done((f32[72,256]{1,0:T(8,128)S(1)}, f32[72,256]{1,0:T(8,128)S(1)}, u32[]{:S(2)}, u32[]{:S(2)}) %collective-permute-start.5) | collective-permute-done | bytes 73760 | tf_op jit(solution)/shard_map/ppermute | solution.py:397
  49.3 0.8 back_modes.1
  50.1 8.5 %all-to-all-start = ((f32[32,24,128]{2,1,0:T(8,128)}), f32[32,24,128]{2,1,0:T(8,128)S(1)}, u32[]{:S(2)}, u32[]{:S(2)}) async-start(f32[32,24,128]{2,1,0:T(8,128)} %get-tuple-element.41), calls=%async_computation | async-start | bytes 786432 | tf_op jit(solution)/shard_map/all_to_all | solution.py:471
  58.6 10.0 %all_gather.7.back_ref = f32[256,256]{1,0:T(8,128)} all-gather(f32[64,256]{1,0:T(8,128)S(1)} %get-tuple-element.42), channel_id=1, replica_groups=mesh['dp'=32,'gz'=4] {'gz'}, dimensions={0}, use_global_device_ids=true | all-gather | bytes 327680 | tf_op jit(solution)/shard_map/all_gather | solution.py:472
  68.6 0.8 all-to-all-done.got_ref
  69.3 1.2 %sample_sum.1 = (f32[32,8,8,128]{3,2,1,0:T(8,128)}, f32[16,16]{1,0:T(8,128)}, f32[1,16]{1,0:T(1,128)}) custom-call(f32[32,24,128]{2,1,0:T(8,128)S(1)} %all-to-all-done.got_ref), custom_call_target="tpu_custom_call" | custom-call | tf_op jit(solution)/shard_map/sample_sum/pallas_call | solution.py:474
  70.5 7.0 %all-to-all-start.1 = ((f32[32,8,8,128]{3,2,1,0:T(8,128)}), f32[32,8,8,128]{3,2,1,0:T(8,128)S(1)}, u32[]{:S(2)}, u32[]{:S(2)}) async-start(f32[32,8,8,128]{3,2,1,0:T(8,128)} %get-tuple-element.45), calls=%async_computation.1 | async-start | bytes 2097152 | tf_op jit(solution)/shard_map/all_to_all | solution.py:482
  77.5 9.7 %field_grad.1 = bf16[1,16,24,9216]{3,2,1,0:T(8,128)(2,1)} custom-call(bf16[1,16,24,9216]{3,2,1,0:T(8,128)(2,1)} %get-tuple-element.35.dpre_hbm, f32[96,256]{1,0:T(8,128)} %copy-done.3, f32[96,256]{1,0:T(8,128)} %copy-done.4, bf16[256,384]{1,0:T(8,128)(2,1)} %copy-done.1, bf16[256,384]{1,0:T(8,128)(2,1)} %copy-done.2, bf16[16,16]{1,0:T(8,128)(2,1)} %weight_ref.7, ...), custom_call_target="tpu_custom_call" | custom-call | flops 2717908992 | bytes 14155776 | tf_op jit(solution)/shard_map/field_grad/pallas_call | solution.py:484
  87.2 7.2 %all-to-all-done.1.got_ref = f32[32,8,8,128]{3,2,1,0:T(8,128)S(1)} async-done(((f32[32,8,8,128]{3,2,1,0:T(8,128)}), f32[32,8,8,128]{3,2,1,0:T(8,128)S(1)}, u32[]{:S(2)}, u32[]{:S(2)}) %all-to-all-start.1) | async-done | bytes 1048608 | tf_op jit(solution)/shard_map/all_to_all | solution.py:482
  94.4 1.0 %place_pieces.1 = f32[4,16,16,256]{3,2,1,0:T(8,128)} custom-call(f32[32,8,8,128]{3,2,1,0:T(8,128)S(1)} %all-to-all-done.1.got_ref), custom_call_target="tpu_custom_call" | custom-call | tf_op jit(solution)/shard_map/place_pieces/pallas_call | solution.py:507
Async XLA Ops:
  0.6 8.9 %copy-start.6 = (f32[16]{0:T(128)S(1)}, f32[16]{0:T(128)}, u32[]{:S(2)}) copy-start(f32[16]{0:T(128)} %param.9) | copy-start | bytes 196
  0.6 14.4 %copy-start = (f32[4,16,16,256]{3,2,1,0:T(8,128)S(1)}, f32[4,16,16,256]{3,2,1,0:T(8,128)}, u32[]{:S(2)}) copy-start(f32[4,16,16,256]{3,2,1,0:T(8,128)} %weight_ref.6) | copy-start | bytes 3145732
  0.7 22.2 %copy-start.5 = (bf16[16,16]{1,0:T(8,128)(2,1)S(1)}, bf16[16,16]{1,0:T(8,128)(2,1)}, u32[]{:S(2)}) copy-start(bf16[16,16]{1,0:T(8,128)(2,1)} %weight_ref.7) | copy-start | bytes 1540
  6.0 35.5 %copy-start.1 = (bf16[256,384]{1,0:T(8,128)(2,1)}, bf16[256,384]{1,0:T(8,128)(2,1)S(1)}, u32[]{:S(2)}) copy-start(bf16[256,384]{1,0:T(8,128)(2,1)S(1)} %get-tuple-element.28.high) | copy-start | bytes 589828
  6.0 35.5 %copy-start.2 = (bf16[256,384]{1,0:T(8,128)(2,1)}, bf16[256,384]{1,0:T(8,128)(2,1)S(1)}, u32[]{:S(2)}) copy-start(bf16[256,384]{1,0:T(8,128)(2,1)S(1)} %get-tuple-element.29.low) | copy-start | bytes 589828
  6.0 35.5 %copy-start.3 = (f32[96,256]{1,0:T(8,128)}, f32[96,256]{1,0:T(8,128)S(1)}, u32[]{:S(2)}) copy-start(f32[96,256]{1,0:T(8,128)S(1)} %get-tuple-element.26.outer) | copy-start | bytes 294916
  6.0 35.5 %copy-start.4 = (f32[96,256]{1,0:T(8,128)}, f32[96,256]{1,0:T(8,128)S(1)}, u32[]{:S(2)}) copy-start(f32[96,256]{1,0:T(8,128)S(1)} %get-tuple-element.27.inner) | copy-start | bytes 294916
  6.0 3.6 %collective-permute-start = (f32[64,256]{1,0:T(8,128)S(1)}, f32[64,256]{1,0:T(8,128)S(1)}, u32[]{:S(2)}, u32[]{:S(2)}) collective-permute-start(f32[64,256]{1,0:T(8,128)S(1)} %get-tuple-element.31), channel_id=1, source_target_pairs={{0,1},{1,0},{2,3},{3,2},{4,5},{5,4},{6,7},{7,6},{8,9},{9,8},{10,11... | collective-permute-start | bytes 196616 | tf_op jit(solution)/shard_map/ppermute | solution.py:397
  6.1 6.0 %collective-permute-start.1 = (f32[64,256]{1,0:T(8,128)S(1)}, f32[64,256]{1,0:T(8,128)S(1)}, u32[]{:S(2)}, u32[]{:S(2)}) collective-permute-start(f32[64,256]{1,0:T(8,128)S(1)} %get-tuple-element.32), channel_id=1, source_target_pairs={{0,2},{1,3},{2,0},{3,1},{4,6},{5,7},{6,4},{7,5},{8,10},{9,11},{10,... | collective-permute-start | bytes 196616 | tf_op jit(solution)/shard_map/ppermute | solution.py:397
  9.5 5.6 %collective-permute-start.2 = (f32[64,256]{1,0:T(8,128)S(1)}, f32[64,256]{1,0:T(8,128)S(1)}, u32[]{:S(2)}, u32[]{:S(2)}) collective-permute-start(f32[64,256]{1,0:T(8,128)S(1)} %get-tuple-element.33), channel_id=1, source_target_pairs={{0,3},{1,2},{2,1},{3,0},{4,7},{5,6},{6,5},{7,4},{8,11},{9,10},{10,... | collective-permute-start | bytes 196616 | tf_op jit(solution)/shard_map/ppermute | solution.py:397
  41.6 3.4 %collective-permute-start.3 = (f32[72,256]{1,0:T(8,128)S(1)}, f32[72,256]{1,0:T(8,128)S(1)}, u32[]{:S(2)}, u32[]{:S(2)}) collective-permute-start(f32[72,256]{1,0:T(8,128)S(1)} %get-tuple-element.37), channel_id=1, source_target_pairs={{0,1},{1,0},{2,3},{3,2},{4,5},{5,4},{6,7},{7,6},{8,9},{9,8},{10,11... | collective-permute-start | bytes 221192 | tf_op jit(solution)/shard_map/ppermute | solution.py:397
  42.0 5.9 %collective-permute-start.4 = (f32[72,256]{1,0:T(8,128)S(1)}, f32[72,256]{1,0:T(8,128)S(1)}, u32[]{:S(2)}, u32[]{:S(2)}) collective-permute-start(f32[72,256]{1,0:T(8,128)S(1)} %get-tuple-element.38), channel_id=1, source_target_pairs={{0,2},{1,3},{2,0},{3,1},{4,6},{5,7},{6,4},{7,5},{8,10},{9,11},{10,... | collective-permute-start | bytes 221192 | tf_op jit(solution)/shard_map/ppermute | solution.py:397
  43.3 6.0 %collective-permute-start.5 = (f32[72,256]{1,0:T(8,128)S(1)}, f32[72,256]{1,0:T(8,128)S(1)}, u32[]{:S(2)}, u32[]{:S(2)}) collective-permute-start(f32[72,256]{1,0:T(8,128)S(1)} %get-tuple-element.39), channel_id=1, source_target_pairs={{0,3},{1,2},{2,1},{3,0},{4,7},{5,6},{6,5},{7,4},{8,11},{9,10},{10,... | collective-permute-start | bytes 221192 | tf_op jit(solution)/shard_map/ppermute | solution.py:397
  50.1 19.2 %all-to-all-start = ((f32[32,24,128]{2,1,0:T(8,128)}), f32[32,24,128]{2,1,0:T(8,128)S(1)}, u32[]{:S(2)}, u32[]{:S(2)}) async-start(f32[32,24,128]{2,1,0:T(8,128)} %get-tuple-element.41), calls=%async_computation | async-start | bytes 786432 | tf_op jit(solution)/shard_map/all_to_all | solution.py:471
  70.5 23.9 %all-to-all-start.1 = ((f32[32,8,8,128]{3,2,1,0:T(8,128)}), f32[32,8,8,128]{3,2,1,0:T(8,128)S(1)}, u32[]{:S(2)}, u32[]{:S(2)}) async-start(f32[32,8,8,128]{3,2,1,0:T(8,128)} %get-tuple-element.45), calls=%async_computation.1 | async-start | bytes 2097152 | tf_op jit(solution)/shard_map/all_to_all | solution.py:482

commit v3 on v2

--- a/solution.py
+++ b/solution.py
@@ -107,7 +107,7 @@
 
 
 def chunk(step):
-    return pl.ds(pl.multiple_of(step * WIDTH, LANES), WIDTH)
+    return slice(step * WIDTH, (step + 1) * WIDTH)
 
 
 def copies_in(source, target, sems):
@@ -133,7 +133,7 @@
 def kron_rows(outer, inner, step):
     table = inner[...]
     rows = [
-        (outer[pl.ds(step * (WIDTH // N) + k, 1), :] * table).astype(bf16)
+        (outer[step * (WIDTH // N) + k : step * (WIDTH // N) + k + 1, :] * table).astype(bf16)
         for k in range(WIDTH // N)
     ]
     return jnp.concatenate(rows, 0)
@@ -149,13 +149,10 @@
     high[...], low[...] = split(row_matrix(slab_ref[0]))
     acc[...] = jnp.zeros_like(acc)
 
-    def body(step, carry):
+    for step in range(CHUNKS):
         kron = kron_rows(outer, inner, step)
         fetch(step).wait()
         acc[...] += matmul(field[:, :, chunk(step)].reshape(C * ROWS, WIDTH), kron)
-        return carry
-
-    lax.fori_loop(0, CHUNKS, body, 0)
     send_parts(slab_ref[0], high, low, acc[...], scale_fwd, parts)
 
 
@@ -175,7 +172,7 @@
     *rest,
 ):
     parts = rest[:GZ]
-    down, bias_rows, field, cot, out, lines, acc, point_acc, kron, kron_t, *sems = rest[GZ:]
+    down, bias_cols, field, cot, out, lines, acc, point_acc, kron, kron_t, *sems = rest[GZ:]
     field_sems, cot_sems, out_sems = sems
     fetch_field = copies_in(field_hbm, field, field_sems)
     fetch_cot = copies_in(cot_hbm, cot, cot_sems)
@@ -184,31 +181,41 @@
         fetch_field(step).start()
         fetch_cot(step).start()
     down[...] = spread(weight_ref[...].T)
-    bias_rows[...] = jnp.dot(
-        one_hot_rows(jnp.float32),
-        bias_ref[...],
-        precision=HIGHEST,
-        preferred_element_type=jnp.float32,
+    bias_high, bias_low = split(
+        jnp.dot(
+            one_hot_rows(jnp.float32),
+            bias_ref[...],
+            precision=HIGHEST,
+            preferred_element_type=jnp.float32,
+        )
     )
+    lane = iota((C * SUB, C), 1)
+    bias_cols[...] = jnp.where(
+        lane == 0,
+        bias_high.astype(jnp.float32),
+        jnp.where(lane == 1, bias_low.astype(jnp.float32), 0.0),
+    ).astype(bf16)
+    ones = jnp.ones((C, sub_width), bf16)
     full = product((high[...], low[...]), split(mixed_ref[...]), TN)
     lines[...] = (scale_inv * full).reshape(C, ROWS, MODES).astype(bf16)
     acc[...] = jnp.zeros_like(acc)
     point_acc[...] = jnp.zeros_like(point_acc)
 
-    def body(step, carry):
+    for step in range(CHUNKS):
         kron[...] = kron_rows(outer, inner, step)
         kron_t[...] = kron[...].T
         fetch_field(step).wait()
         fetch_cot(step).wait()
         for s in range(WIDTH // sub_width):
-            cols = pl.ds(pl.multiple_of(step * WIDTH + s * sub_width, LANES), sub_width)
+            cols = slice(step * WIDTH + s * sub_width, step * WIDTH + (s + 1) * sub_width)
             table = kron_t[:, s * sub_width : (s + 1) * sub_width]
             for x in range(ROWS // SUB):
                 rows = slice(x * SUB, (x + 1) * SUB)
                 values = field[:, rows, cols].reshape(C * SUB, sub_width)
-                left = jnp.concatenate([lines[:, rows, :].reshape(C * SUB, MODES), down[...]], 1)
-                pre = matmul(left, jnp.concatenate([table, values], 0))
-                pre = pre + bias_rows[...]
+                left = jnp.concatenate(
+                    [lines[:, rows, :].reshape(C * SUB, MODES), down[...], bias_cols[...]], 1
+                )
+                pre = matmul(left, jnp.concatenate([table, values, ones], 0))
                 grad = cot[:, rows, cols].reshape(C * SUB, sub_width).astype(jnp.float32)
                 dpre = (grad * gelu_slope(pre)).astype(bf16)
                 out[:, rows, cols] = dpre.reshape(C, SUB, sub_width)
@@ -222,9 +229,6 @@
                 NT,
             )
         acc[...] += matmul(out[:, :, cols].reshape(C * ROWS, WIDTH), kron[...])
-        return carry
-
-    lax.fori_loop(0, CHUNKS, body, 0)
     send_parts(slab_ref[0], high, low, acc[...], scale_inv, parts)
     hot = one_hot_rows(jnp.float32)
     half = jnp.dot(
@@ -330,15 +334,20 @@
 
 def field_grad_kernel(
     sub_width,
+    slab_ref,
     dpre_hbm,
     outer,
     inner,
     high,
     low,
     weight_ref,
-    back_ref,
+    own_ref,
+    one_ref,
+    two_ref,
+    three_ref,
     out_hbm,
     up,
+    back,
     dpre,
     out,
     lines,
@@ -351,14 +360,16 @@
     for step in range(CHUNKS):
         fetch(step).start()
     up[...] = spread(weight_ref[...])
-    full = product((high[...], low[...]), split(back_ref[...]), TN)
+    for k, ref in enumerate((own_ref, one_ref, two_ref, three_ref)):
+        back[pl.ds(pl.multiple_of((slab_ref[0] ^ k) * OWNED, OWNED), OWNED), :] = ref[...]
+    full = product((high[...], low[...]), split(back[...]), TN)
     lines[...] = (scale_fwd * full).reshape(C, ROWS, MODES).astype(bf16)
 
-    def body(step, carry):
+    for step in range(CHUNKS):
         kron_t[...] = kron_rows(outer, inner, step).T
         fetch(step).wait()
         for s in range(WIDTH // sub_width):
-            cols = pl.ds(pl.multiple_of(step * WIDTH + s * sub_width, LANES), sub_width)
+            cols = slice(step * WIDTH + s * sub_width, step * WIDTH + (s + 1) * sub_width)
             table = kron_t[:, s * sub_width : (s + 1) * sub_width]
             for x in range(ROWS // SUB):
                 rows = slice(x * SUB, (x + 1) * SUB)
@@ -367,9 +378,6 @@
                 grad = matmul(left, jnp.concatenate([table, values], 0))
                 out[:, rows, cols] = grad.astype(bf16).reshape(C, SUB, sub_width)
         store(step).start()
-        return carry
-
-    lax.fori_loop(0, CHUNKS, body, 0)
     for step in range(CHUNKS):
         store(step).wait()
 
@@ -433,7 +441,7 @@
         out_specs=(ANY,) + (VM,) * GZ,
         scratch_shapes=[
             pltpu.VMEM((C * SUB, C * SUB), bf16),
-            pltpu.VMEM((C * SUB, 1), jnp.float32),
+            pltpu.VMEM((C * SUB, C), bf16),
             pltpu.VMEM((C, ROWS, CELLS), bf16),
             pltpu.VMEM((C, ROWS, CELLS), bf16),
             pltpu.VMEM((C, ROWS, CELLS), bf16),
@@ -469,8 +477,7 @@
     )(*exchange(grad_parts), spec_weight, coef)
 
     got = lax.all_to_all(send, "dp", 0, 0, tiled=True)
-    back_all = lax.all_gather(back, "gz", axis=0, tiled=True)
-    got, back_all = lax.optimization_barrier((got, back_all))
+    back_parts = exchange([back] * GZ)
     copies, point_grad, bias_grad = pl.pallas_call(
         functools.partial(
             outer_kernel, 1.0 / math.sqrt(dp * N), 1.0 / math.sqrt(dp * N * N * N)
@@ -479,15 +486,17 @@
         compiler_params=limit(8),
         name="sample_sum",
     )(got)
+    copies, *back_parts = lax.optimization_barrier((copies, *back_parts))
     owned = lax.all_to_all(copies, "dp", 0, 0, tiled=True)
 
     field_grad = pl.pallas_call(
         functools.partial(field_grad_kernel, 768),
         out_shape=jax.ShapeDtypeStruct(field.shape, bf16),
-        in_specs=[ANY] + [VM] * 6,
+        in_specs=[SM, ANY] + [VM] * 9,
         out_specs=ANY,
         scratch_shapes=[
             pltpu.VMEM((C * SUB, C * SUB), bf16),
+            pltpu.VMEM((M * C, MODES), jnp.float32),
             pltpu.VMEM((C, ROWS, CELLS), bf16),
             pltpu.VMEM((C, ROWS, CELLS), bf16),
             pltpu.VMEM((C, ROWS, MODES), bf16),
@@ -502,7 +511,7 @@
             transcendentals=0,
         ),
         name="field_grad",
-    )(dpre, outer, inner, high, low, point_weight, back_all)
+    )(slab, dpre, outer, inner, high, low, point_weight, *back_parts)
 
     spec_grad = pl.pallas_call(
         place_kernel,

time: 95.9 us -> 92.4 us (0.964)
  blocking collectives: 17.7 us -> 7.92 us
  waiting for transfers between devices: 17.7 us -> 24.9 us
  Pallas kernels: 36.8 us -> 33.5 us
  starting transfers between devices: 22.4 us -> 24.7 us
    all_gather x1 -> x0, blocking collectives: 9.95 us -> none  [shards(): back_all = lax.all_gather(back, 'gz', axis=0, tiled=True)]
    all_to_all x1, waiting for transfers between devices: 0.75 us -> 7.27 us  [shards(): got = lax.all_to_all(send, 'dp', 0, 0, tiled=True)]
    ppermute x6 -> x9, starting transfers between devices: 6.94 us -> 10.5 us  [exchange(): got.append(lax.ppermute(parts[k], 'gz', [(g, g ^ k) for g in range(GZ)]))]
    pallas_call x1, Pallas kernels: 18.6 us -> 15.7 us  [shards(): pl.pallas_call(functools.partial(slope_kernel, 768), out_shape=(jax.Shape...]
    pallas_call x1, Pallas kernels: 9.75 us -> 8.43 us  [shards(): pl.pallas_call(functools.partial(field_grad_kernel, 768), out_shape=jax.S...]
    all_to_all x1, starting transfers between devices: 6.96 us -> 5.88 us  [shards(): owned = lax.all_to_all(copies, 'dp', 0, 0, tiled=True)]
    ppermute x6 -> x9, waiting for transfers between devices: 9.76 us -> 9.62 us  [exchange(): got.append(lax.ppermute(parts[k], 'gz', [(g, g ^ k) for g in range(GZ)]))]
  transfers between devices with their start and end apart: 8 -> 11, of which waited for: 6 -> 6; matrix products, arithmetic and copies ran while one was open for 0% -> 0% of each run, Pallas kernels for 10% -> 10%
where the time goes in v3:
time: 92.4 us; the launch traced here: 92.1 us
  Pallas kernels  33.5 us (36%)
  waiting for transfers between devices  24.9 us (27%)
  starting transfers between devices  24.7 us (27%)
  blocking collectives  7.92 us (9%)
    pallas_call x1, Pallas kernels, shards(): pl.pallas_call(functools.partial(slope_kernel, 768), out_shape=(jax.Shape...  15.7 us
    ppermute x9, starting transfers between devices, exchange(): got.append(lax.ppermute(parts[k], 'gz', [(g, g ^ k) for g in range(GZ)]))  10.5 us
    ppermute x9, waiting for transfers between devices, exchange(): got.append(lax.ppermute(parts[k], 'gz', [(g, g ^ k) for g in range(GZ)]))  9.62 us
    pallas_call x1, Pallas kernels, shards(): pl.pallas_call(functools.partial(field_grad_kernel, 768), out_shape=jax.S...  8.43 us
    all_to_all x1, starting transfers between devices, shards(): got = lax.all_to_all(send, 'dp', 0, 0, tiled=True)  8.33 us
    all_to_all x1, waiting for transfers between devices, shards(): owned = lax.all_to_all(copies, 'dp', 0, 0, tiled=True)  8.05 us
    all_gather x1, blocking collectives, shards(): mixed_all = lax.all_gather(mixed, 'gz', axis=0, tiled=True)  7.92 us
    all_to_all x1, waiting for transfers between devices, shards(): got = lax.all_to_all(send, 'dp', 0, 0, tiled=True)  7.27 us
  transfers between devices with their start and end apart: 11, of which 6 were waited for; matrix products, arithmetic and copies ran while one was open for 0% of the time, Pallas kernels for 10%

profile of v3, /device:TPU:0, one launch (start us, length us, event | category | flops | bytes accessed | tf_op | source)
XLA Modules:
  0.0 92.1 jit_solution(7180349447907752867)
XLA Ops:
  0.6 0.0 copy-start.10
  0.6 0.0 copy-start
  0.7 0.0 copy-start.6
  0.7 6.3 %field_modes.1 = (f32[64,256]{1,0:T(8,128)S(1)}, f32[64,256]{1,0:T(8,128)S(1)}, f32[64,256]{1,0:T(8,128)S(1)}, f32[64,256]{1,0:T(8,128)S(1)}, f32[96,256]{1,0:T(...) custom-call(s32[1]{0:T(128)} %bitcast.slab_ref, ...), custom_call_target="tpu_custom_call" | custom-call | tf_op jit(solution)/shard_map/field_modes/pallas_call | solution.py:408
  6.9 0.0 copy-start.1
  6.9 0.0 copy-start.2
  7.0 0.0 copy-start.3
  7.0 0.0 copy-start.4
  7.0 0.1 collective-permute-start
  7.1 3.4 %collective-permute-start.1 = (f32[64,256]{1,0:T(8,128)S(1)}, f32[64,256]{1,0:T(8,128)S(1)}, u32[]{:S(2)}, u32[]{:S(2)}) collective-permute-start(f32[64,256]{1,0:T(8,128)S(1)} %get-tuple-element.35), channel_id=1, source_target_pairs={{0,2},{1,3},{2,0},{3,1},{4,6},{5,7},{6,4},{7,5},{8,10},{9,11},{10,... | collective-permute-start | bytes 196616 | tf_op jit(solution)/shard_map/ppermute | solution.py:405
  10.4 0.1 collective-permute-start.2
  10.5 0.0 copy-done.10
  10.5 0.1 copy.9.bias_ref
  10.6 0.0 collective-permute-done.one_ref
  10.6 2.5 %collective-permute-done.1.two_ref = f32[64,256]{1,0:T(8,128)S(1)} collective-permute-done((f32[64,256]{1,0:T(8,128)S(1)}, f32[64,256]{1,0:T(8,128)S(1)}, u32[]{:S(2)}, u32[]{:S(2)}) %collective-permute-start.1) | collective-permute-done | bytes 65568 | tf_op jit(solution)/shard_map/ppermute | solution.py:405
  13.1 2.9 %collective-permute-done.2.three_ref = f32[64,256]{1,0:T(8,128)S(1)} collective-permute-done((f32[64,256]{1,0:T(8,128)S(1)}, f32[64,256]{1,0:T(8,128)S(1)}, u32[]{:S(2)}, u32[]{:S(2)}) %collective-permute-start.2) | collective-permute-done | bytes 65568 | tf_op jit(solution)/shard_map/ppermute | solution.py:405
  16.0 0.0 copy-done
  16.0 0.1 mix_modes.1
  16.1 7.9 %all_gather.3.mixed_ref = f32[256,256]{1,0:T(8,128)} all-gather(f32[64,256]{1,0:T(8,128)S(1)} %get-tuple-element.37), channel_id=1, replica_groups=mesh['dp'=32,'gz'=4] {'gz'}, dimensions={0}, use_global_device_ids=true | all-gather | bytes 327680 | tf_op jit(solution)/shard_map/all_gather | solution.py:434
  24.0 0.0 copy-done.6
  24.0 15.7 %slope_and_modes.1 = (bf16[1,16,24,9216]{3,2,1,0:T(8,128)(2,1)}, f32[72,256]{1,0:T(8,128)S(1)}, f32[72,256]{1,0:T(8,128)S(1)}, f32[72,256]{1,0:T(8,128)S(1)}, f32[72,256]{1,0:T(8,128)S(1)}) custom-call(s32[1]{0:T(128)} %bitcast.slab_ref, bf16[1,16,24,9216]{3,2,1,0:T(8,128)(2,1)} %field_hbm.3, bf16[1,16,24,9216]{3,2,1,0:T(8,128)(2,1)} %cot_hbm.1, ...), custom_call_target="tpu_custom_call" | custom-call | tf_op jit(solution)/shard_map/slope_and_modes/pallas_call | solution.py:436
  39.7 0.0 copy-done.1
  39.7 0.0 copy-done.2
  39.8 0.0 copy-done.3
  39.8 0.0 copy-done.4
  39.8 0.4 collective-permute-start.3
  40.2 1.3 %collective-permute-start.4 = (f32[72,256]{1,0:T(8,128)S(1)}, f32[72,256]{1,0:T(8,128)S(1)}, u32[]{:S(2)}, u32[]{:S(2)}) collective-permute-start(f32[72,256]{1,0:T(8,128)S(1)} %get-tuple-element.41), channel_id=1, source_target_pairs={{0,2},{1,3},{2,0},{3,1},{4,6},{5,7},{6,4},{7,5},{8,10},{9,11},{10,... | collective-permute-start | bytes 221192 | tf_op jit(solution)/shard_map/ppermute | solution.py:405
  41.5 1.8 %collective-permute-start.5 = (f32[72,256]{1,0:T(8,128)S(1)}, f32[72,256]{1,0:T(8,128)S(1)}, u32[]{:S(2)}, u32[]{:S(2)}) collective-permute-start(f32[72,256]{1,0:T(8,128)S(1)} %get-tuple-element.42), channel_id=1, source_target_pairs={{0,3},{1,2},{2,1},{3,0},{4,7},{5,6},{6,5},{7,4},{8,11},{9,10},{10,... | collective-permute-start | bytes 221192 | tf_op jit(solution)/shard_map/ppermute | solution.py:405
  43.3 0.0 collective-permute-done.3.one_ref
  43.3 3.0 %collective-permute-done.4.two_ref = f32[72,256]{1,0:T(8,128)S(1)} collective-permute-done((f32[72,256]{1,0:T(8,128)S(1)}, f32[72,256]{1,0:T(8,128)S(1)}, u32[]{:S(2)}, u32[]{:S(2)}) %collective-permute-start.4) | collective-permute-done | bytes 73760 | tf_op jit(solution)/shard_map/ppermute | solution.py:405
  46.4 1.2 %collective-permute-done.5.three_ref = f32[72,256]{1,0:T(8,128)S(1)} collective-permute-done((f32[72,256]{1,0:T(8,128)S(1)}, f32[72,256]{1,0:T(8,128)S(1)}, u32[]{:S(2)}, u32[]{:S(2)}) %collective-permute-start.5) | collective-permute-done | bytes 73760 | tf_op jit(solution)/shard_map/ppermute | solution.py:405
  47.5 0.8 back_modes.1
  48.3 0.0 copy-start.5
  48.3 8.3 %all-to-all-start = ((f32[32,24,128]{2,1,0:T(8,128)}), f32[32,24,128]{2,1,0:T(8,128)S(1)}, u32[]{:S(2)}, u32[]{:S(2)}) async-start(f32[32,24,128]{2,1,0:T(8,128)} %get-tuple-element.44), calls=%async_computation | async-start | bytes 786432 | tf_op jit(solution)/shard_map/all_to_all | solution.py:479
  56.7 2.1 %collective-permute-start.8 = (f32[64,256]{1,0:T(8,128)S(1)}, f32[64,256]{1,0:T(8,128)S(1)}, u32[]{:S(2)}, u32[]{:S(2)}) collective-permute-start(f32[64,256]{1,0:T(8,128)S(1)} %get-tuple-element.47.own_ref), channel_id=1, source_target_pairs={{0,3},{1,2},{2,1},{3,0},{4,7},{5,6},{6,5},{7,4},{8,11},{9,10},{10,... | collective-permute-start | bytes 196616 | tf_op jit(solution)/shard_map/ppermute | solution.py:405
  58.8 0.9 %collective-permute-start.7 = (f32[64,256]{1,0:T(8,128)S(1)}, f32[64,256]{1,0:T(8,128)S(1)}, u32[]{:S(2)}, u32[]{:S(2)}) collective-permute-start(f32[64,256]{1,0:T(8,128)S(1)} %get-tuple-element.47.own_ref), channel_id=1, source_target_pairs={{0,2},{1,3},{2,0},{3,1},{4,6},{5,7},{6,4},{7,5},{8,10},{9,11},{10,... | collective-permute-start | bytes 196616 | tf_op jit(solution)/shard_map/ppermute | solution.py:405
  59.7 0.4 collective-permute-start.6
  60.1 7.3 %all-to-all-done.got_ref = f32[32,24,128]{2,1,0:T(8,128)S(1)} async-done(((f32[32,24,128]{2,1,0:T(8,128)}), f32[32,24,128]{2,1,0:T(8,128)S(1)}, u32[]{:S(2)}, u32[]{:S(2)}) %all-to-all-start) | async-done | bytes 393248 | tf_op jit(solution)/shard_map/all_to_all | solution.py:479
  67.4 1.2 %sample_sum.1 = (f32[32,8,8,128]{3,2,1,0:T(8,128)}, f32[16,16]{1,0:T(8,128)}, f32[1,16]{1,0:T(1,128)}) custom-call(f32[32,24,128]{2,1,0:T(8,128)S(1)} %all-to-all-done.got_ref), custom_call_target="tpu_custom_call" | custom-call | tf_op jit(solution)/shard_map/sample_sum/pallas_call | solution.py:481
  68.6 0.0 collective-permute-done.8.three_ref
  68.6 0.0 copy-start.7
  68.6 0.0 collective-permute-done.7.two_ref
  68.6 0.0 copy-start.8
  68.6 0.0 collective-permute-done.6.one_ref
  68.6 0.0 copy-start.9
  68.6 5.9 %all-to-all-start.1 = ((f32[32,8,8,128]{3,2,1,0:T(8,128)}), f32[32,8,8,128]{3,2,1,0:T(8,128)S(1)}, u32[]{:S(2)}, u32[]{:S(2)}) async-start(f32[32,8,8,128]{3,2,1,0:T(8,128)} %get-tuple-element.51), calls=%async_computation.1 | async-start | bytes 2097152 | tf_op jit(solution)/shard_map/all_to_all | solution.py:490
  74.5 0.0 copy-done.5
  74.5 0.0 copy-done.7
  74.5 0.0 copy-done.8
  74.5 0.0 copy-done.9
  74.5 8.4 %field_grad.1 = bf16[1,16,24,9216]{3,2,1,0:T(8,128)(2,1)} custom-call(s32[1]{0:T(128)} %bitcast.slab_ref, bf16[1,16,24,9216]{3,2,1,0:T(8,128)(2,1)} %get-tuple-element.38.dpre_hbm, f32[96,256]{1,0:T(8,128)} %copy-done.3, f32[96,256]{1,0:T(8,128)} %copy-done.4, bf16[256,384]{1,0:T(8,128)(2,1)} %copy-done.1, bf16[256,384]{1,0:T(8,128)(2,1)} %copy-done.2, ...), custom_call_target="tpu_custom_call" | custom-call | flops 2717908992 | bytes 14155776 | tf_op jit(solution)/shard_map/field_grad/pallas_call | solution.py:492
  83.0 8.0 %all-to-all-done.1.got_ref = f32[32,8,8,128]{3,2,1,0:T(8,128)S(1)} async-done(((f32[32,8,8,128]{3,2,1,0:T(8,128)}), f32[32,8,8,128]{3,2,1,0:T(8,128)S(1)}, u32[]{:S(2)}, u32[]{:S(2)}) %all-to-all-start.1) | async-done | bytes 1048608 | tf_op jit(solution)/shard_map/all_to_all | solution.py:490
  91.0 1.0 %place_pieces.1 = f32[4,16,16,256]{3,2,1,0:T(8,128)} custom-call(f32[32,8,8,128]{3,2,1,0:T(8,128)S(1)} %all-to-all-done.1.got_ref), custom_call_target="tpu_custom_call" | custom-call | tf_op jit(solution)/shard_map/place_pieces/pallas_call | solution.py:516
Async XLA Ops:
  0.6 9.9 %copy-start.10 = (f32[16]{0:T(128)S(1)}, f32[16]{0:T(128)}, u32[]{:S(2)}) copy-start(f32[16]{0:T(128)} %param.9) | copy-start | bytes 196
  0.6 15.4 %copy-start = (f32[4,16,16,256]{3,2,1,0:T(8,128)S(1)}, f32[4,16,16,256]{3,2,1,0:T(8,128)}, u32[]{:S(2)}) copy-start(f32[4,16,16,256]{3,2,1,0:T(8,128)} %weight_ref.6) | copy-start | bytes 3145732
  0.7 23.4 %copy-start.6 = (bf16[16,16]{1,0:T(8,128)(2,1)S(1)}, bf16[16,16]{1,0:T(8,128)(2,1)}, u32[]{:S(2)}) copy-start(bf16[16,16]{1,0:T(8,128)(2,1)} %weight_ref.7) | copy-start | bytes 1540
  6.9 32.8 %copy-start.1 = (bf16[256,384]{1,0:T(8,128)(2,1)}, bf16[256,384]{1,0:T(8,128)(2,1)S(1)}, u32[]{:S(2)}) copy-start(bf16[256,384]{1,0:T(8,128)(2,1)S(1)} %get-tuple-element.31.high) | copy-start | bytes 589828
  6.9 32.8 %copy-start.2 = (bf16[256,384]{1,0:T(8,128)(2,1)}, bf16[256,384]{1,0:T(8,128)(2,1)S(1)}, u32[]{:S(2)}) copy-start(bf16[256,384]{1,0:T(8,128)(2,1)S(1)} %get-tuple-element.32.low) | copy-start | bytes 589828
  7.0 32.8 %copy-start.3 = (f32[96,256]{1,0:T(8,128)}, f32[96,256]{1,0:T(8,128)S(1)}, u32[]{:S(2)}) copy-start(f32[96,256]{1,0:T(8,128)S(1)} %get-tuple-element.29.outer) | copy-start | bytes 294916
  7.0 32.8 %copy-start.4 = (f32[96,256]{1,0:T(8,128)}, f32[96,256]{1,0:T(8,128)S(1)}, u32[]{:S(2)}) copy-start(f32[96,256]{1,0:T(8,128)S(1)} %get-tuple-element.30.inner) | copy-start | bytes 294916
  7.0 3.6 %collective-permute-start = (f32[64,256]{1,0:T(8,128)S(1)}, f32[64,256]{1,0:T(8,128)S(1)}, u32[]{:S(2)}, u32[]{:S(2)}) collective-permute-start(f32[64,256]{1,0:T(8,128)S(1)} %get-tuple-element.34), channel_id=1, source_target_pairs={{0,1},{1,0},{2,3},{3,2},{4,5},{5,4},{6,7},{7,6},{8,9},{9,8},{10,11... | collective-permute-start | bytes 196616 | tf_op jit(solution)/shard_map/ppermute | solution.py:405
  7.1 6.0 %collective-permute-start.1 = (f32[64,256]{1,0:T(8,128)S(1)}, f32[64,256]{1,0:T(8,128)S(1)}, u32[]{:S(2)}, u32[]{:S(2)}) collective-permute-start(f32[64,256]{1,0:T(8,128)S(1)} %get-tuple-element.35), channel_id=1, source_target_pairs={{0,2},{1,3},{2,0},{3,1},{4,6},{5,7},{6,4},{7,5},{8,10},{9,11},{10,... | collective-permute-start | bytes 196616 | tf_op jit(solution)/shard_map/ppermute | solution.py:405
  10.4 5.6 %collective-permute-start.2 = (f32[64,256]{1,0:T(8,128)S(1)}, f32[64,256]{1,0:T(8,128)S(1)}, u32[]{:S(2)}, u32[]{:S(2)}) collective-permute-start(f32[64,256]{1,0:T(8,128)S(1)} %get-tuple-element.36), channel_id=1, source_target_pairs={{0,3},{1,2},{2,1},{3,0},{4,7},{5,6},{6,5},{7,4},{8,11},{9,10},{10,... | collective-permute-start | bytes 196616 | tf_op jit(solution)/shard_map/ppermute | solution.py:405
  39.8 3.6 %collective-permute-start.3 = (f32[72,256]{1,0:T(8,128)S(1)}, f32[72,256]{1,0:T(8,128)S(1)}, u32[]{:S(2)}, u32[]{:S(2)}) collective-permute-start(f32[72,256]{1,0:T(8,128)S(1)} %get-tuple-element.40), channel_id=1, source_target_pairs={{0,1},{1,0},{2,3},{3,2},{4,5},{5,4},{6,7},{7,6},{8,9},{9,8},{10,11... | collective-permute-start | bytes 221192 | tf_op jit(solution)/shard_map/ppermute | solution.py:405
  40.2 6.2 %collective-permute-start.4 = (f32[72,256]{1,0:T(8,128)S(1)}, f32[72,256]{1,0:T(8,128)S(1)}, u32[]{:S(2)}, u32[]{:S(2)}) collective-permute-start(f32[72,256]{1,0:T(8,128)S(1)} %get-tuple-element.41), channel_id=1, source_target_pairs={{0,2},{1,3},{2,0},{3,1},{4,6},{5,7},{6,4},{7,5},{8,10},{9,11},{10,... | collective-permute-start | bytes 221192 | tf_op jit(solution)/shard_map/ppermute | solution.py:405
  41.5 6.0 %collective-permute-start.5 = (f32[72,256]{1,0:T(8,128)S(1)}, f32[72,256]{1,0:T(8,128)S(1)}, u32[]{:S(2)}, u32[]{:S(2)}) collective-permute-start(f32[72,256]{1,0:T(8,128)S(1)} %get-tuple-element.42), channel_id=1, source_target_pairs={{0,3},{1,2},{2,1},{3,0},{4,7},{5,6},{6,5},{7,4},{8,11},{9,10},{10,... | collective-permute-start | bytes 221192 | tf_op jit(solution)/shard_map/ppermute | solution.py:405
  48.3 26.2 %copy-start.5 = (f32[64,256]{1,0:T(8,128)}, f32[64,256]{1,0:T(8,128)S(1)}, u32[]{:S(2)}) copy-start(f32[64,256]{1,0:T(8,128)S(1)} %get-tuple-element.47.own_ref) | copy-start | bytes 196612
  48.3 19.1 %all-to-all-start = ((f32[32,24,128]{2,1,0:T(8,128)}), f32[32,24,128]{2,1,0:T(8,128)S(1)}, u32[]{:S(2)}, u32[]{:S(2)}) async-start(f32[32,24,128]{2,1,0:T(8,128)} %get-tuple-element.44), calls=%async_computation | async-start | bytes 786432 | tf_op jit(solution)/shard_map/all_to_all | solution.py:479
  56.7 11.9 %collective-permute-start.8 = (f32[64,256]{1,0:T(8,128)S(1)}, f32[64,256]{1,0:T(8,128)S(1)}, u32[]{:S(2)}, u32[]{:S(2)}) collective-permute-start(f32[64,256]{1,0:T(8,128)S(1)} %get-tuple-element.47.own_ref), channel_id=1, source_target_pairs={{0,3},{1,2},{2,1},{3,0},{4,7},{5,6},{6,5},{7,4},{8,11},{9,10},{10,... | collective-permute-start | bytes 196616 | tf_op jit(solution)/shard_map/ppermute | solution.py:405
  58.8 9.8 %collective-permute-start.7 = (f32[64,256]{1,0:T(8,128)S(1)}, f32[64,256]{1,0:T(8,128)S(1)}, u32[]{:S(2)}, u32[]{:S(2)}) collective-permute-start(f32[64,256]{1,0:T(8,128)S(1)} %get-tuple-element.47.own_ref), channel_id=1, source_target_pairs={{0,2},{1,3},{2,0},{3,1},{4,6},{5,7},{6,4},{7,5},{8,10},{9,11},{10,... | collective-permute-start | bytes 196616 | tf_op jit(solution)/shard_map/ppermute | solution.py:405
  59.7 8.9 %collective-permute-start.6 = (f32[64,256]{1,0:T(8,128)S(1)}, f32[64,256]{1,0:T(8,128)S(1)}, u32[]{:S(2)}, u32[]{:S(2)}) collective-permute-start(f32[64,256]{1,0:T(8,128)S(1)} %get-tuple-element.47.own_ref), channel_id=1, source_target_pairs={{0,1},{1,0},{2,3},{3,2},{4,5},{5,4},{6,7},{7,6},{8,9},{9,8},{10,11... | collective-permute-start | bytes 196616 | tf_op jit(solution)/shard_map/ppermute | solution.py:405
  68.6 5.9 %copy-start.7 = (f32[64,256]{1,0:T(8,128)}, f32[64,256]{1,0:T(8,128)S(1)}, u32[]{:S(2)}) copy-start(f32[64,256]{1,0:T(8,128)S(1)} %collective-permute-done.8.three_ref) | copy-start | bytes 196612
  68.6 5.9 %copy-start.8 = (f32[64,256]{1,0:T(8,128)}, f32[64,256]{1,0:T(8,128)S(1)}, u32[]{:S(2)}) copy-start(f32[64,256]{1,0:T(8,128)S(1)} %collective-permute-done.7.two_ref) | copy-start | bytes 196612
  68.6 5.9 %copy-start.9 = (f32[64,256]{1,0:T(8,128)}, f32[64,256]{1,0:T(8,128)S(1)}, u32[]{:S(2)}) copy-start(f32[64,256]{1,0:T(8,128)S(1)} %collective-permute-done.6.one_ref) | copy-start | bytes 196612
  68.6 22.4 %all-to-all-start.1 = ((f32[32,8,8,128]{3,2,1,0:T(8,128)}), f32[32,8,8,128]{3,2,1,0:T(8,128)S(1)}, u32[]{:S(2)}, u32[]{:S(2)}) async-start(f32[32,8,8,128]{3,2,1,0:T(8,128)} %get-tuple-element.51), calls=%async_computation.1 | async-start | bytes 2097152 | tf_op jit(solution)/shard_map/all_to_all | solution.py:490

commit v4 on v3

--- a/solution.py
+++ b/solution.py
@@ -107,7 +107,9 @@
 
 
 def chunk(step):
-    return slice(step * WIDTH, (step + 1) * WIDTH)
+    if isinstance(step, int):
+        return slice(step * WIDTH, (step + 1) * WIDTH)
+    return pl.ds(pl.multiple_of(step * WIDTH, LANES), WIDTH)
 
 
 def copies_in(source, target, sems):
@@ -133,7 +135,7 @@
 def kron_rows(outer, inner, step):
     table = inner[...]
     rows = [
-        (outer[step * (WIDTH // N) + k : step * (WIDTH // N) + k + 1, :] * table).astype(bf16)
+        (outer[pl.ds(step * (WIDTH // N) + k, 1), :] * table).astype(bf16)
         for k in range(WIDTH // N)
     ]
     return jnp.concatenate(rows, 0)
@@ -149,10 +151,13 @@
     high[...], low[...] = split(row_matrix(slab_ref[0]))
     acc[...] = jnp.zeros_like(acc)
 
-    for step in range(CHUNKS):
+    def body(step, carry):
         kron = kron_rows(outer, inner, step)
         fetch(step).wait()
         acc[...] += matmul(field[:, :, chunk(step)].reshape(C * ROWS, WIDTH), kron)
+        return carry
+
+    lax.fori_loop(0, CHUNKS, body, 0)
     send_parts(slab_ref[0], high, low, acc[...], scale_fwd, parts)
 
 
@@ -230,16 +235,8 @@
             )
         acc[...] += matmul(out[:, :, cols].reshape(C * ROWS, WIDTH), kron[...])
     send_parts(slab_ref[0], high, low, acc[...], scale_inv, parts)
-    hot = one_hot_rows(jnp.float32)
-    half = jnp.dot(
-        jnp.where(same_sub(), point_acc[...], 0.0),
-        hot,
-        precision=HIGHEST,
-        preferred_element_type=jnp.float32,
-    )
-    point = lax.dot_general(hot, half, TN, precision=HIGHEST, preferred_element_type=jnp.float32)
     sums = acc[:, 0:LANES].reshape(C, ROWS, LANES).sum(1)[:, 0:1]
-    packed = pack_small(point, sums)
+    packed = pack_small(point_acc[...], sums)
     for k in range(GZ):
         parts[k][OWNED : OWNED + SUB, 0:LANES] = packed
         parts[k][OWNED : OWNED + SUB, LANES:MODES] = jnp.zeros_like(packed)
@@ -251,15 +248,18 @@
     return iota((C, LANES), 0), iota((C, LANES), 1)
 
 
-def pack_small(point, sums):
+def pack_small(blocks, sums):
+    fold = jnp.where((iota((C * SUB, LANES), 0) >> 3) == (iota((C * SUB, LANES), 1) & 15), 1.0, 0.0)
+    fold = fold.astype(bf16)
+    high, low = split(jnp.where(same_sub(), blocks, 0.0))
+    wide = matmul(high, fold) + matmul(low, fold)
+    channel = (iota((C * SUB, LANES), 0) >> 3) & 7
+    wide = jnp.where(channel == (iota((C * SUB, LANES), 1) >> 4), wide, 0.0)
+    first = wide[0 : 8 * SUB].sum(0, keepdims=True)
+    second = wide[8 * SUB :].sum(0, keepdims=True)
     row, lane = lane_masks()
-    tile = jnp.where((lane & 15) == row, 1.0, 0.0)
-    wide = jnp.dot(point, tile, precision=HIGHEST, preferred_element_type=jnp.float32)
-    wide = jnp.where((row & 7) == (lane >> 4), wide, 0.0)
     vector = jnp.where(row == lane, sums, 0.0).sum(0, keepdims=True)
-    low = wide[0:8].sum(0, keepdims=True)
-    high = wide[8:16].sum(0, keepdims=True)
-    return jnp.concatenate([low, high, vector, jnp.zeros((5, LANES), jnp.float32)], 0)
+    return jnp.concatenate([first, second, vector, jnp.zeros((5, LANES), jnp.float32)], 0)
 
 
 def unpack_small(packed):
@@ -271,14 +271,12 @@
     return point, packed[2:3, 0:C]
 
 
-def gathered_sum(refs):
-    own, one, two, three = (ref[...] for ref in refs)
-    return (own + one) + (two + three)
-
-
-def mix_kernel(own_ref, one_ref, two_ref, three_ref, weight_ref, coef_ref, mixed_ref):
-    coef = gathered_sum((own_ref, one_ref, two_ref, three_ref))
-    coef_ref[...] = coef
+def add_kernel(a_ref, b_ref, out_ref):
+    out_ref[...] = a_ref[...] + b_ref[...]
+
+
+def mix_kernel(own_ref, one_ref, two_ref, weight_ref, coef_ref, mixed_ref):
+    coef_ref[...] = (own_ref[...] + one_ref[...]) + two_ref[...]
     for a in range(M // GZ):
         total = jnp.zeros((C, MODES), jnp.float32)
         for i in range(C):
@@ -291,8 +289,8 @@
         yield owner, owner // 8, owner // 4 % 2 * SUB, owner // 2 % 2 * SUB, owner % 2 * LANES
 
 
-def back_kernel(own_ref, one_ref, two_ref, three_ref, weight_ref, coef_ref, back_ref, send_ref):
-    full = gathered_sum((own_ref, one_ref, two_ref, three_ref))
+def back_kernel(own_ref, one_ref, two_ref, weight_ref, coef_ref, back_ref, send_ref):
+    full = (own_ref[...] + one_ref[...]) + two_ref[...]
     small = full[OWNED : OWNED + SUB, 0:LANES]
     for owner, a, i, o, p in pieces():
         send_ref[owner, 0:SUB, :] = coef_ref[a * C + i : a * C + i + SUB, p : p + LANES]
@@ -399,11 +397,19 @@
     dp = lax.axis_size("dp")
     slab = lax.axis_index("gz").astype(jnp.int32).reshape(1)
 
-    def exchange(parts):
-        got = [parts[0]]
-        for k in range(1, GZ):
-            got.append(lax.ppermute(parts[k], "gz", [(g, g ^ k) for g in range(GZ)]))
-        return got
+    def flip(values, k):
+        return lax.ppermute(values, "gz", [(g, g ^ k) for g in range(GZ)])
+
+    def reduce_parts(parts):
+        three = flip(parts[3], 1)
+        one = flip(parts[1], 1)
+        forward = pl.pallas_call(
+            add_kernel,
+            out_shape=jax.ShapeDtypeStruct(three.shape, three.dtype),
+            compiler_params=limit(8),
+            name="add_pair",
+        )(parts[2], three)
+        return parts[0], one, flip(forward, 2)
 
     *coef_parts, outer, inner, high, low = pl.pallas_call(
         field_modes_kernel,
@@ -430,7 +436,7 @@
         out_shape=(shaped(OWNED, MODES), shaped(OWNED, MODES)),
         compiler_params=limit(8),
         name="mix_modes",
-    )(*exchange(coef_parts), spec_weight)
+    )(*reduce_parts(coef_parts), spec_weight)
     mixed_all = lax.all_gather(mixed, "gz", axis=0, tiled=True)
 
     dpre, *grad_parts = pl.pallas_call(
@@ -474,10 +480,11 @@
         out_shape=(shaped(OWNED, MODES), shaped(dp, 3 * SUB, LANES)),
         compiler_params=limit(8),
         name="back_modes",
-    )(*exchange(grad_parts), spec_weight, coef)
+    )(*reduce_parts(grad_parts), spec_weight, coef)
 
     got = lax.all_to_all(send, "dp", 0, 0, tiled=True)
-    back_parts = exchange([back] * GZ)
+    two = flip(back, 2)
+    back_parts = (back, flip(back, 1), two, flip(two, 1))
     copies, point_grad, bias_grad = pl.pallas_call(
         functools.partial(
             outer_kernel, 1.0 / math.sqrt(dp * N), 1.0 / math.sqrt(dp * N * N * N)

time: 92.4 us -> 90.7 us (0.982)
  waiting for transfers between devices: 24.9 us -> 22.7 us
  starting transfers between devices: 24.7 us -> 25.9 us
    all_to_all x1, waiting for transfers between devices: 7.27 us -> 2.48 us  [shards(): got = lax.all_to_all(send, 'dp', 0, 0, tiled=True)]
    ppermute x9, waiting for transfers between devices: 9.62 us -> 11.5 us  [flip(): return lax.ppermute(values, 'gz', [(g, g ^ k) for g in range(GZ)])]
    pallas_call x1, Pallas kernels: 6.26 us -> 5.3 us  [shards(): pl.pallas_call(field_modes_kernel, out_shape=tuple((shaped(OWNED, MODES)...]
  transfers between devices with their start and end apart: 11 -> 11, of which waited for: 6 -> 7; matrix products, arithmetic and copies ran while one was open for 0% -> 0% of each run, Pallas kernels for 10% -> 11%
where the time goes in v4:
time: 90.7 us; the launch traced here: 90.4 us
  Pallas kernels  32.6 us (36%)
  starting transfers between devices  25.9 us (29%)
  waiting for transfers between devices  22.7 us (25%)
  blocking collectives  8.16 us (9%)
    pallas_call x1, Pallas kernels, shards(): pl.pallas_call(functools.partial(slope_kernel, 768), out_shape=(jax.Shape...  15.8 us
    ppermute x9, waiting for transfers between devices, flip(): return lax.ppermute(values, 'gz', [(g, g ^ k) for g in range(GZ)])  11.5 us
    ppermute x9, starting transfers between devices, flip(): return lax.ppermute(values, 'gz', [(g, g ^ k) for g in range(GZ)])  10.9 us
    all_to_all x1, starting transfers between devices, shards(): got = lax.all_to_all(send, 'dp', 0, 0, tiled=True)  9.02 us
    all_to_all x1, waiting for transfers between devices, shards(): owned = lax.all_to_all(copies, 'dp', 0, 0, tiled=True)  8.67 us
    pallas_call x1, Pallas kernels, shards(): pl.pallas_call(functools.partial(field_grad_kernel, 768), out_shape=jax.S...  8.43 us
    all_gather x1, blocking collectives, shards(): mixed_all = lax.all_gather(mixed, 'gz', axis=0, tiled=True)  8.16 us
    all_to_all x1, starting transfers between devices, shards(): owned = lax.all_to_all(copies, 'dp', 0, 0, tiled=True)  6.07 us
  transfers between devices with their start and end apart: 11, of which 7 were waited for; matrix products, arithmetic and copies ran while one was open for 0% of the time, Pallas kernels for 11%

profile of v4, /device:TPU:0, one launch (start us, length us, event | category | flops | bytes accessed | tf_op | source)
XLA Modules:
  0.0 90.4 jit_solution(1935083158047674366)
XLA Ops:
  0.6 0.0 copy-start.10
  0.6 0.0 copy-start
  0.7 0.0 copy-start.6
  0.7 5.3 %field_modes.1 = (f32[64,256]{1,0:T(8,128)S(1)}, f32[64,256]{1,0:T(8,128)S(1)}, f32[64,256]{1,0:T(8,128)S(1)}, f32[64,256]{1,0:T(8,128)S(1)}, f32[96,256]{1,0:T(...) custom-call(s32[1]{0:T(128)} %bitcast.slab_ref, ...), custom_call_target="tpu_custom_call" | custom-call | tf_op jit(solution)/shard_map/field_modes/pallas_call | solution.py:414
  6.0 0.0 copy-start.1
  6.0 0.0 copy-start.2
  6.0 0.0 copy-start.3
  6.0 0.0 copy-start.4
  6.0 0.1 collective-permute-start.1
  6.1 0.5 collective-permute-start
  6.6 0.7 collective-permute-done.1.b_ref
  7.4 3.4 %collective-permute-start.2 = (f32[64,256]{1,0:T(8,128)S(1)}, f32[64,256]{1,0:T(8,128)S(1)}, u32[]{:S(2)}, u32[]{:S(2)}) collective-permute-start(f32[64,256]{1,0:T(8,128)S(1)} %add_pair.2), channel_id=1, source_target_pairs={{0,2},{1,3},{2,0},{3,1},{4,6},{5,7},{6,4},{7,5},{8,10},{9,11},{10,... | collective-permute-start | bytes 196616 | tf_op jit(solution)/shard_map/ppermute | solution.py:401
  10.7 0.0 copy-done.10
  10.7 0.1 copy.9.bias_ref
  10.8 0.0 collective-permute-done.one_ref
  10.8 2.4 %collective-permute-done.2.two_ref = f32[64,256]{1,0:T(8,128)S(1)} collective-permute-done((f32[64,256]{1,0:T(8,128)S(1)}, f32[64,256]{1,0:T(8,128)S(1)}, u32[]{:S(2)}, u32[]{:S(2)}) %collective-permute-start.2) | collective-permute-done | bytes 65568 | tf_op jit(solution)/shard_map/ppermute | solution.py:401
  13.2 0.0 copy-done
  13.2 0.1 mix_modes.1
  13.3 8.2 %all_gather.3.mixed_ref = f32[256,256]{1,0:T(8,128)} all-gather(f32[64,256]{1,0:T(8,128)S(1)} %get-tuple-element.37), channel_id=1, replica_groups=mesh['dp'=32,'gz'=4] {'gz'}, dimensions={0}, use_global_device_ids=true | all-gather | bytes 327680 | tf_op jit(solution)/shard_map/all_gather | solution.py:440
  21.5 0.0 copy-done.6
  21.5 15.8 %slope_and_modes.1 = (bf16[1,16,24,9216]{3,2,1,0:T(8,128)(2,1)}, f32[72,256]{1,0:T(8,128)S(1)}, f32[72,256]{1,0:T(8,128)S(1)}, f32[72,256]{1,0:T(8,128)S(1)}, f32[72,256]{1,0:T(8,128)S(1)}) custom-call(s32[1]{0:T(128)} %bitcast.slab_ref, bf16[1,16,24,9216]{3,2,1,0:T(8,128)(2,1)} %field_hbm.3, bf16[1,16,24,9216]{3,2,1,0:T(8,128)(2,1)} %cot_hbm.1, ...), custom_call_target="tpu_custom_call" | custom-call | tf_op jit(solution)/shard_map/slope_and_modes/pallas_call | solution.py:442
  37.3 0.0 copy-done.1
  37.3 0.0 copy-done.2
  37.3 0.0 copy-done.3
  37.3 0.0 copy-done.4
  37.3 0.4 collective-permute-start.4
  37.7 0.2 collective-permute-start.3
  37.9 0.8 collective-permute-done.4.b_ref
  38.7 3.3 %collective-permute-start.5 = (f32[72,256]{1,0:T(8,128)S(1)}, f32[72,256]{1,0:T(8,128)S(1)}, u32[]{:S(2)}, u32[]{:S(2)}) collective-permute-start(f32[72,256]{1,0:T(8,128)S(1)} %add_pair.3), channel_id=1, source_target_pairs={{0,2},{1,3},{2,0},{3,1},{4,6},{5,7},{6,4},{7,5},{8,10},{9,11},{10,... | collective-permute-start | bytes 221192 | tf_op jit(solution)/shard_map/ppermute | solution.py:401
  42.0 0.0 collective-permute-done.3.one_ref
  42.0 3.0 %collective-permute-done.5.two_ref = f32[72,256]{1,0:T(8,128)S(1)} collective-permute-done((f32[72,256]{1,0:T(8,128)S(1)}, f32[72,256]{1,0:T(8,128)S(1)}, u32[]{:S(2)}, u32[]{:S(2)}) %collective-permute-start.5) | collective-permute-done | bytes 73760 | tf_op jit(solution)/shard_map/ppermute | solution.py:401
  45.0 0.8 back_modes.1
  45.8 0.0 copy-start.5
  45.8 9.0 %all-to-all-start = ((f32[32,24,128]{2,1,0:T(8,128)}), f32[32,24,128]{2,1,0:T(8,128)S(1)}, u32[]{:S(2)}, u32[]{:S(2)}) async-start(f32[32,24,128]{2,1,0:T(8,128)} %get-tuple-element.44), calls=%async_computation | async-start | bytes 786432 | tf_op jit(solution)/shard_map/all_to_all | solution.py:485
  54.8 3.0 %collective-permute-start.7 = (f32[64,256]{1,0:T(8,128)S(1)}, f32[64,256]{1,0:T(8,128)S(1)}, u32[]{:S(2)}, u32[]{:S(2)}) collective-permute-start(f32[64,256]{1,0:T(8,128)S(1)} %get-tuple-element.47.own_ref), channel_id=1, source_target_pairs={{0,2},{1,3},{2,0},{3,1},{4,6},{5,7},{6,4},{7,5},{8,10},{9,11},{10,... | collective-permute-start | bytes 196616 | tf_op jit(solution)/shard_map/ppermute | solution.py:401
  57.8 0.0 collective-permute-start.6
  57.8 4.6 %collective-permute-done.7.two_ref = f32[64,256]{1,0:T(8,128)S(1)} collective-permute-done((f32[64,256]{1,0:T(8,128)S(1)}, f32[64,256]{1,0:T(8,128)S(1)}, u32[]{:S(2)}, u32[]{:S(2)}) %collective-permute-start.7) | collective-permute-done | bytes 65568 | tf_op jit(solution)/shard_map/ppermute | solution.py:401
  62.4 0.0 copy-start.7
  62.4 0.0 collective-permute-start.8
  62.4 2.5 %all-to-all-done.got_ref = f32[32,24,128]{2,1,0:T(8,128)S(1)} async-done(((f32[32,24,128]{2,1,0:T(8,128)}), f32[32,24,128]{2,1,0:T(8,128)S(1)}, u32[]{:S(2)}, u32[]{:S(2)}) %all-to-all-start) | async-done | bytes 393248 | tf_op jit(solution)/shard_map/all_to_all | solution.py:485
  64.9 1.2 %sample_sum.1 = (f32[32,8,8,128]{3,2,1,0:T(8,128)}, f32[16,16]{1,0:T(8,128)}, f32[1,16]{1,0:T(1,128)}) custom-call(f32[32,24,128]{2,1,0:T(8,128)S(1)} %all-to-all-done.got_ref), custom_call_target="tpu_custom_call" | custom-call | tf_op jit(solution)/shard_map/sample_sum/pallas_call | solution.py:488
  66.1 0.0 collective-permute-done.6.one_ref
  66.1 0.0 copy-start.8
  66.1 0.0 collective-permute-done.8.three_ref
  66.1 0.0 copy-start.9
  66.1 6.1 %all-to-all-start.1 = ((f32[32,8,8,128]{3,2,1,0:T(8,128)}), f32[32,8,8,128]{3,2,1,0:T(8,128)S(1)}, u32[]{:S(2)}, u32[]{:S(2)}) async-start(f32[32,8,8,128]{3,2,1,0:T(8,128)} %get-tuple-element.51), calls=%async_computation.1 | async-start | bytes 2097152 | tf_op jit(solution)/shard_map/all_to_all | solution.py:497
  72.2 0.0 copy-done.5
  72.2 0.0 copy-done.7
  72.2 0.0 copy-done.8
  72.2 0.0 copy-done.9
  72.2 8.4 %field_grad.1 = bf16[1,16,24,9216]{3,2,1,0:T(8,128)(2,1)} custom-call(s32[1]{0:T(128)} %bitcast.slab_ref, bf16[1,16,24,9216]{3,2,1,0:T(8,128)(2,1)} %get-tuple-element.38.dpre_hbm, f32[96,256]{1,0:T(8,128)} %copy-done.3, f32[96,256]{1,0:T(8,128)} %copy-done.4, bf16[256,384]{1,0:T(8,128)(2,1)} %copy-done.1, bf16[256,384]{1,0:T(8,128)(2,1)} %copy-done.2, ...), custom_call_target="tpu_custom_call" | custom-call | flops 2717908992 | bytes 14155776 | tf_op jit(solution)/shard_map/field_grad/pallas_call | solution.py:499
  80.7 8.7 %all-to-all-done.1.got_ref = f32[32,8,8,128]{3,2,1,0:T(8,128)S(1)} async-done(((f32[32,8,8,128]{3,2,1,0:T(8,128)}), f32[32,8,8,128]{3,2,1,0:T(8,128)S(1)}, u32[]{:S(2)}, u32[]{:S(2)}) %all-to-all-start.1) | async-done | bytes 1048608 | tf_op jit(solution)/shard_map/all_to_all | solution.py:497
  89.3 1.0 %place_pieces.1 = f32[4,16,16,256]{3,2,1,0:T(8,128)} custom-call(f32[32,8,8,128]{3,2,1,0:T(8,128)S(1)} %all-to-all-done.1.got_ref), custom_call_target="tpu_custom_call" | custom-call | tf_op jit(solution)/shard_map/place_pieces/pallas_call | solution.py:523
  (2 shorter events, 0.0 us)
Async XLA Ops:
  0.6 10.1 %copy-start.10 = (f32[16]{0:T(128)S(1)}, f32[16]{0:T(128)}, u32[]{:S(2)}) copy-start(f32[16]{0:T(128)} %param.9) | copy-start | bytes 196
  0.6 12.6 %copy-start = (f32[4,16,16,256]{3,2,1,0:T(8,128)S(1)}, f32[4,16,16,256]{3,2,1,0:T(8,128)}, u32[]{:S(2)}) copy-start(f32[4,16,16,256]{3,2,1,0:T(8,128)} %weight_ref.6) | copy-start | bytes 3145732
  0.7 20.8 %copy-start.6 = (bf16[16,16]{1,0:T(8,128)(2,1)S(1)}, bf16[16,16]{1,0:T(8,128)(2,1)}, u32[]{:S(2)}) copy-start(bf16[16,16]{1,0:T(8,128)(2,1)} %weight_ref.7) | copy-start | bytes 1540
  6.0 31.3 %copy-start.1 = (bf16[256,384]{1,0:T(8,128)(2,1)}, bf16[256,384]{1,0:T(8,128)(2,1)S(1)}, u32[]{:S(2)}) copy-start(bf16[256,384]{1,0:T(8,128)(2,1)S(1)} %get-tuple-element.31.high) | copy-start | bytes 589828
  6.0 31.3 %copy-start.2 = (bf16[256,384]{1,0:T(8,128)(2,1)}, bf16[256,384]{1,0:T(8,128)(2,1)S(1)}, u32[]{:S(2)}) copy-start(bf16[256,384]{1,0:T(8,128)(2,1)S(1)} %get-tuple-element.32.low) | copy-start | bytes 589828
  6.0 31.3 %copy-start.3 = (f32[96,256]{1,0:T(8,128)}, f32[96,256]{1,0:T(8,128)S(1)}, u32[]{:S(2)}) copy-start(f32[96,256]{1,0:T(8,128)S(1)} %get-tuple-element.29.outer) | copy-start | bytes 294916
  6.0 31.3 %copy-start.4 = (f32[96,256]{1,0:T(8,128)}, f32[96,256]{1,0:T(8,128)S(1)}, u32[]{:S(2)}) copy-start(f32[96,256]{1,0:T(8,128)S(1)} %get-tuple-element.30.inner) | copy-start | bytes 294916
  6.0 1.3 %collective-permute-start.1 = (f32[64,256]{1,0:T(8,128)S(1)}, f32[64,256]{1,0:T(8,128)S(1)}, u32[]{:S(2)}, u32[]{:S(2)}) collective-permute-start(f32[64,256]{1,0:T(8,128)S(1)} %get-tuple-element.36), channel_id=1, source_target_pairs={{0,1},{1,0},{2,3},{3,2},{4,5},{5,4},{6,7},{7,6},{8,9},{9,8},{10,11... | collective-permute-start | bytes 196616 | tf_op jit(solution)/shard_map/ppermute | solution.py:401
  6.1 4.7 %collective-permute-start = (f32[64,256]{1,0:T(8,128)S(1)}, f32[64,256]{1,0:T(8,128)S(1)}, u32[]{:S(2)}, u32[]{:S(2)}) collective-permute-start(f32[64,256]{1,0:T(8,128)S(1)} %get-tuple-element.34), channel_id=1, source_target_pairs={{0,1},{1,0},{2,3},{3,2},{4,5},{5,4},{6,7},{7,6},{8,9},{9,8},{10,11... | collective-permute-start | bytes 196616 | tf_op jit(solution)/shard_map/ppermute | solution.py:401
  7.4 5.8 %collective-permute-start.2 = (f32[64,256]{1,0:T(8,128)S(1)}, f32[64,256]{1,0:T(8,128)S(1)}, u32[]{:S(2)}, u32[]{:S(2)}) collective-permute-start(f32[64,256]{1,0:T(8,128)S(1)} %add_pair.2), channel_id=1, source_target_pairs={{0,2},{1,3},{2,0},{3,1},{4,6},{5,7},{6,4},{7,5},{8,10},{9,11},{10,... | collective-permute-start | bytes 196616 | tf_op jit(solution)/shard_map/ppermute | solution.py:401
  37.3 1.3 %collective-permute-start.4 = (f32[72,256]{1,0:T(8,128)S(1)}, f32[72,256]{1,0:T(8,128)S(1)}, u32[]{:S(2)}, u32[]{:S(2)}) collective-permute-start(f32[72,256]{1,0:T(8,128)S(1)} %get-tuple-element.42), channel_id=1, source_target_pairs={{0,1},{1,0},{2,3},{3,2},{4,5},{5,4},{6,7},{7,6},{8,9},{9,8},{10,11... | collective-permute-start | bytes 221192 | tf_op jit(solution)/shard_map/ppermute | solution.py:401
  37.7 4.3 %collective-permute-start.3 = (f32[72,256]{1,0:T(8,128)S(1)}, f32[72,256]{1,0:T(8,128)S(1)}, u32[]{:S(2)}, u32[]{:S(2)}) collective-permute-start(f32[72,256]{1,0:T(8,128)S(1)} %get-tuple-element.40), channel_id=1, source_target_pairs={{0,1},{1,0},{2,3},{3,2},{4,5},{5,4},{6,7},{7,6},{8,9},{9,8},{10,11... | collective-permute-start | bytes 221192 | tf_op jit(solution)/shard_map/ppermute | solution.py:401
  38.7 6.3 %collective-permute-start.5 = (f32[72,256]{1,0:T(8,128)S(1)}, f32[72,256]{1,0:T(8,128)S(1)}, u32[]{:S(2)}, u32[]{:S(2)}) collective-permute-start(f32[72,256]{1,0:T(8,128)S(1)} %add_pair.3), channel_id=1, source_target_pairs={{0,2},{1,3},{2,0},{3,1},{4,6},{5,7},{6,4},{7,5},{8,10},{9,11},{10,... | collective-permute-start | bytes 221192 | tf_op jit(solution)/shard_map/ppermute | solution.py:401
  45.8 26.4 %copy-start.5 = (f32[64,256]{1,0:T(8,128)}, f32[64,256]{1,0:T(8,128)S(1)}, u32[]{:S(2)}) copy-start(f32[64,256]{1,0:T(8,128)S(1)} %get-tuple-element.47.own_ref) | copy-start | bytes 196612
  45.8 19.1 %all-to-all-start = ((f32[32,24,128]{2,1,0:T(8,128)}), f32[32,24,128]{2,1,0:T(8,128)S(1)}, u32[]{:S(2)}, u32[]{:S(2)}) async-start(f32[32,24,128]{2,1,0:T(8,128)} %get-tuple-element.44), calls=%async_computation | async-start | bytes 786432 | tf_op jit(solution)/shard_map/all_to_all | solution.py:485
  54.8 7.6 %collective-permute-start.7 = (f32[64,256]{1,0:T(8,128)S(1)}, f32[64,256]{1,0:T(8,128)S(1)}, u32[]{:S(2)}, u32[]{:S(2)}) collective-permute-start(f32[64,256]{1,0:T(8,128)S(1)} %get-tuple-element.47.own_ref), channel_id=1, source_target_pairs={{0,2},{1,3},{2,0},{3,1},{4,6},{5,7},{6,4},{7,5},{8,10},{9,11},{10,... | collective-permute-start | bytes 196616 | tf_op jit(solution)/shard_map/ppermute | solution.py:401
  57.8 8.3 %collective-permute-start.6 = (f32[64,256]{1,0:T(8,128)S(1)}, f32[64,256]{1,0:T(8,128)S(1)}, u32[]{:S(2)}, u32[]{:S(2)}) collective-permute-start(f32[64,256]{1,0:T(8,128)S(1)} %get-tuple-element.47.own_ref), channel_id=1, source_target_pairs={{0,1},{1,0},{2,3},{3,2},{4,5},{5,4},{6,7},{7,6},{8,9},{9,8},{10,11... | collective-permute-start | bytes 196616 | tf_op jit(solution)/shard_map/ppermute | solution.py:401
  62.4 9.8 %copy-start.7 = (f32[64,256]{1,0:T(8,128)}, f32[64,256]{1,0:T(8,128)S(1)}, u32[]{:S(2)}) copy-start(f32[64,256]{1,0:T(8,128)S(1)} %collective-permute-done.7.two_ref) | copy-start | bytes 196612
  62.4 3.7 %collective-permute-start.8 = (f32[64,256]{1,0:T(8,128)S(1)}, f32[64,256]{1,0:T(8,128)S(1)}, u32[]{:S(2)}, u32[]{:S(2)}) collective-permute-start(f32[64,256]{1,0:T(8,128)S(1)} %collective-permute-done.7.two_ref), channel_id=1, source_target_pairs={{0,1},{1,0},{2,3},{3,2},{4,5},{5,4},{6,7},{7,6},{8,9},{9,8},{10,11... | collective-permute-start | bytes 196616 | tf_op jit(solution)/shard_map/ppermute | solution.py:401
  66.1 6.1 %copy-start.8 = (f32[64,256]{1,0:T(8,128)}, f32[64,256]{1,0:T(8,128)S(1)}, u32[]{:S(2)}) copy-start(f32[64,256]{1,0:T(8,128)S(1)} %collective-permute-done.6.one_ref) | copy-start | bytes 196612
  66.1 6.1 %copy-start.9 = (f32[64,256]{1,0:T(8,128)}, f32[64,256]{1,0:T(8,128)S(1)}, u32[]{:S(2)}) copy-start(f32[64,256]{1,0:T(8,128)S(1)} %collective-permute-done.8.three_ref) | copy-start | bytes 196612
  66.1 23.2 %all-to-all-start.1 = ((f32[32,8,8,128]{3,2,1,0:T(8,128)}), f32[32,8,8,128]{3,2,1,0:T(8,128)S(1)}, u32[]{:S(2)}, u32[]{:S(2)}) async-start(f32[32,8,8,128]{3,2,1,0:T(8,128)} %get-tuple-element.51), calls=%async_computation.1 | async-start | bytes 2097152 | tf_op jit(solution)/shard_map/all_to_all | solution.py:497

commit v5 on v4

--- a/solution.py
+++ b/solution.py
@@ -98,12 +98,11 @@
     return jnp.where(same_sub(), matmul(tall, hot, NT), 0.0).astype(bf16)
 
 
-def send_parts(slab, high_ref, low_ref, acc, scale, refs):
-    pair = split(acc)
+def send_parts(slab, high_ref, low_ref, acc, scale, joined, refs):
+    joined[...] = scale * product((high_ref[...], low_ref[...]), split(acc), NN)
     for k in range(GZ):
         first = pl.multiple_of((slab ^ k) * OWNED, OWNED)
-        rows = (high_ref[pl.ds(first, OWNED), :], low_ref[pl.ds(first, OWNED), :])
-        refs[k][0:OWNED, :] = scale * product(rows, pair, NN)
+        refs[k][0:OWNED, :] = joined[pl.ds(first, OWNED), :]
 
 
 def chunk(step):
@@ -143,7 +142,7 @@
 
 def field_modes_kernel(slab_ref, field_hbm, *rest):
     parts = rest[:GZ]
-    outer, inner, high, low, field, acc, sems = rest[GZ:]
+    outer, inner, high, low, field, acc, joined, sems = rest[GZ:]
     fetch = copies_in(field_hbm, field, sems)
     for step in range(CHUNKS):
         fetch(step).start()
@@ -158,7 +157,12 @@
         return carry
 
     lax.fori_loop(0, CHUNKS, body, 0)
-    send_parts(slab_ref[0], high, low, acc[...], scale_fwd, parts)
+    send_parts(slab_ref[0], high, low, acc[...], scale_fwd, joined, parts)
+
+
+def join_parts(slab, refs, joined):
+    for k, ref in enumerate(refs):
+        joined[pl.ds(pl.multiple_of((slab ^ k) * OWNED, OWNED), OWNED), :] = ref[...]
 
 
 def slope_kernel(
@@ -172,12 +176,15 @@
     low,
     weight_ref,
     bias_ref,
-    mixed_ref,
+    own_ref,
+    one_ref,
+    two_ref,
+    three_ref,
     dpre_hbm,
     *rest,
 ):
     parts = rest[:GZ]
-    down, bias_cols, field, cot, out, lines, acc, point_acc, kron, kron_t, *sems = rest[GZ:]
+    mixed, down, bias_cols, field, cot, out, lines, acc, point_acc, kron, kron_t, *sems = rest[GZ:]
     field_sems, cot_sems, out_sems = sems
     fetch_field = copies_in(field_hbm, field, field_sems)
     fetch_cot = copies_in(cot_hbm, cot, cot_sems)
@@ -201,7 +208,8 @@
         jnp.where(lane == 1, bias_low.astype(jnp.float32), 0.0),
     ).astype(bf16)
     ones = jnp.ones((C, sub_width), bf16)
-    full = product((high[...], low[...]), split(mixed_ref[...]), TN)
+    join_parts(slab_ref[0], (own_ref, one_ref, two_ref, three_ref), mixed)
+    full = product((high[...], low[...]), split(mixed[...]), TN)
     lines[...] = (scale_inv * full).reshape(C, ROWS, MODES).astype(bf16)
     acc[...] = jnp.zeros_like(acc)
     point_acc[...] = jnp.zeros_like(point_acc)
@@ -234,7 +242,7 @@
                 NT,
             )
         acc[...] += matmul(out[:, :, cols].reshape(C * ROWS, WIDTH), kron[...])
-    send_parts(slab_ref[0], high, low, acc[...], scale_inv, parts)
+    send_parts(slab_ref[0], high, low, acc[...], scale_inv, mixed, parts)
     sums = acc[:, 0:LANES].reshape(C, ROWS, LANES).sum(1)[:, 0:1]
     packed = pack_small(point_acc[...], sums)
     for k in range(GZ):
@@ -358,8 +366,7 @@
     for step in range(CHUNKS):
         fetch(step).start()
     up[...] = spread(weight_ref[...])
-    for k, ref in enumerate((own_ref, one_ref, two_ref, three_ref)):
-        back[pl.ds(pl.multiple_of((slab_ref[0] ^ k) * OWNED, OWNED), OWNED), :] = ref[...]
+    join_parts(slab_ref[0], (own_ref, one_ref, two_ref, three_ref), back)
     full = product((high[...], low[...]), split(back[...]), TN)
     lines[...] = (scale_fwd * full).reshape(C, ROWS, MODES).astype(bf16)
 
@@ -425,6 +432,7 @@
         scratch_shapes=[
             pltpu.VMEM((C, ROWS, CELLS), bf16),
             pltpu.VMEM((C * ROWS, MODES), jnp.float32),
+            pltpu.VMEM((M * C, MODES), jnp.float32),
             pltpu.SemaphoreType.DMA((CHUNKS,)),
         ],
         compiler_params=limit(53),
@@ -437,15 +445,17 @@
         compiler_params=limit(8),
         name="mix_modes",
     )(*reduce_parts(coef_parts), spec_weight)
-    mixed_all = lax.all_gather(mixed, "gz", axis=0, tiled=True)
+    mixed_two = flip(mixed, 2)
+    mixed_parts = (mixed, flip(mixed, 1), mixed_two, flip(mixed_two, 1))
 
     dpre, *grad_parts = pl.pallas_call(
         functools.partial(slope_kernel, 768),
         out_shape=(jax.ShapeDtypeStruct(field.shape, bf16),)
         + tuple(shaped(OWNED + SUB, MODES) for _ in range(GZ)),
-        in_specs=[SM, ANY, ANY] + [VM] * 7,
+        in_specs=[SM, ANY, ANY] + [VM] * 10,
         out_specs=(ANY,) + (VM,) * GZ,
         scratch_shapes=[
+            pltpu.VMEM((M * C, MODES), jnp.float32),
             pltpu.VMEM((C * SUB, C * SUB), bf16),
             pltpu.VMEM((C * SUB, C), bf16),
             pltpu.VMEM((C, ROWS, CELLS), bf16),
@@ -472,7 +482,7 @@
         low,
         point_weight,
         bias.reshape(C, 1),
-        mixed_all,
+        *mixed_parts,
     )
 
     back, send = pl.pallas_call(
@@ -483,8 +493,6 @@
     )(*reduce_parts(grad_parts), spec_weight, coef)
 
     got = lax.all_to_all(send, "dp", 0, 0, tiled=True)
-    two = flip(back, 2)
-    back_parts = (back, flip(back, 1), two, flip(two, 1))
     copies, point_grad, bias_grad = pl.pallas_call(
         functools.partial(
             outer_kernel, 1.0 / math.sqrt(dp * N), 1.0 / math.sqrt(dp * N * N * N)
@@ -493,8 +501,10 @@
         compiler_params=limit(8),
         name="sample_sum",
     )(got)
-    copies, *back_parts = lax.optimization_barrier((copies, *back_parts))
     owned = lax.all_to_all(copies, "dp", 0, 0, tiled=True)
+    bias_grad, back = lax.optimization_barrier((bias_grad, back))
+    two = flip(back, 2)
+    back_parts = (back, flip(back, 1), two, flip(two, 1))
 
     field_grad = pl.pallas_call(
         functools.partial(field_grad_kernel, 768),

time: 90.7 us -> 94.4 us (1.041); the launches traced: 90.4 us -> 92.9 us
  blocking collectives: 8.16 us -> 18.8 us
  starting transfers between devices: 25.9 us -> 18.3 us
  Pallas kernels: 32.6 us -> 31 us
  local copies, waits for them, and re-layouts: 0.13 us -> 1.4 us
    all_to_all x0 -> x1, blocking collectives: none -> 18.8 us  [shards(): got = lax.all_to_all(send, 'dp', 0, 0, tiled=True)]
    ppermute x9 -> x12, waiting for transfers between devices: 11.5 us -> 22.6 us  [flip(): return lax.ppermute(values, 'gz', [(g, g ^ k) for g in range(GZ)])]
    all_to_all x1 -> x0, starting transfers between devices: 9.02 us -> none  [shards(): got = lax.all_to_all(send, 'dp', 0, 0, tiled=True)]
    all_to_all x1, waiting for transfers between devices: 8.67 us -> 0.01 us  [shards(): owned = lax.all_to_all(copies, 'dp', 0, 0, tiled=True)]
    all_gather x1 -> x0, blocking collectives: 8.16 us -> none  [shards(): mixed_all = lax.all_gather(mixed, 'gz', axis=0, tiled=True)]
    ppermute x9 -> x12, starting transfers between devices: 10.9 us -> 14.3 us  [flip(): return lax.ppermute(values, 'gz', [(g, g ^ k) for g in range(GZ)])]
    all_to_all x1 -> x0, waiting for transfers between devices: 2.48 us -> none  [shards(): got = lax.all_to_all(send, 'dp', 0, 0, tiled=True)]
    all_to_all x1, starting transfers between devices: 6.07 us -> 3.93 us  [shards(): owned = lax.all_to_all(copies, 'dp', 0, 0, tiled=True)]
  transfers between devices with their start and end apart: 11 -> 13, of which waited for: 7 -> 8; matrix products, arithmetic and copies ran while one was open for 0% -> 0% of each run, Pallas kernels for 11% -> 9%
where the time goes in v5:
time: 94.4 us; the launch traced here: 92.9 us
  Pallas kernels  31 us (33%)
  waiting for transfers between devices  22.6 us (24%)
  blocking collectives  18.8 us (20%)
  starting transfers between devices  18.3 us (19%)
  local copies, waits for them, and re-layouts  1.4 us (1%)
    ppermute x12, waiting for transfers between devices, flip(): return lax.ppermute(values, 'gz', [(g, g ^ k) for g in range(GZ)])  22.6 us
    all_to_all x1, blocking collectives, shards(): got = lax.all_to_all(send, 'dp', 0, 0, tiled=True)  18.8 us
    pallas_call x1, Pallas kernels, shards(): pl.pallas_call(functools.partial(slope_kernel, 768), out_shape=(jax.Shape...  14.9 us
    ppermute x12, starting transfers between devices, flip(): return lax.ppermute(values, 'gz', [(g, g ^ k) for g in range(GZ)])  14.3 us
    pallas_call x1, Pallas kernels, shards(): pl.pallas_call(functools.partial(field_grad_kernel, 768), out_shape=jax.S...  8.43 us
    pallas_call x1, Pallas kernels, shards(): pl.pallas_call(field_modes_kernel, out_shape=tuple((shaped(OWNED, MODES)...  5.14 us
    all_to_all x1, starting transfers between devices, shards(): owned = lax.all_to_all(copies, 'dp', 0, 0, tiled=True)  3.93 us
  transfers between devices with their start and end apart: 13, of which 8 were waited for; matrix products, arithmetic and copies ran while one was open for 0% of the time, Pallas kernels for 9%

profile of v5, /device:TPU:0, one launch (start us, length us, event | category | flops | bytes accessed | tf_op | source)
XLA Modules:
  0.0 92.9 jit_solution(6543776539052269434)
XLA Ops:
  0.6 0.0 copy-start
  0.6 0.0 copy-start.10
  0.7 0.0 copy-start.6
  0.7 5.1 %field_modes.1 = (f32[64,256]{1,0:T(8,128)S(1)}, f32[64,256]{1,0:T(8,128)S(1)}, f32[64,256]{1,0:T(8,128)S(1)}, f32[64,256]{1,0:T(8,128)S(1)}, f32[96,256]{1,0:T(...) custom-call(s32[1]{0:T(128)} %bitcast.slab_ref, ...), custom_call_target="tpu_custom_call" | custom-call | tf_op jit(solution)/shard_map/field_modes/pallas_call | solution.py:421
  5.8 0.0 copy-start.2
  5.8 0.7 copy-done.2
  6.5 0.0 copy-start.1
  6.5 0.0 copy-start.3
  6.5 0.0 copy-start.4
  6.5 0.0 collective-permute-start.1
  6.5 0.5 collective-permute-start
  7.0 0.7 collective-permute-done.1.b_ref
  7.8 3.4 %collective-permute-start.2 = (f32[64,256]{1,0:T(8,128)S(1)}, f32[64,256]{1,0:T(8,128)S(1)}, u32[]{:S(2)}, u32[]{:S(2)}) collective-permute-start(f32[64,256]{1,0:T(8,128)S(1)} %add_pair.2), channel_id=1, source_target_pairs={{0,2},{1,3},{2,0},{3,1},{4,6},{5,7},{6,4},{7,5},{8,10},{9,11},{10,... | collective-permute-start | bytes 196616 | tf_op jit(solution)/shard_map/ppermute | solution.py:408
  11.1 0.0 collective-permute-done.one_ref
  11.1 2.5 %collective-permute-done.2.two_ref = f32[64,256]{1,0:T(8,128)S(1)} collective-permute-done((f32[64,256]{1,0:T(8,128)S(1)}, f32[64,256]{1,0:T(8,128)S(1)}, u32[]{:S(2)}, u32[]{:S(2)}) %collective-permute-start.2) | collective-permute-done | bytes 65568 | tf_op jit(solution)/shard_map/ppermute | solution.py:408
  13.6 0.0 copy-done
  13.6 0.1 mix_modes.1
  13.7 3.4 %collective-permute-start.4 = (f32[64,256]{1,0:T(8,128)S(1)}, f32[64,256]{1,0:T(8,128)S(1)}, u32[]{:S(2)}, u32[]{:S(2)}) collective-permute-start(f32[64,256]{1,0:T(8,128)S(1)} %get-tuple-element.34.own_ref), channel_id=1, source_target_pairs={{0,2},{1,3},{2,0},{3,1},{4,6},{5,7},{6,4},{7,5},{8,10},{9,11},{10,... | collective-permute-start | bytes 196616 | tf_op jit(solution)/shard_map/ppermute | solution.py:408
  17.1 0.0 collective-permute-start.3
  17.1 2.5 %collective-permute-done.4.two_ref = f32[64,256]{1,0:T(8,128)S(1)} collective-permute-done((f32[64,256]{1,0:T(8,128)S(1)}, f32[64,256]{1,0:T(8,128)S(1)}, u32[]{:S(2)}, u32[]{:S(2)}) %collective-permute-start.4) | collective-permute-done | bytes 65568 | tf_op jit(solution)/shard_map/ppermute | solution.py:408
  19.6 0.0 collective-permute-start.5
  19.6 0.0 copy-done.10
  19.6 0.1 copy.9.bias_ref
  19.6 0.0 collective-permute-done.3.one_ref
  19.6 1.2 %collective-permute-done.5.three_ref = f32[64,256]{1,0:T(8,128)S(1)} collective-permute-done((f32[64,256]{1,0:T(8,128)S(1)}, f32[64,256]{1,0:T(8,128)S(1)}, u32[]{:S(2)}, u32[]{:S(2)}) %collective-permute-start.5) | collective-permute-done | bytes 65568 | tf_op jit(solution)/shard_map/ppermute | solution.py:408
  20.8 0.0 copy-done.6
  20.8 14.9 %slope_and_modes.1 = (bf16[1,16,24,9216]{3,2,1,0:T(8,128)(2,1)}, f32[72,256]{1,0:T(8,128)S(1)}, f32[72,256]{1,0:T(8,128)S(1)}, f32[72,256]{1,0:T(8,128)S(1)}, f32[72,256]{1,0:T(8,128)S(1)}) custom-call(s32[1]{0:T(128)} %bitcast.slab_ref, bf16[1,16,24,9216]{3,2,1,0:T(8,128)(2,1)} %field_hbm.3, bf16[1,16,24,9216]{3,2,1,0:T(8,128)(2,1)} %cot_hbm.1, ...), custom_call_target="tpu_custom_call" | custom-call | tf_op jit(solution)/shard_map/slope_and_modes/pallas_call | solution.py:451
  35.7 0.0 copy-done.1
  35.7 0.0 copy-done.3
  35.7 0.0 copy-done.4
  35.8 0.2 collective-permute-start.7
  36.0 0.4 collective-permute-start.6
  36.3 0.8 collective-permute-done.7.b_ref
  37.1 3.6 %collective-permute-start.8 = (f32[72,256]{1,0:T(8,128)S(1)}, f32[72,256]{1,0:T(8,128)S(1)}, u32[]{:S(2)}, u32[]{:S(2)}) collective-permute-start(f32[72,256]{1,0:T(8,128)S(1)} %add_pair.3), channel_id=1, source_target_pairs={{0,2},{1,3},{2,0},{3,1},{4,6},{5,7},{6,4},{7,5},{8,10},{9,11},{10,... | collective-permute-start | bytes 221192 | tf_op jit(solution)/shard_map/ppermute | solution.py:408
  40.7 0.0 collective-permute-done.6.one_ref
  40.7 2.6 %collective-permute-done.8.two_ref = f32[72,256]{1,0:T(8,128)S(1)} collective-permute-done((f32[72,256]{1,0:T(8,128)S(1)}, f32[72,256]{1,0:T(8,128)S(1)}, u32[]{:S(2)}, u32[]{:S(2)}) %collective-permute-start.8) | collective-permute-done | bytes 73760 | tf_op jit(solution)/shard_map/ppermute | solution.py:408
  43.3 0.2 back_modes.1
  43.5 0.0 copy-start.5
  43.5 18.8 %all_to_all.10.got_ref = f32[32,24,128]{2,1,0:T(8,128)S(1)} all-to-all(f32[32,24,128]{2,1,0:T(8,128)S(1)} %get-tuple-element.41), channel_id=1, replica_groups=mesh['dp'=32,'gz'=4] {'dp'}, dimensions={0} | all-to-all | bytes 786432 | tf_op jit(solution)/shard_map/all_to_all | solution.py:495
  62.3 1.2 %sample_sum.1 = (f32[32,8,8,128]{3,2,1,0:T(8,128)}, f32[16,16]{1,0:T(8,128)}, f32[1,16]{1,0:T(1,128)}) custom-call(f32[32,24,128]{2,1,0:T(8,128)S(1)} %all_to_all.10.got_ref), custom_call_target="tpu_custom_call" | custom-call | tf_op jit(solution)/shard_map/sample_sum/pallas_call | solution.py:496
  63.5 3.9 %all-to-all-start.1 = ((f32[32,8,8,128]{3,2,1,0:T(8,128)}), f32[32,8,8,128]{3,2,1,0:T(8,128)S(1)}, u32[]{:S(2)}, u32[]{:S(2)}) async-start(f32[32,8,8,128]{3,2,1,0:T(8,128)} %get-tuple-element.45), calls=%async_computation.1 | async-start | bytes 2097152 | tf_op jit(solution)/shard_map/all_to_all | solution.py:504
  67.4 2.9 %collective-permute-start.10 = (f32[64,256]{1,0:T(8,128)S(1)}, f32[64,256]{1,0:T(8,128)S(1)}, u32[]{:S(2)}, u32[]{:S(2)}) collective-permute-start(f32[64,256]{1,0:T(8,128)S(1)} %get-tuple-element.44.own_ref), channel_id=1, source_target_pairs={{0,2},{1,3},{2,0},{3,1},{4,6},{5,7},{6,4},{7,5},{8,10},{9,11},{10,... | collective-permute-start | bytes 196616 | tf_op jit(solution)/shard_map/ppermute | solution.py:408
  70.3 0.0 collective-permute-start.9
  70.4 11.1 %collective-permute-done.10.two_ref = f32[64,256]{1,0:T(8,128)S(1)} collective-permute-done((f32[64,256]{1,0:T(8,128)S(1)}, f32[64,256]{1,0:T(8,128)S(1)}, u32[]{:S(2)}, u32[]{:S(2)}) %collective-permute-start.10) | collective-permute-done | bytes 65568 | tf_op jit(solution)/shard_map/ppermute | solution.py:408
  81.5 0.0 copy-start.7
  81.5 0.0 collective-permute-start.11
  81.5 0.0 collective-permute-done.9.one_ref
  81.5 0.0 copy-start.8
  81.5 1.2 %collective-permute-done.11.three_ref = f32[64,256]{1,0:T(8,128)S(1)} collective-permute-done((f32[64,256]{1,0:T(8,128)S(1)}, f32[64,256]{1,0:T(8,128)S(1)}, u32[]{:S(2)}, u32[]{:S(2)}) %collective-permute-start.11) | collective-permute-done | bytes 65568 | tf_op jit(solution)/shard_map/ppermute | solution.py:408
  82.7 0.0 copy-start.9
  82.7 0.0 copy-done.5
  82.7 0.0 copy-done.7
  82.7 0.0 copy-done.8
  82.8 0.6 copy-done.9
  83.4 8.4 %field_grad.1 = bf16[1,16,24,9216]{3,2,1,0:T(8,128)(2,1)} custom-call(s32[1]{0:T(128)} %bitcast.slab_ref, bf16[1,16,24,9216]{3,2,1,0:T(8,128)(2,1)} %get-tuple-element.35.dpre_hbm, f32[96,256]{1,0:T(8,128)} %copy-done.3, f32[96,256]{1,0:T(8,128)} %copy-done.4, bf16[256,384]{1,0:T(8,128)(2,1)} %copy-done.1, bf16[256,384]{1,0:T(8,128)(2,1)} %copy-done.2, ...), custom_call_target="tpu_custom_call" | custom-call | flops 2717908992 | bytes 14155776 | tf_op jit(solution)/shard_map/field_grad/pallas_call | solution.py:509
  91.8 0.0 all-to-all-done.1.got_ref
  91.8 1.0 %place_pieces.1 = f32[4,16,16,256]{3,2,1,0:T(8,128)} custom-call(f32[32,8,8,128]{3,2,1,0:T(8,128)S(1)} %all-to-all-done.1.got_ref), custom_call_target="tpu_custom_call" | custom-call | tf_op jit(solution)/shard_map/place_pieces/pallas_call | solution.py:533
  (2 shorter events, 0.0 us)
Async XLA Ops:
  0.6 13.0 %copy-start = (f32[4,16,16,256]{3,2,1,0:T(8,128)S(1)}, f32[4,16,16,256]{3,2,1,0:T(8,128)}, u32[]{:S(2)}) copy-start(f32[4,16,16,256]{3,2,1,0:T(8,128)} %weight_ref.6) | copy-start | bytes 3145732
  0.6 18.9 %copy-start.10 = (f32[16]{0:T(128)S(1)}, f32[16]{0:T(128)}, u32[]{:S(2)}) copy-start(f32[16]{0:T(128)} %param.9) | copy-start | bytes 196
  0.7 20.2 %copy-start.6 = (bf16[16,16]{1,0:T(8,128)(2,1)S(1)}, bf16[16,16]{1,0:T(8,128)(2,1)}, u32[]{:S(2)}) copy-start(bf16[16,16]{1,0:T(8,128)(2,1)} %weight_ref.7) | copy-start | bytes 1540
  5.8 0.7 copy-start.2
  6.5 29.2 %copy-start.1 = (bf16[256,384]{1,0:T(8,128)(2,1)}, bf16[256,384]{1,0:T(8,128)(2,1)S(1)}, u32[]{:S(2)}) copy-start(bf16[256,384]{1,0:T(8,128)(2,1)S(1)} %get-tuple-element.28.high) | copy-start | bytes 589828
  6.5 29.2 %copy-start.3 = (f32[96,256]{1,0:T(8,128)}, f32[96,256]{1,0:T(8,128)S(1)}, u32[]{:S(2)}) copy-start(f32[96,256]{1,0:T(8,128)S(1)} %get-tuple-element.26.outer) | copy-start | bytes 294916
  6.5 29.3 %copy-start.4 = (f32[96,256]{1,0:T(8,128)}, f32[96,256]{1,0:T(8,128)S(1)}, u32[]{:S(2)}) copy-start(f32[96,256]{1,0:T(8,128)S(1)} %get-tuple-element.27.inner) | copy-start | bytes 294916
  6.5 1.3 %collective-permute-start.1 = (f32[64,256]{1,0:T(8,128)S(1)}, f32[64,256]{1,0:T(8,128)S(1)}, u32[]{:S(2)}, u32[]{:S(2)}) collective-permute-start(f32[64,256]{1,0:T(8,128)S(1)} %get-tuple-element.33), channel_id=1, source_target_pairs={{0,1},{1,0},{2,3},{3,2},{4,5},{5,4},{6,7},{7,6},{8,9},{9,8},{10,11... | collective-permute-start | bytes 196616 | tf_op jit(solution)/shard_map/ppermute | solution.py:408
  6.5 4.6 %collective-permute-start = (f32[64,256]{1,0:T(8,128)S(1)}, f32[64,256]{1,0:T(8,128)S(1)}, u32[]{:S(2)}, u32[]{:S(2)}) collective-permute-start(f32[64,256]{1,0:T(8,128)S(1)} %get-tuple-element.31), channel_id=1, source_target_pairs={{0,1},{1,0},{2,3},{3,2},{4,5},{5,4},{6,7},{7,6},{8,9},{9,8},{10,11... | collective-permute-start | bytes 196616 | tf_op jit(solution)/shard_map/ppermute | solution.py:408
  7.8 5.8 %collective-permute-start.2 = (f32[64,256]{1,0:T(8,128)S(1)}, f32[64,256]{1,0:T(8,128)S(1)}, u32[]{:S(2)}, u32[]{:S(2)}) collective-permute-start(f32[64,256]{1,0:T(8,128)S(1)} %add_pair.2), channel_id=1, source_target_pairs={{0,2},{1,3},{2,0},{3,1},{4,6},{5,7},{6,4},{7,5},{8,10},{9,11},{10,... | collective-permute-start | bytes 196616 | tf_op jit(solution)/shard_map/ppermute | solution.py:408
  13.7 5.8 %collective-permute-start.4 = (f32[64,256]{1,0:T(8,128)S(1)}, f32[64,256]{1,0:T(8,128)S(1)}, u32[]{:S(2)}, u32[]{:S(2)}) collective-permute-start(f32[64,256]{1,0:T(8,128)S(1)} %get-tuple-element.34.own_ref), channel_id=1, source_target_pairs={{0,2},{1,3},{2,0},{3,1},{4,6},{5,7},{6,4},{7,5},{8,10},{9,11},{10,... | collective-permute-start | bytes 196616 | tf_op jit(solution)/shard_map/ppermute | solution.py:408
  17.1 2.6 %collective-permute-start.3 = (f32[64,256]{1,0:T(8,128)S(1)}, f32[64,256]{1,0:T(8,128)S(1)}, u32[]{:S(2)}, u32[]{:S(2)}) collective-permute-start(f32[64,256]{1,0:T(8,128)S(1)} %get-tuple-element.34.own_ref), channel_id=1, source_target_pairs={{0,1},{1,0},{2,3},{3,2},{4,5},{5,4},{6,7},{7,6},{8,9},{9,8},{10,11... | collective-permute-start | bytes 196616 | tf_op jit(solution)/shard_map/ppermute | solution.py:408
  19.6 1.3 %collective-permute-start.5 = (f32[64,256]{1,0:T(8,128)S(1)}, f32[64,256]{1,0:T(8,128)S(1)}, u32[]{:S(2)}, u32[]{:S(2)}) collective-permute-start(f32[64,256]{1,0:T(8,128)S(1)} %collective-permute-done.4.two_ref), channel_id=1, source_target_pairs={{0,1},{1,0},{2,3},{3,2},{4,5},{5,4},{6,7},{7,6},{8,9},{9,8},{10,11... | collective-permute-start | bytes 196616 | tf_op jit(solution)/shard_map/ppermute | solution.py:408
  35.8 1.3 %collective-permute-start.7 = (f32[72,256]{1,0:T(8,128)S(1)}, f32[72,256]{1,0:T(8,128)S(1)}, u32[]{:S(2)}, u32[]{:S(2)}) collective-permute-start(f32[72,256]{1,0:T(8,128)S(1)} %get-tuple-element.39), channel_id=1, source_target_pairs={{0,1},{1,0},{2,3},{3,2},{4,5},{5,4},{6,7},{7,6},{8,9},{9,8},{10,11... | collective-permute-start | bytes 221192 | tf_op jit(solution)/shard_map/ppermute | solution.py:408
  36.0 4.7 %collective-permute-start.6 = (f32[72,256]{1,0:T(8,128)S(1)}, f32[72,256]{1,0:T(8,128)S(1)}, u32[]{:S(2)}, u32[]{:S(2)}) collective-permute-start(f32[72,256]{1,0:T(8,128)S(1)} %get-tuple-element.37), channel_id=1, source_target_pairs={{0,1},{1,0},{2,3},{3,2},{4,5},{5,4},{6,7},{7,6},{8,9},{9,8},{10,11... | collective-permute-start | bytes 221192 | tf_op jit(solution)/shard_map/ppermute | solution.py:408
  37.1 6.2 %collective-permute-start.8 = (f32[72,256]{1,0:T(8,128)S(1)}, f32[72,256]{1,0:T(8,128)S(1)}, u32[]{:S(2)}, u32[]{:S(2)}) collective-permute-start(f32[72,256]{1,0:T(8,128)S(1)} %add_pair.3), channel_id=1, source_target_pairs={{0,2},{1,3},{2,0},{3,1},{4,6},{5,7},{6,4},{7,5},{8,10},{9,11},{10,... | collective-permute-start | bytes 221192 | tf_op jit(solution)/shard_map/ppermute | solution.py:408
  43.5 39.2 %copy-start.5 = (f32[64,256]{1,0:T(8,128)}, f32[64,256]{1,0:T(8,128)S(1)}, u32[]{:S(2)}) copy-start(f32[64,256]{1,0:T(8,128)S(1)} %get-tuple-element.44.own_ref) | copy-start | bytes 196612
  63.5 28.3 %all-to-all-start.1 = ((f32[32,8,8,128]{3,2,1,0:T(8,128)}), f32[32,8,8,128]{3,2,1,0:T(8,128)S(1)}, u32[]{:S(2)}, u32[]{:S(2)}) async-start(f32[32,8,8,128]{3,2,1,0:T(8,128)} %get-tuple-element.45), calls=%async_computation.1 | async-start | bytes 2097152 | tf_op jit(solution)/shard_map/all_to_all | solution.py:504
  67.4 14.1 %collective-permute-start.10 = (f32[64,256]{1,0:T(8,128)S(1)}, f32[64,256]{1,0:T(8,128)S(1)}, u32[]{:S(2)}, u32[]{:S(2)}) collective-permute-start(f32[64,256]{1,0:T(8,128)S(1)} %get-tuple-element.44.own_ref), channel_id=1, source_target_pairs={{0,2},{1,3},{2,0},{3,1},{4,6},{5,7},{6,4},{7,5},{8,10},{9,11},{10,... | collective-permute-start | bytes 196616 | tf_op jit(solution)/shard_map/ppermute | solution.py:408
  70.3 11.1 %collective-permute-start.9 = (f32[64,256]{1,0:T(8,128)S(1)}, f32[64,256]{1,0:T(8,128)S(1)}, u32[]{:S(2)}, u32[]{:S(2)}) collective-permute-start(f32[64,256]{1,0:T(8,128)S(1)} %get-tuple-element.44.own_ref), channel_id=1, source_target_pairs={{0,1},{1,0},{2,3},{3,2},{4,5},{5,4},{6,7},{7,6},{8,9},{9,8},{10,11... | collective-permute-start | bytes 196616 | tf_op jit(solution)/shard_map/ppermute | solution.py:408
  81.5 1.3 %copy-start.7 = (f32[64,256]{1,0:T(8,128)}, f32[64,256]{1,0:T(8,128)S(1)}, u32[]{:S(2)}) copy-start(f32[64,256]{1,0:T(8,128)S(1)} %collective-permute-done.10.two_ref) | copy-start | bytes 196612
  81.5 1.3 %collective-permute-start.11 = (f32[64,256]{1,0:T(8,128)S(1)}, f32[64,256]{1,0:T(8,128)S(1)}, u32[]{:S(2)}, u32[]{:S(2)}) collective-permute-start(f32[64,256]{1,0:T(8,128)S(1)} %collective-permute-done.10.two_ref), channel_id=1, source_target_pairs={{0,1},{1,0},{2,3},{3,2},{4,5},{5,4},{6,7},{7,6},{8,9},{9,8},{10,11... | collective-permute-start | bytes 196616 | tf_op jit(solution)/shard_map/ppermute | solution.py:408
  81.5 1.3 %copy-start.8 = (f32[64,256]{1,0:T(8,128)}, f32[64,256]{1,0:T(8,128)S(1)}, u32[]{:S(2)}) copy-start(f32[64,256]{1,0:T(8,128)S(1)} %collective-permute-done.9.one_ref) | copy-start | bytes 196612
  82.7 0.6 copy-start.9

commit v6 on v5

--- a/solution.py
+++ b/solution.py
@@ -170,10 +170,6 @@
     slab_ref,
     field_hbm,
     cot_hbm,
-    outer,
-    inner,
-    high,
-    low,
     weight_ref,
     bias_ref,
     own_ref,
@@ -184,7 +180,7 @@
     *rest,
 ):
     parts = rest[:GZ]
-    mixed, down, bias_cols, field, cot, out, lines, acc, point_acc, kron, kron_t, *sems = rest[GZ:]
+    outer, inner, high, low, mixed, down, bias_cols, field, cot, out, lines, acc, point_acc, kron, kron_t, *sems = rest[GZ:]
     field_sems, cot_sems, out_sems = sems
     fetch_field = copies_in(field_hbm, field, field_sems)
     fetch_cot = copies_in(cot_hbm, cot, cot_sems)
@@ -192,6 +188,8 @@
     for step in range(CHUNKS):
         fetch_field(step).start()
         fetch_cot(step).start()
+    outer[...], inner[...] = cell_tables()
+    high[...], low[...] = split(row_matrix(slab_ref[0]))
     down[...] = spread(weight_ref[...].T)
     bias_high, bias_low = split(
         jnp.dot(
@@ -342,16 +340,14 @@
     sub_width,
     slab_ref,
     dpre_hbm,
-    outer,
-    inner,
-    high,
-    low,
     weight_ref,
     own_ref,
     one_ref,
     two_ref,
     three_ref,
     out_hbm,
+    outer,
+    inner,
     up,
     back,
     dpre,
@@ -365,9 +361,10 @@
     store = copies_out(out, out_hbm, out_sems)
     for step in range(CHUNKS):
         fetch(step).start()
+    outer[...], inner[...] = cell_tables()
     up[...] = spread(weight_ref[...])
     join_parts(slab_ref[0], (own_ref, one_ref, two_ref, three_ref), back)
-    full = product((high[...], low[...]), split(back[...]), TN)
+    full = product(split(row_matrix(slab_ref[0])), split(back[...]), TN)
     lines[...] = (scale_fwd * full).reshape(C, ROWS, MODES).astype(bf16)
 
     for step in range(CHUNKS):
@@ -418,18 +415,16 @@
         )(parts[2], three)
         return parts[0], one, flip(forward, 2)
 
-    *coef_parts, outer, inner, high, low = pl.pallas_call(
+    coef_parts = pl.pallas_call(
         field_modes_kernel,
-        out_shape=tuple(shaped(OWNED, MODES) for _ in range(GZ))
-        + (
-            shaped(N, MODES),
-            shaped(N, MODES),
-            shaped(M * C, C * ROWS, dtype=bf16),
-            shaped(M * C, C * ROWS, dtype=bf16),
-        ),
+        out_shape=tuple(shaped(OWNED, MODES) for _ in range(GZ)),
         in_specs=[SM, ANY],
-        out_specs=(VM,) * (GZ + 4),
+        out_specs=(VM,) * GZ,
         scratch_shapes=[
+            pltpu.VMEM((N, MODES), jnp.float32),
+            pltpu.VMEM((N, MODES), jnp.float32),
+            pltpu.VMEM((M * C, C * ROWS), bf16),
+            pltpu.VMEM((M * C, C * ROWS), bf16),
             pltpu.VMEM((C, ROWS, CELLS), bf16),
             pltpu.VMEM((C * ROWS, MODES), jnp.float32),
             pltpu.VMEM((M * C, MODES), jnp.float32),
@@ -452,9 +447,13 @@
         functools.partial(slope_kernel, 768),
         out_shape=(jax.ShapeDtypeStruct(field.shape, bf16),)
         + tuple(shaped(OWNED + SUB, MODES) for _ in range(GZ)),
-        in_specs=[SM, ANY, ANY] + [VM] * 10,
+        in_specs=[SM, ANY, ANY] + [VM] * 6,
         out_specs=(ANY,) + (VM,) * GZ,
         scratch_shapes=[
+            pltpu.VMEM((N, MODES), jnp.float32),
+            pltpu.VMEM((N, MODES), jnp.float32),
+            pltpu.VMEM((M * C, C * ROWS), bf16),
+            pltpu.VMEM((M * C, C * ROWS), bf16),
             pltpu.VMEM((M * C, MODES), jnp.float32),
             pltpu.VMEM((C * SUB, C * SUB), bf16),
             pltpu.VMEM((C * SUB, C), bf16),
@@ -476,10 +475,6 @@
         slab,
         field,
         cotangent,
-        outer,
-        inner,
-        high,
-        low,
         point_weight,
         bias.reshape(C, 1),
         *mixed_parts,
@@ -493,6 +488,8 @@
     )(*reduce_parts(grad_parts), spec_weight, coef)
 
     got = lax.all_to_all(send, "dp", 0, 0, tiled=True)
+    two = flip(back, 2)
+    back_parts = (back, flip(back, 1), two, flip(two, 1))
     copies, point_grad, bias_grad = pl.pallas_call(
         functools.partial(
             outer_kernel, 1.0 / math.sqrt(dp * N), 1.0 / math.sqrt(dp * N * N * N)
@@ -501,17 +498,17 @@
         compiler_params=limit(8),
         name="sample_sum",
     )(got)
+    copies, *back_parts = lax.optimization_barrier((copies, *back_parts))
     owned = lax.all_to_all(copies, "dp", 0, 0, tiled=True)
-    bias_grad, back = lax.optimization_barrier((bias_grad, back))
-    two = flip(back, 2)
-    back_parts = (back, flip(back, 1), two, flip(two, 1))
 
     field_grad = pl.pallas_call(
         functools.partial(field_grad_kernel, 768),
         out_shape=jax.ShapeDtypeStruct(field.shape, bf16),
-        in_specs=[SM, ANY] + [VM] * 9,
+        in_specs=[SM, ANY] + [VM] * 5,
         out_specs=ANY,
         scratch_shapes=[
+            pltpu.VMEM((N, MODES), jnp.float32),
+            pltpu.VMEM((N, MODES), jnp.float32),
             pltpu.VMEM((C * SUB, C * SUB), bf16),
             pltpu.VMEM((M * C, MODES), jnp.float32),
             pltpu.VMEM((C, ROWS, CELLS), bf16),
@@ -528,7 +525,7 @@
             transcendentals=0,
         ),
         name="field_grad",
-    )(slab, dpre, outer, inner, high, low, point_weight, *back_parts)
+    )(slab, dpre, point_weight, *back_parts)
 
     spec_grad = pl.pallas_call(
         place_kernel,

time: 94.4 us -> 87.7 us (0.929); the launches traced: 92.9 us -> 87.3 us
  blocking collectives: 18.8 us -> 0 us
  starting transfers between devices: 18.3 us -> 29.6 us
  waiting for transfers between devices: 22.6 us -> 25.9 us
  local copies, waits for them, and re-layouts: 1.4 us -> 0.11 us
    all_to_all x1 -> x0, blocking collectives: 18.8 us -> none  [shards(): got = lax.all_to_all(send, 'dp', 0, 0, tiled=True)]
    all_to_all x0 -> x1, starting transfers between devices: none -> 9.25 us  [shards(): got = lax.all_to_all(send, 'dp', 0, 0, tiled=True)]
    all_to_all x1, waiting for transfers between devices: 0.01 us -> 8.93 us  [shards(): owned = lax.all_to_all(copies, 'dp', 0, 0, tiled=True)]
    ppermute x12, waiting for transfers between devices: 22.6 us -> 14.9 us  [flip(): return lax.ppermute(values, 'gz', [(g, g ^ k) for g in range(GZ)])]
    all_to_all x0 -> x1, waiting for transfers between devices: none -> 2.09 us  [shards(): got = lax.all_to_all(send, 'dp', 0, 0, tiled=True)]
    all_to_all x1, starting transfers between devices: 3.93 us -> 5.91 us  [shards(): owned = lax.all_to_all(copies, 'dp', 0, 0, tiled=True)]
    unnamed x22 -> x14, local copies, waits for them, and re-layouts: 1.31 us -> 0.03 us
  transfers between devices with their start and end apart: 13 -> 14, of which waited for: 8 -> 9; matrix products, arithmetic and copies ran while one was open for 0% -> 0% of each run, Pallas kernels for 9% -> 11%
where the time goes in v6:
time: 87.7 us; the launch traced here: 87.3 us
  Pallas kernels  30.9 us (35%)
  starting transfers between devices  29.6 us (34%)
  waiting for transfers between devices  25.9 us (30%)
    ppermute x12, waiting for transfers between devices, flip(): return lax.ppermute(values, 'gz', [(g, g ^ k) for g in range(GZ)])  14.9 us
    pallas_call x1, Pallas kernels, shards(): pl.pallas_call(functools.partial(slope_kernel, 768), out_shape=(jax.Shape...  14.4 us
    ppermute x12, starting transfers between devices, flip(): return lax.ppermute(values, 'gz', [(g, g ^ k) for g in range(GZ)])  14.4 us
    all_to_all x1, starting transfers between devices, shards(): got = lax.all_to_all(send, 'dp', 0, 0, tiled=True)  9.25 us
    all_to_all x1, waiting for transfers between devices, shards(): owned = lax.all_to_all(copies, 'dp', 0, 0, tiled=True)  8.93 us
    pallas_call x1, Pallas kernels, shards(): pl.pallas_call(functools.partial(field_grad_kernel, 768), out_shape=jax.S...  8.17 us
    all_to_all x1, starting transfers between devices, shards(): owned = lax.all_to_all(copies, 'dp', 0, 0, tiled=True)  5.91 us
    pallas_call x1, Pallas kernels, shards(): pl.pallas_call(field_modes_kernel, out_shape=tuple((shaped(OWNED, MODES)...  5.17 us
  transfers between devices with their start and end apart: 14, of which 9 were waited for; matrix products, arithmetic and copies ran while one was open for 0% of the time, Pallas kernels for 11%

profile of v6, /device:TPU:0, one launch (start us, length us, event | category | flops | bytes accessed | tf_op | source)
XLA Modules:
  0.0 87.3 jit_solution(10250957261464176217)
XLA Ops:
  0.6 0.0 copy-start
  0.6 0.0 copy-start.6
  0.7 0.0 copy-start.2
  0.7 5.2 %field_modes.1 = (f32[64,256]{1,0:T(8,128)S(1)}, f32[64,256]{1,0:T(8,128)S(1)}, f32[64,256]{1,0:T(8,128)S(1)}, f32[64,256]{1,0:T(8,128)S(1)}) custom-call(s32[1]{0:T(128)} %bitcast.slab_ref, bf16[1,16,24,9216]{3,2,1,0:T(8,128)(2,1)} %field_hbm.3), custom_call_target="tpu_custom_call" | custom-call | tf_op jit(solution)/shard_map/field_modes/pallas_call | solution.py:418
  5.8 0.1 collective-permute-start.1
  5.9 0.5 collective-permute-start
  6.4 0.7 collective-permute-done.1.b_ref
  7.2 3.4 %collective-permute-start.2 = (f32[64,256]{1,0:T(8,128)S(1)}, f32[64,256]{1,0:T(8,128)S(1)}, u32[]{:S(2)}, u32[]{:S(2)}) collective-permute-start(f32[64,256]{1,0:T(8,128)S(1)} %add_pair.2), channel_id=1, source_target_pairs={{0,2},{1,3},{2,0},{3,1},{4,6},{5,7},{6,4},{7,5},{8,10},{9,11},{10,... | collective-permute-start | bytes 196616 | tf_op jit(solution)/shard_map/ppermute | solution.py:405
  10.5 0.0 collective-permute-done.one_ref
  10.5 2.5 %collective-permute-done.2.two_ref = f32[64,256]{1,0:T(8,128)S(1)} collective-permute-done((f32[64,256]{1,0:T(8,128)S(1)}, f32[64,256]{1,0:T(8,128)S(1)}, u32[]{:S(2)}, u32[]{:S(2)}) %collective-permute-start.2) | collective-permute-done | bytes 65568 | tf_op jit(solution)/shard_map/ppermute | solution.py:405
  13.0 0.0 copy-done
  13.0 0.1 mix_modes.1
  13.1 3.4 %collective-permute-start.4 = (f32[64,256]{1,0:T(8,128)S(1)}, f32[64,256]{1,0:T(8,128)S(1)}, u32[]{:S(2)}, u32[]{:S(2)}) collective-permute-start(f32[64,256]{1,0:T(8,128)S(1)} %get-tuple-element.29.own_ref), channel_id=1, source_target_pairs={{0,2},{1,3},{2,0},{3,1},{4,6},{5,7},{6,4},{7,5},{8,10},{9,11},{10,... | collective-permute-start | bytes 196616 | tf_op jit(solution)/shard_map/ppermute | solution.py:405
  16.5 0.0 collective-permute-start.3
  16.5 2.5 %collective-permute-done.4.two_ref = f32[64,256]{1,0:T(8,128)S(1)} collective-permute-done((f32[64,256]{1,0:T(8,128)S(1)}, f32[64,256]{1,0:T(8,128)S(1)}, u32[]{:S(2)}, u32[]{:S(2)}) %collective-permute-start.4) | collective-permute-done | bytes 65568 | tf_op jit(solution)/shard_map/ppermute | solution.py:405
  19.0 0.0 collective-permute-start.5
  19.0 0.0 copy-done.6
  19.0 0.1 copy.9.bias_ref
  19.1 0.0 collective-permute-done.3.one_ref
  19.1 1.2 %collective-permute-done.5.three_ref = f32[64,256]{1,0:T(8,128)S(1)} collective-permute-done((f32[64,256]{1,0:T(8,128)S(1)}, f32[64,256]{1,0:T(8,128)S(1)}, u32[]{:S(2)}, u32[]{:S(2)}) %collective-permute-start.5) | collective-permute-done | bytes 65568 | tf_op jit(solution)/shard_map/ppermute | solution.py:405
  20.2 0.0 copy-done.2
  20.2 14.4 %slope_and_modes.1 = (bf16[1,16,24,9216]{3,2,1,0:T(8,128)(2,1)}, f32[72,256]{1,0:T(8,128)S(1)}, f32[72,256]{1,0:T(8,128)S(1)}, f32[72,256]{1,0:T(8,128)S(1)}, f32[72,256]{1,0:T(8,128)S(1)}) custom-call(s32[1]{0:T(128)} %bitcast.slab_ref, bf16[1,16,24,9216]{3,2,1,0:T(8,128)(2,1)} %field_hbm.3, bf16[1,16,24,9216]{3,2,1,0:T(8,128)(2,1)} %cot_hbm.1, ...), custom_call_target="tpu_custom_call" | custom-call | tf_op jit(solution)/shard_map/slope_and_modes/pallas_call | solution.py:446
  34.7 0.5 collective-permute-start.7
  35.2 0.4 collective-permute-start.6
  35.5 0.8 collective-permute-done.7.b_ref
  36.3 3.4 %collective-permute-start.8 = (f32[72,256]{1,0:T(8,128)S(1)}, f32[72,256]{1,0:T(8,128)S(1)}, u32[]{:S(2)}, u32[]{:S(2)}) collective-permute-start(f32[72,256]{1,0:T(8,128)S(1)} %add_pair.3), channel_id=1, source_target_pairs={{0,2},{1,3},{2,0},{3,1},{4,6},{5,7},{6,4},{7,5},{8,10},{9,11},{10,... | collective-permute-start | bytes 221192 | tf_op jit(solution)/shard_map/ppermute | solution.py:405
  39.6 0.0 collective-permute-done.6.one_ref
  39.6 2.6 %collective-permute-done.8.two_ref = f32[72,256]{1,0:T(8,128)S(1)} collective-permute-done((f32[72,256]{1,0:T(8,128)S(1)}, f32[72,256]{1,0:T(8,128)S(1)}, u32[]{:S(2)}, u32[]{:S(2)}) %collective-permute-start.8) | collective-permute-done | bytes 73760 | tf_op jit(solution)/shard_map/ppermute | solution.py:405
  42.2 0.8 back_modes.1
  43.0 0.0 copy-start.1
  43.0 9.2 %all-to-all-start = ((f32[32,24,128]{2,1,0:T(8,128)}), f32[32,24,128]{2,1,0:T(8,128)S(1)}, u32[]{:S(2)}, u32[]{:S(2)}) async-start(f32[32,24,128]{2,1,0:T(8,128)} %get-tuple-element.36), calls=%async_computation | async-start | bytes 786432 | tf_op jit(solution)/shard_map/all_to_all | solution.py:490
  52.3 3.0 %collective-permute-start.10 = (f32[64,256]{1,0:T(8,128)S(1)}, f32[64,256]{1,0:T(8,128)S(1)}, u32[]{:S(2)}, u32[]{:S(2)}) collective-permute-start(f32[64,256]{1,0:T(8,128)S(1)} %get-tuple-element.39.own_ref), channel_id=1, source_target_pairs={{0,2},{1,3},{2,0},{3,1},{4,6},{5,7},{6,4},{7,5},{8,10},{9,11},{10,... | collective-permute-start | bytes 196616 | tf_op jit(solution)/shard_map/ppermute | solution.py:405
  55.3 0.0 collective-permute-start.9
  55.3 4.7 %collective-permute-done.10.two_ref = f32[64,256]{1,0:T(8,128)S(1)} collective-permute-done((f32[64,256]{1,0:T(8,128)S(1)}, f32[64,256]{1,0:T(8,128)S(1)}, u32[]{:S(2)}, u32[]{:S(2)}) %collective-permute-start.10) | collective-permute-done | bytes 65568 | tf_op jit(solution)/shard_map/ppermute | solution.py:405
  59.9 0.0 copy-start.3
  59.9 0.0 collective-permute-start.11
  59.9 2.1 %all-to-all-done.got_ref = f32[32,24,128]{2,1,0:T(8,128)S(1)} async-done(((f32[32,24,128]{2,1,0:T(8,128)}), f32[32,24,128]{2,1,0:T(8,128)S(1)}, u32[]{:S(2)}, u32[]{:S(2)}) %all-to-all-start) | async-done | bytes 393248 | tf_op jit(solution)/shard_map/all_to_all | solution.py:490
  62.0 1.2 %sample_sum.1 = (f32[32,8,8,128]{3,2,1,0:T(8,128)}, f32[16,16]{1,0:T(8,128)}, f32[1,16]{1,0:T(1,128)}) custom-call(f32[32,24,128]{2,1,0:T(8,128)S(1)} %all-to-all-done.got_ref), custom_call_target="tpu_custom_call" | custom-call | tf_op jit(solution)/shard_map/sample_sum/pallas_call | solution.py:493
  63.2 0.0 collective-permute-done.9.one_ref
  63.2 0.0 copy-start.4
  63.2 0.0 collective-permute-done.11.three_ref
  63.2 0.0 copy-start.5
  63.2 5.9 %all-to-all-start.1 = ((f32[32,8,8,128]{3,2,1,0:T(8,128)}), f32[32,8,8,128]{3,2,1,0:T(8,128)S(1)}, u32[]{:S(2)}, u32[]{:S(2)}) async-start(f32[32,8,8,128]{3,2,1,0:T(8,128)} %get-tuple-element.43), calls=%async_computation.1 | async-start | bytes 2097152 | tf_op jit(solution)/shard_map/all_to_all | solution.py:502
  69.1 0.0 copy-done.1
  69.2 0.0 copy-done.3
  69.2 0.0 copy-done.4
  69.2 0.0 copy-done.5
  69.2 8.2 %field_grad.1 = bf16[1,16,24,9216]{3,2,1,0:T(8,128)(2,1)} custom-call(s32[1]{0:T(128)} %bitcast.slab_ref, bf16[1,16,24,9216]{3,2,1,0:T(8,128)(2,1)} %get-tuple-element.30.dpre_hbm, bf16[16,16]{1,0:T(8,128)(2,1)} %weight_ref.7, f32[64,256]{1,0:T(8,128)} %copy-done.1, f32[64,256]{1,0:T(8,128)} %copy-done.4, f32[64,256]{1,0:T(8,128)} %copy-done.3, ...), custom_call_target="tpu_custom_call" | custom-call | flops 2717908992 | bytes 14155776 | tf_op jit(solution)/shard_map/field_grad/pallas_call | solution.py:504
  77.4 8.9 %all-to-all-done.1.got_ref = f32[32,8,8,128]{3,2,1,0:T(8,128)S(1)} async-done(((f32[32,8,8,128]{3,2,1,0:T(8,128)}), f32[32,8,8,128]{3,2,1,0:T(8,128)S(1)}, u32[]{:S(2)}, u32[]{:S(2)}) %all-to-all-start.1) | async-done | bytes 1048608 | tf_op jit(solution)/shard_map/all_to_all | solution.py:502
  86.3 1.0 %place_pieces.1 = f32[4,16,16,256]{3,2,1,0:T(8,128)} custom-call(f32[32,8,8,128]{3,2,1,0:T(8,128)S(1)} %all-to-all-done.1.got_ref), custom_call_target="tpu_custom_call" | custom-call | tf_op jit(solution)/shard_map/place_pieces/pallas_call | solution.py:530
  (2 shorter events, 0.0 us)
Async XLA Ops:
  0.6 12.4 %copy-start = (f32[4,16,16,256]{3,2,1,0:T(8,128)S(1)}, f32[4,16,16,256]{3,2,1,0:T(8,128)}, u32[]{:S(2)}) copy-start(f32[4,16,16,256]{3,2,1,0:T(8,128)} %weight_ref.6) | copy-start | bytes 3145732
  0.6 18.4 %copy-start.6 = (f32[16]{0:T(128)S(1)}, f32[16]{0:T(128)}, u32[]{:S(2)}) copy-start(f32[16]{0:T(128)} %param.9) | copy-start | bytes 196
  0.7 19.6 %copy-start.2 = (bf16[16,16]{1,0:T(8,128)(2,1)S(1)}, bf16[16,16]{1,0:T(8,128)(2,1)}, u32[]{:S(2)}) copy-start(bf16[16,16]{1,0:T(8,128)(2,1)} %weight_ref.7) | copy-start | bytes 1540
  5.8 1.3 %collective-permute-start.1 = (f32[64,256]{1,0:T(8,128)S(1)}, f32[64,256]{1,0:T(8,128)S(1)}, u32[]{:S(2)}, u32[]{:S(2)}) collective-permute-start(f32[64,256]{1,0:T(8,128)S(1)} %get-tuple-element.28), channel_id=1, source_target_pairs={{0,1},{1,0},{2,3},{3,2},{4,5},{5,4},{6,7},{7,6},{8,9},{9,8},{10,11... | collective-permute-start | bytes 196616 | tf_op jit(solution)/shard_map/ppermute | solution.py:405
  5.9 4.6 %collective-permute-start = (f32[64,256]{1,0:T(8,128)S(1)}, f32[64,256]{1,0:T(8,128)S(1)}, u32[]{:S(2)}, u32[]{:S(2)}) collective-permute-start(f32[64,256]{1,0:T(8,128)S(1)} %get-tuple-element.26), channel_id=1, source_target_pairs={{0,1},{1,0},{2,3},{3,2},{4,5},{5,4},{6,7},{7,6},{8,9},{9,8},{10,11... | collective-permute-start | bytes 196616 | tf_op jit(solution)/shard_map/ppermute | solution.py:405
  7.2 5.8 %collective-permute-start.2 = (f32[64,256]{1,0:T(8,128)S(1)}, f32[64,256]{1,0:T(8,128)S(1)}, u32[]{:S(2)}, u32[]{:S(2)}) collective-permute-start(f32[64,256]{1,0:T(8,128)S(1)} %add_pair.2), channel_id=1, source_target_pairs={{0,2},{1,3},{2,0},{3,1},{4,6},{5,7},{6,4},{7,5},{8,10},{9,11},{10,... | collective-permute-start | bytes 196616 | tf_op jit(solution)/shard_map/ppermute | solution.py:405
  13.1 5.8 %collective-permute-start.4 = (f32[64,256]{1,0:T(8,128)S(1)}, f32[64,256]{1,0:T(8,128)S(1)}, u32[]{:S(2)}, u32[]{:S(2)}) collective-permute-start(f32[64,256]{1,0:T(8,128)S(1)} %get-tuple-element.29.own_ref), channel_id=1, source_target_pairs={{0,2},{1,3},{2,0},{3,1},{4,6},{5,7},{6,4},{7,5},{8,10},{9,11},{10,... | collective-permute-start | bytes 196616 | tf_op jit(solution)/shard_map/ppermute | solution.py:405
  16.5 2.6 %collective-permute-start.3 = (f32[64,256]{1,0:T(8,128)S(1)}, f32[64,256]{1,0:T(8,128)S(1)}, u32[]{:S(2)}, u32[]{:S(2)}) collective-permute-start(f32[64,256]{1,0:T(8,128)S(1)} %get-tuple-element.29.own_ref), channel_id=1, source_target_pairs={{0,1},{1,0},{2,3},{3,2},{4,5},{5,4},{6,7},{7,6},{8,9},{9,8},{10,11... | collective-permute-start | bytes 196616 | tf_op jit(solution)/shard_map/ppermute | solution.py:405
  19.0 1.3 %collective-permute-start.5 = (f32[64,256]{1,0:T(8,128)S(1)}, f32[64,256]{1,0:T(8,128)S(1)}, u32[]{:S(2)}, u32[]{:S(2)}) collective-permute-start(f32[64,256]{1,0:T(8,128)S(1)} %collective-permute-done.4.two_ref), channel_id=1, source_target_pairs={{0,1},{1,0},{2,3},{3,2},{4,5},{5,4},{6,7},{7,6},{8,9},{9,8},{10,11... | collective-permute-start | bytes 196616 | tf_op jit(solution)/shard_map/ppermute | solution.py:405
  34.7 1.6 %collective-permute-start.7 = (f32[72,256]{1,0:T(8,128)S(1)}, f32[72,256]{1,0:T(8,128)S(1)}, u32[]{:S(2)}, u32[]{:S(2)}) collective-permute-start(f32[72,256]{1,0:T(8,128)S(1)} %get-tuple-element.34), channel_id=1, source_target_pairs={{0,1},{1,0},{2,3},{3,2},{4,5},{5,4},{6,7},{7,6},{8,9},{9,8},{10,11... | collective-permute-start | bytes 221192 | tf_op jit(solution)/shard_map/ppermute | solution.py:405
  35.2 4.5 %collective-permute-start.6 = (f32[72,256]{1,0:T(8,128)S(1)}, f32[72,256]{1,0:T(8,128)S(1)}, u32[]{:S(2)}, u32[]{:S(2)}) collective-permute-start(f32[72,256]{1,0:T(8,128)S(1)} %get-tuple-element.32), channel_id=1, source_target_pairs={{0,1},{1,0},{2,3},{3,2},{4,5},{5,4},{6,7},{7,6},{8,9},{9,8},{10,11... | collective-permute-start | bytes 221192 | tf_op jit(solution)/shard_map/ppermute | solution.py:405
  36.3 5.9 %collective-permute-start.8 = (f32[72,256]{1,0:T(8,128)S(1)}, f32[72,256]{1,0:T(8,128)S(1)}, u32[]{:S(2)}, u32[]{:S(2)}) collective-permute-start(f32[72,256]{1,0:T(8,128)S(1)} %add_pair.3), channel_id=1, source_target_pairs={{0,2},{1,3},{2,0},{3,1},{4,6},{5,7},{6,4},{7,5},{8,10},{9,11},{10,... | collective-permute-start | bytes 221192 | tf_op jit(solution)/shard_map/ppermute | solution.py:405
  43.0 26.1 %copy-start.1 = (f32[64,256]{1,0:T(8,128)}, f32[64,256]{1,0:T(8,128)S(1)}, u32[]{:S(2)}) copy-start(f32[64,256]{1,0:T(8,128)S(1)} %get-tuple-element.39.own_ref) | copy-start | bytes 196612
  43.0 19.0 %all-to-all-start = ((f32[32,24,128]{2,1,0:T(8,128)}), f32[32,24,128]{2,1,0:T(8,128)S(1)}, u32[]{:S(2)}, u32[]{:S(2)}) async-start(f32[32,24,128]{2,1,0:T(8,128)} %get-tuple-element.36), calls=%async_computation | async-start | bytes 786432 | tf_op jit(solution)/shard_map/all_to_all | solution.py:490
  52.3 7.6 %collective-permute-start.10 = (f32[64,256]{1,0:T(8,128)S(1)}, f32[64,256]{1,0:T(8,128)S(1)}, u32[]{:S(2)}, u32[]{:S(2)}) collective-permute-start(f32[64,256]{1,0:T(8,128)S(1)} %get-tuple-element.39.own_ref), channel_id=1, source_target_pairs={{0,2},{1,3},{2,0},{3,1},{4,6},{5,7},{6,4},{7,5},{8,10},{9,11},{10,... | collective-permute-start | bytes 196616 | tf_op jit(solution)/shard_map/ppermute | solution.py:405
  55.3 7.9 %collective-permute-start.9 = (f32[64,256]{1,0:T(8,128)S(1)}, f32[64,256]{1,0:T(8,128)S(1)}, u32[]{:S(2)}, u32[]{:S(2)}) collective-permute-start(f32[64,256]{1,0:T(8,128)S(1)} %get-tuple-element.39.own_ref), channel_id=1, source_target_pairs={{0,1},{1,0},{2,3},{3,2},{4,5},{5,4},{6,7},{7,6},{8,9},{9,8},{10,11... | collective-permute-start | bytes 196616 | tf_op jit(solution)/shard_map/ppermute | solution.py:405
  59.9 9.2 %copy-start.3 = (f32[64,256]{1,0:T(8,128)}, f32[64,256]{1,0:T(8,128)S(1)}, u32[]{:S(2)}) copy-start(f32[64,256]{1,0:T(8,128)S(1)} %collective-permute-done.10.two_ref) | copy-start | bytes 196612
  59.9 3.3 %collective-permute-start.11 = (f32[64,256]{1,0:T(8,128)S(1)}, f32[64,256]{1,0:T(8,128)S(1)}, u32[]{:S(2)}, u32[]{:S(2)}) collective-permute-start(f32[64,256]{1,0:T(8,128)S(1)} %collective-permute-done.10.two_ref), channel_id=1, source_target_pairs={{0,1},{1,0},{2,3},{3,2},{4,5},{5,4},{6,7},{7,6},{8,9},{9,8},{10,11... | collective-permute-start | bytes 196616 | tf_op jit(solution)/shard_map/ppermute | solution.py:405
  63.2 6.0 %copy-start.4 = (f32[64,256]{1,0:T(8,128)}, f32[64,256]{1,0:T(8,128)S(1)}, u32[]{:S(2)}) copy-start(f32[64,256]{1,0:T(8,128)S(1)} %collective-permute-done.9.one_ref) | copy-start | bytes 196612
  63.2 6.0 %copy-start.5 = (f32[64,256]{1,0:T(8,128)}, f32[64,256]{1,0:T(8,128)S(1)}, u32[]{:S(2)}) copy-start(f32[64,256]{1,0:T(8,128)S(1)} %collective-permute-done.11.three_ref) | copy-start | bytes 196612
  63.2 23.1 %all-to-all-start.1 = ((f32[32,8,8,128]{3,2,1,0:T(8,128)}), f32[32,8,8,128]{3,2,1,0:T(8,128)S(1)}, u32[]{:S(2)}, u32[]{:S(2)}) async-start(f32[32,8,8,128]{3,2,1,0:T(8,128)} %get-tuple-element.43), calls=%async_computation.1 | async-start | bytes 2097152 | tf_op jit(solution)/shard_map/all_to_all | solution.py:502

commit v7 on v6

--- a/solution.py
+++ b/solution.py
@@ -295,15 +295,19 @@
         yield owner, owner // 8, owner // 4 % 2 * SUB, owner // 2 % 2 * SUB, owner % 2 * LANES
 
 
-def back_kernel(own_ref, one_ref, two_ref, weight_ref, coef_ref, back_ref, send_ref):
+def send_kernel(own_ref, one_ref, two_ref, coef_ref, full_ref, send_ref):
     full = (own_ref[...] + one_ref[...]) + two_ref[...]
+    full_ref[...] = full
     small = full[OWNED : OWNED + SUB, 0:LANES]
     for owner, a, i, o, p in pieces():
         send_ref[owner, 0:SUB, :] = coef_ref[a * C + i : a * C + i + SUB, p : p + LANES]
         send_ref[owner, SUB : 2 * SUB, :] = full[a * C + o : a * C + o + SUB, p : p + LANES]
         send_ref[owner, 2 * SUB : 3 * SUB, :] = small
+
+
+def back_kernel(full_ref, weight_ref, back_ref):
     for a in range(M // GZ):
-        grad = full[a * C : (a + 1) * C]
+        grad = full_ref[a * C : (a + 1) * C]
         for i in range(C):
             back_ref[a * C + i : a * C + i + 1, :] = (weight_ref[a, i] * grad).sum(
                 0, keepdims=True
@@ -331,9 +335,19 @@
     bias_ref[...] = sums * cell_norm
 
 
-def place_kernel(got_ref, out_ref):
-    for owner, a, i, o, p in pieces():
-        out_ref[a, i : i + SUB, o : o + SUB, p : p + LANES] = got_ref[owner]
+def place_kernel(got_ref, out_hbm, sems):
+    copies = [
+        pltpu.make_async_copy(
+            got_ref.at[owner],
+            out_hbm.at[a, i : i + SUB, o : o + SUB, p : p + LANES],
+            sems.at[owner],
+        )
+        for owner, a, i, o, p in pieces()
+    ]
+    for copy in copies:
+        copy.start()
+    for copy in copies:
+        copy.wait()
 
 
 def field_grad_kernel(
@@ -480,12 +494,18 @@
         *mixed_parts,
     )
 
-    back, send = pl.pallas_call(
+    full, send = pl.pallas_call(
+        send_kernel,
+        out_shape=(shaped(OWNED + SUB, MODES), shaped(dp, 3 * SUB, LANES)),
+        compiler_params=limit(8),
+        name="pieces_out",
+    )(*reduce_parts(grad_parts), coef)
+    back = pl.pallas_call(
         back_kernel,
-        out_shape=(shaped(OWNED, MODES), shaped(dp, 3 * SUB, LANES)),
+        out_shape=shaped(OWNED, MODES),
         compiler_params=limit(8),
         name="back_modes",
-    )(*reduce_parts(grad_parts), spec_weight, coef)
+    )(full, spec_weight)
 
     got = lax.all_to_all(send, "dp", 0, 0, tiled=True)
     two = flip(back, 2)
@@ -530,6 +550,9 @@
     spec_grad = pl.pallas_call(
         place_kernel,
         out_shape=shaped(M // GZ, C, C, MODES),
+        in_specs=[VM],
+        out_specs=ANY,
+        scratch_shapes=[pltpu.SemaphoreType.DMA((dp,))],
         compiler_params=limit(8),
         name="place_pieces",
     )(owned)

time: 87.7 us -> 88 us (level)
    pallas_call x2 -> x3, Pallas kernels: 1.84 us -> 2.19 us  [the longest x1 1.23 us: shards(): pl.pallas_call(place_kernel, out_shape=shaped(M // GZ, C, C, MODES), in_s...]
where the time goes in v7:
time: 88 us; the launch traced here: 87.7 us
  Pallas kernels  31.3 us (36%)
  starting transfers between devices  29.6 us (34%)
  waiting for transfers between devices  25.7 us (29%)
  between operations  0.97 us (1%)
    ppermute x12, waiting for transfers between devices, flip(): return lax.ppermute(values, 'gz', [(g, g ^ k) for g in range(GZ)])  14.7 us
    pallas_call x1, Pallas kernels, shards(): pl.pallas_call(functools.partial(slope_kernel, 768), out_shape=(jax.Shape...  14.4 us
    ppermute x12, starting transfers between devices, flip(): return lax.ppermute(values, 'gz', [(g, g ^ k) for g in range(GZ)])  14.4 us
    all_to_all x1, starting transfers between devices, shards(): got = lax.all_to_all(send, 'dp', 0, 0, tiled=True)  9.25 us
    all_to_all x1, waiting for transfers between devices, shards(): owned = lax.all_to_all(copies, 'dp', 0, 0, tiled=True)  8.94 us
    pallas_call x1, Pallas kernels, shards(): pl.pallas_call(functools.partial(field_grad_kernel, 768), out_shape=jax.S...  8.17 us
    all_to_all x1, starting transfers between devices, shards(): owned = lax.all_to_all(copies, 'dp', 0, 0, tiled=True)  5.91 us
    pallas_call x1, Pallas kernels, shards(): pl.pallas_call(field_modes_kernel, out_shape=tuple((shaped(OWNED, MODES)...  5.17 us
  transfers between devices with their start and end apart: 14, of which 9 were waited for; matrix products, arithmetic and copies ran while one was open for 0% of the time, Pallas kernels for 11%

profile of v7, /device:TPU:0, one launch (start us, length us, event | category | flops | bytes accessed | tf_op | source)
XLA Modules:
  0.0 87.7 jit_solution(12651695360298151472)
XLA Ops:
  0.6 0.0 copy-start
  0.6 0.0 copy-start.6
  0.7 0.0 copy-start.2
  0.7 5.2 %field_modes.1 = (f32[64,256]{1,0:T(8,128)S(1)}, f32[64,256]{1,0:T(8,128)S(1)}, f32[64,256]{1,0:T(8,128)S(1)}, f32[64,256]{1,0:T(8,128)S(1)}) custom-call(s32[1]{0:T(128)} %bitcast.slab_ref, bf16[1,16,24,9216]{3,2,1,0:T(8,128)(2,1)} %field_hbm.3), custom_call_target="tpu_custom_call" | custom-call | tf_op jit(solution)/shard_map/field_modes/pallas_call | solution.py:432
  5.8 0.1 collective-permute-start.1
  5.9 0.5 collective-permute-start
  6.4 0.7 collective-permute-done.1.b_ref
  7.2 3.4 %collective-permute-start.2 = (f32[64,256]{1,0:T(8,128)S(1)}, f32[64,256]{1,0:T(8,128)S(1)}, u32[]{:S(2)}, u32[]{:S(2)}) collective-permute-start(f32[64,256]{1,0:T(8,128)S(1)} %add_pair.2), channel_id=1, source_target_pairs={{0,2},{1,3},{2,0},{3,1},{4,6},{5,7},{6,4},{7,5},{8,10},{9,11},{10,... | collective-permute-start | bytes 196616 | tf_op jit(solution)/shard_map/ppermute | solution.py:419
  10.5 0.0 collective-permute-done.one_ref
  10.5 2.5 %collective-permute-done.2.two_ref = f32[64,256]{1,0:T(8,128)S(1)} collective-permute-done((f32[64,256]{1,0:T(8,128)S(1)}, f32[64,256]{1,0:T(8,128)S(1)}, u32[]{:S(2)}, u32[]{:S(2)}) %collective-permute-start.2) | collective-permute-done | bytes 65568 | tf_op jit(solution)/shard_map/ppermute | solution.py:419
  13.0 0.0 copy-done
  13.0 0.1 mix_modes.1
  13.1 3.4 %collective-permute-start.4 = (f32[64,256]{1,0:T(8,128)S(1)}, f32[64,256]{1,0:T(8,128)S(1)}, u32[]{:S(2)}, u32[]{:S(2)}) collective-permute-start(f32[64,256]{1,0:T(8,128)S(1)} %get-tuple-element.29.own_ref), channel_id=1, source_target_pairs={{0,2},{1,3},{2,0},{3,1},{4,6},{5,7},{6,4},{7,5},{8,10},{9,11},{10,... | collective-permute-start | bytes 196616 | tf_op jit(solution)/shard_map/ppermute | solution.py:419
  16.5 0.0 collective-permute-start.3
  16.5 2.5 %collective-permute-done.4.two_ref = f32[64,256]{1,0:T(8,128)S(1)} collective-permute-done((f32[64,256]{1,0:T(8,128)S(1)}, f32[64,256]{1,0:T(8,128)S(1)}, u32[]{:S(2)}, u32[]{:S(2)}) %collective-permute-start.4) | collective-permute-done | bytes 65568 | tf_op jit(solution)/shard_map/ppermute | solution.py:419
  19.0 0.0 collective-permute-start.5
  19.0 0.0 copy-done.6
  19.0 0.1 copy.9.bias_ref
  19.1 0.0 collective-permute-done.3.one_ref
  19.1 1.2 %collective-permute-done.5.three_ref = f32[64,256]{1,0:T(8,128)S(1)} collective-permute-done((f32[64,256]{1,0:T(8,128)S(1)}, f32[64,256]{1,0:T(8,128)S(1)}, u32[]{:S(2)}, u32[]{:S(2)}) %collective-permute-start.5) | collective-permute-done | bytes 65568 | tf_op jit(solution)/shard_map/ppermute | solution.py:419
  20.2 0.0 copy-done.2
  20.2 14.4 %slope_and_modes.1 = (bf16[1,16,24,9216]{3,2,1,0:T(8,128)(2,1)}, f32[72,256]{1,0:T(8,128)S(1)}, f32[72,256]{1,0:T(8,128)S(1)}, f32[72,256]{1,0:T(8,128)S(1)}, f32[72,256]{1,0:T(8,128)S(1)}) custom-call(s32[1]{0:T(128)} %bitcast.slab_ref, bf16[1,16,24,9216]{3,2,1,0:T(8,128)(2,1)} %field_hbm.3, bf16[1,16,24,9216]{3,2,1,0:T(8,128)(2,1)} %cot_hbm.1, ...), custom_call_target="tpu_custom_call" | custom-call | tf_op jit(solution)/shard_map/slope_and_modes/pallas_call | solution.py:460
  34.7 0.5 collective-permute-start.7
  35.2 0.4 collective-permute-start.6
  35.5 0.8 collective-permute-done.7.b_ref
  36.3 3.4 %collective-permute-start.8 = (f32[72,256]{1,0:T(8,128)S(1)}, f32[72,256]{1,0:T(8,128)S(1)}, u32[]{:S(2)}, u32[]{:S(2)}) collective-permute-start(f32[72,256]{1,0:T(8,128)S(1)} %add_pair.3), channel_id=1, source_target_pairs={{0,2},{1,3},{2,0},{3,1},{4,6},{5,7},{6,4},{7,5},{8,10},{9,11},{10,... | collective-permute-start | bytes 221192 | tf_op jit(solution)/shard_map/ppermute | solution.py:419
  39.6 0.0 collective-permute-done.6.one_ref
  39.6 2.6 %collective-permute-done.8.two_ref = f32[72,256]{1,0:T(8,128)S(1)} collective-permute-done((f32[72,256]{1,0:T(8,128)S(1)}, f32[72,256]{1,0:T(8,128)S(1)}, u32[]{:S(2)}, u32[]{:S(2)}) %collective-permute-start.8) | collective-permute-done | bytes 73760 | tf_op jit(solution)/shard_map/ppermute | solution.py:419
  42.2 0.8 pieces_out.1
  43.0 9.2 %all-to-all-start = ((f32[32,24,128]{2,1,0:T(8,128)}), f32[32,24,128]{2,1,0:T(8,128)S(1)}, u32[]{:S(2)}, u32[]{:S(2)}) async-start(f32[32,24,128]{2,1,0:T(8,128)} %get-tuple-element.36), calls=%async_computation | async-start | bytes 786432 | tf_op jit(solution)/shard_map/all_to_all | solution.py:510
  52.3 0.2 back_modes.1.own_ref
  52.4 0.0 copy-start.1
  52.5 3.0 %collective-permute-start.10 = (f32[64,256]{1,0:T(8,128)S(1)}, f32[64,256]{1,0:T(8,128)S(1)}, u32[]{:S(2)}, u32[]{:S(2)}) collective-permute-start(f32[64,256]{1,0:T(8,128)S(1)} %back_modes.1.own_ref), channel_id=1, source_target_pairs={{0,2},{1,3},{2,0},{3,1},{4,6},{5,7},{6,4},{7,5},{8,10},{9,11},{10,... | collective-permute-start | bytes 196616 | tf_op jit(solution)/shard_map/ppermute | solution.py:419
  55.4 0.0 collective-permute-start.9
  55.4 4.5 %collective-permute-done.10.two_ref = f32[64,256]{1,0:T(8,128)S(1)} collective-permute-done((f32[64,256]{1,0:T(8,128)S(1)}, f32[64,256]{1,0:T(8,128)S(1)}, u32[]{:S(2)}, u32[]{:S(2)}) %collective-permute-start.10) | collective-permute-done | bytes 65568 | tf_op jit(solution)/shard_map/ppermute | solution.py:419
  59.9 0.0 copy-start.3
  59.9 0.0 collective-permute-start.11
  59.9 2.1 %all-to-all-done.got_ref = f32[32,24,128]{2,1,0:T(8,128)S(1)} async-done(((f32[32,24,128]{2,1,0:T(8,128)}), f32[32,24,128]{2,1,0:T(8,128)S(1)}, u32[]{:S(2)}, u32[]{:S(2)}) %all-to-all-start) | async-done | bytes 393248 | tf_op jit(solution)/shard_map/all_to_all | solution.py:510
  62.0 1.2 %sample_sum.1 = (f32[32,8,8,128]{3,2,1,0:T(8,128)}, f32[16,16]{1,0:T(8,128)}, f32[1,16]{1,0:T(1,128)}) custom-call(f32[32,24,128]{2,1,0:T(8,128)S(1)} %all-to-all-done.got_ref), custom_call_target="tpu_custom_call" | custom-call | tf_op jit(solution)/shard_map/sample_sum/pallas_call | solution.py:513
  63.2 0.0 collective-permute-done.9.one_ref
  63.2 0.0 copy-start.4
  63.2 0.0 collective-permute-done.11.three_ref
  63.2 0.0 copy-start.5
  63.2 5.9 %all-to-all-start.1 = ((f32[32,8,8,128]{3,2,1,0:T(8,128)}), f32[32,8,8,128]{3,2,1,0:T(8,128)S(1)}, u32[]{:S(2)}, u32[]{:S(2)}) async-start(f32[32,8,8,128]{3,2,1,0:T(8,128)} %get-tuple-element.43), calls=%async_computation.1 | async-start | bytes 2097152 | tf_op jit(solution)/shard_map/all_to_all | solution.py:522
  69.1 0.0 copy-done.1
  69.1 0.0 copy-done.3
  69.1 0.0 copy-done.4
  69.2 0.0 copy-done.5
  69.2 8.2 %field_grad.1 = bf16[1,16,24,9216]{3,2,1,0:T(8,128)(2,1)} custom-call(s32[1]{0:T(128)} %bitcast.slab_ref, bf16[1,16,24,9216]{3,2,1,0:T(8,128)(2,1)} %get-tuple-element.30.dpre_hbm, bf16[16,16]{1,0:T(8,128)(2,1)} %weight_ref.7, f32[64,256]{1,0:T(8,128)} %copy-done.1, f32[64,256]{1,0:T(8,128)} %copy-done.4, f32[64,256]{1,0:T(8,128)} %copy-done.3, ...), custom_call_target="tpu_custom_call" | custom-call | flops 2717908992 | bytes 14155776 | tf_op jit(solution)/shard_map/field_grad/pallas_call | solution.py:524
  77.3 8.9 %all-to-all-done.1.got_ref = f32[32,8,8,128]{3,2,1,0:T(8,128)S(1)} async-done(((f32[32,8,8,128]{3,2,1,0:T(8,128)}), f32[32,8,8,128]{3,2,1,0:T(8,128)S(1)}, u32[]{:S(2)}, u32[]{:S(2)}) %all-to-all-start.1) | async-done | bytes 1048608 | tf_op jit(solution)/shard_map/all_to_all | solution.py:522
  86.3 1.2 %place_pieces.1 = f32[4,16,16,256]{3,2,1,0:T(8,128)} custom-call(f32[32,8,8,128]{3,2,1,0:T(8,128)S(1)} %all-to-all-done.1.got_ref), custom_call_target="tpu_custom_call" | custom-call | tf_op jit(solution)/shard_map/place_pieces/pallas_call | solution.py:550
  (2 shorter events, 0.0 us)
Async XLA Ops:
  0.6 12.4 %copy-start = (f32[4,16,16,256]{3,2,1,0:T(8,128)S(1)}, f32[4,16,16,256]{3,2,1,0:T(8,128)}, u32[]{:S(2)}) copy-start(f32[4,16,16,256]{3,2,1,0:T(8,128)} %weight_ref.6) | copy-start | bytes 3145732
  0.6 18.4 %copy-start.6 = (f32[16]{0:T(128)S(1)}, f32[16]{0:T(128)}, u32[]{:S(2)}) copy-start(f32[16]{0:T(128)} %param.9) | copy-start | bytes 196
  0.7 19.6 %copy-start.2 = (bf16[16,16]{1,0:T(8,128)(2,1)S(1)}, bf16[16,16]{1,0:T(8,128)(2,1)}, u32[]{:S(2)}) copy-start(bf16[16,16]{1,0:T(8,128)(2,1)} %weight_ref.7) | copy-start | bytes 1540
  5.8 1.3 %collective-permute-start.1 = (f32[64,256]{1,0:T(8,128)S(1)}, f32[64,256]{1,0:T(8,128)S(1)}, u32[]{:S(2)}, u32[]{:S(2)}) collective-permute-start(f32[64,256]{1,0:T(8,128)S(1)} %get-tuple-element.28), channel_id=1, source_target_pairs={{0,1},{1,0},{2,3},{3,2},{4,5},{5,4},{6,7},{7,6},{8,9},{9,8},{10,11... | collective-permute-start | bytes 196616 | tf_op jit(solution)/shard_map/ppermute | solution.py:419
  5.9 4.6 %collective-permute-start = (f32[64,256]{1,0:T(8,128)S(1)}, f32[64,256]{1,0:T(8,128)S(1)}, u32[]{:S(2)}, u32[]{:S(2)}) collective-permute-start(f32[64,256]{1,0:T(8,128)S(1)} %get-tuple-element.26), channel_id=1, source_target_pairs={{0,1},{1,0},{2,3},{3,2},{4,5},{5,4},{6,7},{7,6},{8,9},{9,8},{10,11... | collective-permute-start | bytes 196616 | tf_op jit(solution)/shard_map/ppermute | solution.py:419
  7.2 5.8 %collective-permute-start.2 = (f32[64,256]{1,0:T(8,128)S(1)}, f32[64,256]{1,0:T(8,128)S(1)}, u32[]{:S(2)}, u32[]{:S(2)}) collective-permute-start(f32[64,256]{1,0:T(8,128)S(1)} %add_pair.2), channel_id=1, source_target_pairs={{0,2},{1,3},{2,0},{3,1},{4,6},{5,7},{6,4},{7,5},{8,10},{9,11},{10,... | collective-permute-start | bytes 196616 | tf_op jit(solution)/shard_map/ppermute | solution.py:419
  13.1 5.8 %collective-permute-start.4 = (f32[64,256]{1,0:T(8,128)S(1)}, f32[64,256]{1,0:T(8,128)S(1)}, u32[]{:S(2)}, u32[]{:S(2)}) collective-permute-start(f32[64,256]{1,0:T(8,128)S(1)} %get-tuple-element.29.own_ref), channel_id=1, source_target_pairs={{0,2},{1,3},{2,0},{3,1},{4,6},{5,7},{6,4},{7,5},{8,10},{9,11},{10,... | collective-permute-start | bytes 196616 | tf_op jit(solution)/shard_map/ppermute | solution.py:419
  16.5 2.6 %collective-permute-start.3 = (f32[64,256]{1,0:T(8,128)S(1)}, f32[64,256]{1,0:T(8,128)S(1)}, u32[]{:S(2)}, u32[]{:S(2)}) collective-permute-start(f32[64,256]{1,0:T(8,128)S(1)} %get-tuple-element.29.own_ref), channel_id=1, source_target_pairs={{0,1},{1,0},{2,3},{3,2},{4,5},{5,4},{6,7},{7,6},{8,9},{9,8},{10,11... | collective-permute-start | bytes 196616 | tf_op jit(solution)/shard_map/ppermute | solution.py:419
  19.0 1.3 %collective-permute-start.5 = (f32[64,256]{1,0:T(8,128)S(1)}, f32[64,256]{1,0:T(8,128)S(1)}, u32[]{:S(2)}, u32[]{:S(2)}) collective-permute-start(f32[64,256]{1,0:T(8,128)S(1)} %collective-permute-done.4.two_ref), channel_id=1, source_target_pairs={{0,1},{1,0},{2,3},{3,2},{4,5},{5,4},{6,7},{7,6},{8,9},{9,8},{10,11... | collective-permute-start | bytes 196616 | tf_op jit(solution)/shard_map/ppermute | solution.py:419
  34.7 1.6 %collective-permute-start.7 = (f32[72,256]{1,0:T(8,128)S(1)}, f32[72,256]{1,0:T(8,128)S(1)}, u32[]{:S(2)}, u32[]{:S(2)}) collective-permute-start(f32[72,256]{1,0:T(8,128)S(1)} %get-tuple-element.34), channel_id=1, source_target_pairs={{0,1},{1,0},{2,3},{3,2},{4,5},{5,4},{6,7},{7,6},{8,9},{9,8},{10,11... | collective-permute-start | bytes 221192 | tf_op jit(solution)/shard_map/ppermute | solution.py:419
  35.2 4.5 %collective-permute-start.6 = (f32[72,256]{1,0:T(8,128)S(1)}, f32[72,256]{1,0:T(8,128)S(1)}, u32[]{:S(2)}, u32[]{:S(2)}) collective-permute-start(f32[72,256]{1,0:T(8,128)S(1)} %get-tuple-element.32), channel_id=1, source_target_pairs={{0,1},{1,0},{2,3},{3,2},{4,5},{5,4},{6,7},{7,6},{8,9},{9,8},{10,11... | collective-permute-start | bytes 221192 | tf_op jit(solution)/shard_map/ppermute | solution.py:419
  36.3 5.9 %collective-permute-start.8 = (f32[72,256]{1,0:T(8,128)S(1)}, f32[72,256]{1,0:T(8,128)S(1)}, u32[]{:S(2)}, u32[]{:S(2)}) collective-permute-start(f32[72,256]{1,0:T(8,128)S(1)} %add_pair.3), channel_id=1, source_target_pairs={{0,2},{1,3},{2,0},{3,1},{4,6},{5,7},{6,4},{7,5},{8,10},{9,11},{10,... | collective-permute-start | bytes 221192 | tf_op jit(solution)/shard_map/ppermute | solution.py:419
  43.0 19.0 %all-to-all-start = ((f32[32,24,128]{2,1,0:T(8,128)}), f32[32,24,128]{2,1,0:T(8,128)S(1)}, u32[]{:S(2)}, u32[]{:S(2)}) async-start(f32[32,24,128]{2,1,0:T(8,128)} %get-tuple-element.36), calls=%async_computation | async-start | bytes 786432 | tf_op jit(solution)/shard_map/all_to_all | solution.py:510
  52.4 16.7 %copy-start.1 = (f32[64,256]{1,0:T(8,128)}, f32[64,256]{1,0:T(8,128)S(1)}, u32[]{:S(2)}) copy-start(f32[64,256]{1,0:T(8,128)S(1)} %back_modes.1.own_ref) | copy-start | bytes 196612
  52.5 7.4 %collective-permute-start.10 = (f32[64,256]{1,0:T(8,128)S(1)}, f32[64,256]{1,0:T(8,128)S(1)}, u32[]{:S(2)}, u32[]{:S(2)}) collective-permute-start(f32[64,256]{1,0:T(8,128)S(1)} %back_modes.1.own_ref), channel_id=1, source_target_pairs={{0,2},{1,3},{2,0},{3,1},{4,6},{5,7},{6,4},{7,5},{8,10},{9,11},{10,... | collective-permute-start | bytes 196616 | tf_op jit(solution)/shard_map/ppermute | solution.py:419
  55.4 7.7 %collective-permute-start.9 = (f32[64,256]{1,0:T(8,128)S(1)}, f32[64,256]{1,0:T(8,128)S(1)}, u32[]{:S(2)}, u32[]{:S(2)}) collective-permute-start(f32[64,256]{1,0:T(8,128)S(1)} %back_modes.1.own_ref), channel_id=1, source_target_pairs={{0,1},{1,0},{2,3},{3,2},{4,5},{5,4},{6,7},{7,6},{8,9},{9,8},{10,11... | collective-permute-start | bytes 196616 | tf_op jit(solution)/shard_map/ppermute | solution.py:419
  59.9 9.2 %copy-start.3 = (f32[64,256]{1,0:T(8,128)}, f32[64,256]{1,0:T(8,128)S(1)}, u32[]{:S(2)}) copy-start(f32[64,256]{1,0:T(8,128)S(1)} %collective-permute-done.10.two_ref) | copy-start | bytes 196612
  59.9 3.3 %collective-permute-start.11 = (f32[64,256]{1,0:T(8,128)S(1)}, f32[64,256]{1,0:T(8,128)S(1)}, u32[]{:S(2)}, u32[]{:S(2)}) collective-permute-start(f32[64,256]{1,0:T(8,128)S(1)} %collective-permute-done.10.two_ref), channel_id=1, source_target_pairs={{0,1},{1,0},{2,3},{3,2},{4,5},{5,4},{6,7},{7,6},{8,9},{9,8},{10,11... | collective-permute-start | bytes 196616 | tf_op jit(solution)/shard_map/ppermute | solution.py:419
  63.2 6.0 %copy-start.4 = (f32[64,256]{1,0:T(8,128)}, f32[64,256]{1,0:T(8,128)S(1)}, u32[]{:S(2)}) copy-start(f32[64,256]{1,0:T(8,128)S(1)} %collective-permute-done.9.one_ref) | copy-start | bytes 196612
  63.2 6.0 %copy-start.5 = (f32[64,256]{1,0:T(8,128)}, f32[64,256]{1,0:T(8,128)S(1)}, u32[]{:S(2)}) copy-start(f32[64,256]{1,0:T(8,128)S(1)} %collective-permute-done.11.three_ref) | copy-start | bytes 196612
  63.2 23.1 %all-to-all-start.1 = ((f32[32,8,8,128]{3,2,1,0:T(8,128)}), f32[32,8,8,128]{3,2,1,0:T(8,128)S(1)}, u32[]{:S(2)}, u32[]{:S(2)}) async-start(f32[32,8,8,128]{3,2,1,0:T(8,128)} %get-tuple-element.43), calls=%async_computation.1 | async-start | bytes 2097152 | tf_op jit(solution)/shard_map/all_to_all | solution.py:522
